TPU v7x, 32 devices: a whole 2x2x4 slice. The times are simulated.
32 devices in a mesh: dp: 16 (over z, x, core), mp: 2 (over y).
Axes of the slice: x: 2, y: 2, z: 4, core: 2. Of those that a mesh axis runs over, the one named last changes fastest.
Arguments:
- tokens: bfloat16 [16, 4096, 1024], P('dp', 'mp'), may hold values from -6 to 6
- prefix: int32 [16], P('dp'), may hold values from 0 to 4096, as said below
- init_state: float32 [16, 512, 1024], P('dp', 'mp'), may hold values from -6 to 6
- cotangent: bfloat16 [16, 4096, 1024], P('dp', 'mp'), may hold values from -6 to 6
- norm_gains: bfloat16 [3, 1024], P(None, 'dp'), may hold values from 0.25 to 1.75
- gate_bias: bfloat16 [1024], P('dp'), may hold values from -2 to 4
- rel_table: bfloat16 [32, 8], P('dp', 'mp'), may hold values from -5 to 5
- tok_in_proj: bfloat16 [1024, 4, 1024], P('dp', None, 'mp'), may hold values from -0.1875 to 0.1875
- tok_out_proj: bfloat16 [2, 1024, 1024], P(None, 'mp', 'dp'), may hold values from -2 to 2
- st_in_proj: bfloat16 [1024, 4, 1024], P('dp', None, 'mp'), may hold values from -0.1875 to 0.1875
- st_out_proj: bfloat16 [2, 1024, 1024], P(None, 'mp', 'dp'), may hold values from -2 to 2
- mlp_up: bfloat16 [1024, 4096], P('dp', 'mp'), may hold values from -0.1875 to 0.1875
- mlp_down: bfloat16 [4096, 1024], P('mp', 'dp'), may hold values from -0.09375 to 0.09375
Outputs:
- mixed: bfloat16 [16, 4096, 1024], P('dp', 'mp')
- final_state: float32 [16, 512, 1024], P('dp', 'mp')
- input_grad: float32 [16, 4096, 1024], P('dp', 'mp')
- grad_norm_gains: float32 [3, 1024], P(None, 'dp')
- grad_gate_bias: float32 [1024], P('dp')
- grad_rel_table: float32 [32, 8], P('dp', 'mp')
- grad_tok_in: float32 [1024, 4, 1024], P('dp', None, 'mp')
- grad_tok_out: float32 [2, 1024, 1024], P(None, 'mp', 'dp')
- grad_st_in: float32 [1024, 4, 1024], P('dp', None, 'mp')
- grad_st_out: float32 [2, 1024, 1024], P(None, 'mp', 'dp')
- grad_mlp_up: float32 [1024, 4096], P('dp', 'mp')
- grad_mlp_down: float32 [4096, 1024], P('mp', 'dp')
Inputs may be any that keep to these rules, and one draw needn't show every extreme that they name: Some sequence has prefix 4096 and some has 0.
All inputs are finite; a program needn't handle non-finite values.
Results may differ from a plain program's by a relative error of at most 0.022.
Values may be sent and summed in bfloat16 or wider, within the bound.
A program may use at most 704 MiB of HBM per device.

v0:
```python
import functools

import jax
import jax.numpy as jnp
from jax import lax
from jax.experimental import pallas as pl
from jax.experimental.pallas import tpu as pltpu
from jax.sharding import PartitionSpec as P

HD = 128
S = 512
W = 512
TILE = 128
EXTRA = 128

EPS = 1e-06
NEG = -1e30
THRESH = (12, 16, 23, 32, 46, 64, 91)
LOG2E = 1.4426950408889634
SCALE = HD ** (-0.5)
SCALE2 = SCALE * LOG2E
VMEM_BYTES = 60 * 1024 * 1024

GRP = ("mpl", "core")
ORIG_DP = ("dph", "core")
SWAP = ("core", "mph", "mpl")

F32 = jnp.float32
BF16 = jnp.bfloat16


def regroup(arr, forward):
    ranks = lax.axis_size(("mph", "mpl"))
    half = ranks // 2
    pairs = []
    for seq in range(2):
        for rank in range(ranks):
            here = seq * ranks + rank
            there = (rank % 2) * ranks + seq * half + rank // 2
            if here != there:
                pairs.append((here, there) if forward else (there, here))
    moved = lax.ppermute(arr, SWAP, pairs)
    seq, rank = lax.axis_index("core"), lax.axis_index(("mph", "mpl"))
    stays = (rank % 2 == seq) & (rank == seq * half + rank // 2)
    return jnp.where(stays, arr, moved)


def shift(arr, step):
    half = lax.axis_size("mpl")
    size = 2 * half

    def place(rank):
        return (rank % 2) * half + rank // 2

    pairs = [(place(i), place((i + step) % size)) for i in range(size)]
    return lax.ppermute(arr, ("core", "mpl"), pairs)


def gather_rot(rows):
    size = lax.axis_size(GRP)
    return jnp.concatenate([rows] + [shift(rows, -k) for k in range(1, size)], 0)


def sum_rot(term, count):
    size = lax.axis_size(GRP)
    sent = [shift(term(k * count, count).astype(BF16), k) for k in range(1, size)]
    total = term(0, count)
    for piece in sent:
        total = total + piece.astype(F32)
    return total


def dot_nn(left, right):
    return lax.dot_general(left, right, (((1,), (0,)), ((), ())), preferred_element_type=F32)


def dot_tn(left, right):
    return lax.dot_general(left, right, (((0,), (0,)), ((), ())), preferred_element_type=F32)


def dot_nt(left, right):
    return lax.dot_general(left, right, (((1,), (1,)), ((), ())), preferred_element_type=F32)


def normalize(values):
    center = values - jnp.mean(values, -1, keepdims=True)
    spread = jnp.mean(center * center, -1, keepdims=True)
    inv = lax.rsqrt(spread + EPS)
    return center * inv, inv


def norm_back(grad, gain, unit, inv):
    scaled = grad * gain
    mean_g = jnp.mean(scaled, -1, keepdims=True)
    mean_x = jnp.mean(scaled * unit, -1, keepdims=True)
    return inv * (scaled - mean_g - unit * mean_x)


def bucket_of(offset, half):
    distance = jnp.abs(offset)
    far_part = jnp.full(offset.shape, 8, jnp.int32)
    for limit in THRESH:
        far_part = far_part + (distance >= limit).astype(jnp.int32)
    magnitude = jnp.where(distance < 8, distance, far_part)
    return magnitude + half * (offset > 0).astype(jnp.int32)


def window_bias(table):
    key_pos = lax.broadcasted_iota(jnp.int32, (2 * W, W), 0) - W
    query_pos = lax.broadcasted_iota(jnp.int32, (2 * W, W), 1)
    which = bucket_of(key_pos - query_pos, table.shape[0] // 2)
    bias = jnp.zeros((table.shape[1], 2 * W, W), F32)
    for entry in range(table.shape[0]):
        bias = jnp.where((which == entry)[None], table[entry][:, None, None], bias)
    return bias


def table_grad(cells, entries):
    heads = cells.shape[0]
    diag = lax.broadcasted_iota(jnp.int32, (3, TILE, TILE), 0) - 1
    key_pos = lax.broadcasted_iota(jnp.int32, (3, TILE, TILE), 1)
    query_pos = lax.broadcasted_iota(jnp.int32, (3, TILE, TILE), 2)
    which = bucket_of(diag * TILE + key_pos - query_pos, entries // 2)
    rows = lax.broadcasted_iota(jnp.int32, (entries, 1, 1, 1), 0)
    hot = (which[None] == rows).astype(F32)
    near = jnp.stack(
        [jnp.sum(hot * cells[h, :3][None], (1, 2, 3)) for h in range(heads)], 1
    )
    far = jnp.sum(cells[:, 3:], (2, 3))
    entry = lax.broadcasted_iota(jnp.int32, (entries, heads), 0)
    left = jnp.where(entry == entries // 2 - 1, far[:, 0][None], 0.0)
    right = jnp.where(entry == entries - 1, far[:, 1][None], 0.0)
    return near + left + right


def reach_of(block, prefix):
    query = block * W + lax.broadcasted_iota(jnp.int32, (1, W), 1)
    return jnp.where(query < prefix, jnp.maximum(query, prefix - 1), query)


def allowed_keys(block, prefix):
    key = block * W + lax.broadcasted_iota(jnp.int32, (W, W), 0)
    return key <= reach_of(block, prefix)


def soft_unit(logits, values):
    top = jnp.max(logits[0], 0, keepdims=True)
    for part in logits[1:]:
        top = jnp.maximum(top, jnp.max(part, 0, keepdims=True))
    total = None
    acc = None
    for part, vals in zip(logits, values):
        expo = jnp.exp2(part - top)
        summed = jnp.sum(expo, 0, keepdims=True)
        mixed = dot_tn(vals, expo.astype(BF16))
        total = summed if total is None else total + summed
        acc = mixed if acc is None else acc + mixed
    return jnp.transpose(acc / total).astype(BF16), top + jnp.log2(total)


def row_dot(grad_out, out):
    prod = grad_out.astype(F32) * out.astype(F32)
    return jnp.sum(jnp.transpose(prod), 0, keepdims=True)


def back_unit(logits, queries, keys, values, grad_out, lse, delta):
    probs = jnp.exp2(logits - lse)
    grad_probs = dot_nt(values, grad_out)
    grad_values = dot_nn(probs.astype(BF16), grad_out)
    grad_scores = probs * (grad_probs - delta)
    low = grad_scores.astype(BF16)
    grad_keys = dot_nn(low, queries) * SCALE
    grad_queries = dot_tn(keys, low)
    return grad_queries, grad_keys, grad_values, grad_scores


def self_forward_kernel(where, q, kp, kc, vp, vc, bias, out, lse):
    block = pl.program_id(0)
    edge = jnp.where(block == 0, NEG, 0.0)
    allowed = allowed_keys(block, where[1])
    for h in range(bias.shape[0]):
        cols = slice(h * HD, (h + 1) * HD)
        before = dot_nt(kp[:, cols], q[:, cols]) * SCALE2 + (bias[h, :W] + edge)
        here = jnp.where(allowed, dot_nt(kc[:, cols], q[:, cols]) * SCALE2 + bias[h, W:], NEG)
        out[:, cols], lse[0, h : h + 1] = soft_unit(
            (before, here), (vp[:, cols], vc[:, cols])
        )


def self_specs(blocks, local_w, order):
    def at(part, delta):
        def index(i, where):
            block = jnp.maximum(order(i) + delta, 0)
            return ((block + blocks - where[0]) % blocks, part)

        return pl.BlockSpec((W, local_w), index)

    return at


def self_forward(where, proj, bias):
    seq_len, width = proj.shape
    local_w = width // 4
    heads = bias.shape[0]
    blocks = seq_len // W
    at = self_specs(blocks, local_w, lambda i: i)
    return pl.pallas_call(
        self_forward_kernel,
        grid_spec=pltpu.PrefetchScalarGridSpec(
            num_scalar_prefetch=1,
            grid=(blocks,),
            in_specs=[
                at(0, 0),
                at(2, -1),
                at(2, 0),
                at(3, -1),
                at(3, 0),
                pl.BlockSpec(bias.shape, lambda i, where: (0, 0, 0)),
            ],
            out_specs=[
                at(0, 0),
                pl.BlockSpec((1, heads, W), lambda i, where: (i, 0, 0)),
            ],
        ),
        out_shape=[
            jax.ShapeDtypeStruct((seq_len, 2 * local_w), BF16),
            jax.ShapeDtypeStruct((blocks, heads, W), F32),
        ],
        compiler_params=pltpu.CompilerParams(vmem_limit_bytes=VMEM_BYTES),
        cost_estimate=pl.CostEstimate(
            flops=seq_len * 2 * W * local_w * 4,
            bytes_accessed=seq_len * local_w * 12 + bias.size * 4,
            transcendentals=seq_len * 2 * W * heads,
        ),
        name="self_forward",
    )(where, proj, proj, proj, proj, proj, bias)


def self_backward_kernel(
    where, q, kp, kc, vp, vc, bias, dout, out, lse, aux, grad_proj, cells, carry
):
    step = pl.program_id(0)
    block = pl.num_programs(0) - 1 - step
    edge = jnp.where(block == 0, NEG, 0.0)
    allowed = allowed_keys(block, where[1])
    heads = bias.shape[0]
    local_w = heads * HD
    tiles = W // TILE

    @pl.when(step == 0)
    def _():
        carry[...] = jnp.zeros_like(carry)
        cells[...] = jnp.zeros_like(cells)

    for h in range(heads):
        cols = slice(h * HD, (h + 1) * HD)
        vcols = slice(local_w + h * HD, local_w + (h + 1) * HD)
        delta = row_dot(dout[:, cols], out[:, cols])
        row_lse = lse[0, h : h + 1]
        before = dot_nt(kp[:, cols], q[:, cols]) * SCALE2 + (bias[h, :W] + edge)
        dq0, dk0, dv0, ds0 = back_unit(
            before, q[:, cols], kp[:, cols], vp[:, cols], dout[:, cols], row_lse, delta
        )
        here = jnp.where(allowed, dot_nt(kc[:, cols], q[:, cols]) * SCALE2 + bias[h, W:], NEG)
        dq1, dk1, dv1, ds1 = back_unit(
            here, q[:, cols], kc[:, cols], vc[:, cols], dout[:, cols], row_lse, delta
        )
        parts = {0: [], 1: [], 2: [], 3: [], 4: []}
        for kt in range(2 * tiles):
            for qt in range(tiles):
                source, row = (ds0, kt) if kt < tiles else (ds1, kt - tiles)
                cell = source[row * TILE : (row + 1) * TILE, qt * TILE : (qt + 1) * TILE]
                diag = kt - tiles - qt
                slot = diag + 1 if -1 <= diag <= 1 else (3 if diag < 0 else 4)
                parts[slot].append(cell)
        for slot, group in parts.items():
            cells[h, slot] += functools.reduce(jnp.add, group)
        grad_proj[:, cols] = (jnp.transpose(dq0 + dq1) * SCALE).astype(BF16)
        grad_proj[:, local_w + h * HD : local_w + (h + 1) * HD] = aux[:, cols]
        grad_proj[:, 2 * local_w + h * HD : 2 * local_w + (h + 1) * HD] = (
            dk1 + carry[:, cols] + aux[:, vcols].astype(F32)
        ).astype(BF16)
        grad_proj[:, 3 * local_w + h * HD : 3 * local_w + (h + 1) * HD] = (
            dv1
            + carry[:, vcols]
            + aux[:, 2 * local_w + h * HD : 2 * local_w + (h + 1) * HD].astype(F32)
        ).astype(BF16)
        carry[:, cols] = dk0
        carry[:, vcols] = dv0


def self_backward(where, proj, bias, grad_att, att, lse, aux):
    seq_len, width = proj.shape
    local_w = width // 4
    heads = bias.shape[0]
    blocks = seq_len // W

    def order(i):
        return blocks - 1 - i

    at = self_specs(blocks, local_w, order)

    def whole(i, where):
        return ((order(i) + blocks - where[0]) % blocks, 0)

    return pl.pallas_call(
        self_backward_kernel,
        grid_spec=pltpu.PrefetchScalarGridSpec(
            num_scalar_prefetch=1,
            grid=(blocks,),
            in_specs=[
                at(0, 0),
                at(2, -1),
                at(2, 0),
                at(3, -1),
                at(3, 0),
                pl.BlockSpec(
                    bias.shape, lambda i, where: (0, 0, 0), pipeline_mode=pl.Buffered(1)
                ),
                at(0, 0),
                at(0, 0),
                pl.BlockSpec((1, heads, W), lambda i, where: (order(i), 0, 0)),
                pl.BlockSpec((W, 3 * local_w), whole),
            ],
            out_specs=[
                pl.BlockSpec((W, width), whole),
                pl.BlockSpec((heads, 5, TILE, TILE), lambda i, where: (0, 0, 0, 0)),
            ],
            scratch_shapes=[pltpu.VMEM((W, 2 * local_w), F32)],
        ),
        out_shape=[
            jax.ShapeDtypeStruct((seq_len, width), BF16),
            jax.ShapeDtypeStruct((heads, 5, TILE, TILE), F32),
        ],
        compiler_params=pltpu.CompilerParams(vmem_limit_bytes=VMEM_BYTES),
        cost_estimate=pl.CostEstimate(
            flops=seq_len * 2 * W * local_w * 10,
            bytes_accessed=seq_len * local_w * 30 + bias.size * 4,
            transcendentals=seq_len * 2 * W * heads,
        ),
        name="self_backward",
    )(where, proj, proj, proj, proj, proj, bias, grad_att, att, lse, aux)


def state_forward_kernel(first, where, *refs):
    refs = list(refs)
    prev = refs.pop(0)
    if not first:
        mine, theirs = refs.pop(0), refs.pop(0)
    gain, gate, w_in, w_out, cq, kc, vc = refs[:7]
    state, norm, sproj, satt, att, lse, part = refs[-7:]
    local_w = cq.shape[1]
    heads = local_w // HD
    if first:
        fresh = prev[...]
    else:
        update = mine[...].astype(F32) + theirs[...].astype(F32)
        fresh = gate[...] * prev[...] + (1.0 - gate[...]) * update
    state[...] = fresh
    unit, _ = normalize(fresh)
    normed = (unit * gain[...]).astype(BF16)
    norm[...] = normed
    for p in range(4):
        cols = slice(p * local_w, (p + 1) * local_w)
        sproj[:, cols] = dot_nn(normed, w_in[:, cols]).astype(BF16)
    for h in range(heads):
        cols = [slice(p * local_w + h * HD, p * local_w + (h + 1) * HD) for p in range(4)]
        sk, sv = sproj[:, cols[2]], sproj[:, cols[3]]
        satt[:, cols[0]], lse[0, h : h + 1] = soft_unit(
            (dot_nt(sk, sproj[:, cols[0]]) * SCALE2,), (sv,)
        )
        satt[:, cols[1]], lse[0, heads + h : heads + h + 1] = soft_unit(
            (dot_nt(kc[:, cols[0]], sproj[:, cols[1]]) * SCALE2,), (vc[:, cols[0]],)
        )
        att[:, cols[0]], lse[0, 2 * heads + h : 2 * heads + h + 1] = soft_unit(
            (dot_nt(sk, cq[:, cols[0]]) * SCALE2,), (sv,)
        )
    part[...] = dot_nt(satt[...], w_out[...]).astype(BF16)


def state_forward(where, block, prev, mine, theirs, gain, gate, w_in, w_out, proj, kept, att):
    first = block == 0
    seq_len, width = proj.shape
    local_w = width // 4
    heads = local_w // HD
    blocks = seq_len // W
    model = prev.shape[1]

    def phys(part):
        return pl.BlockSpec(
            (W, local_w), lambda i, where: ((where[2] + blocks - where[0]) % blocks, part)
        )

    def full(arr):
        return pl.BlockSpec(arr.shape, lambda i, where: (0,) * arr.ndim)

    def row_block(cols):
        return pl.BlockSpec((S, cols), lambda i, where: (where[2], 0))

    anywhere = pl.BlockSpec(memory_space=pl.ANY)
    operands = [prev] + ([] if first else [mine, theirs]) + [gain, gate, w_in, w_out]
    in_specs = [full(arr) for arr in operands] + [phys(1), phys(2), phys(3)]
    operands += [proj, proj, proj]
    aliases = {}
    held = [] if first else list(kept[:3])
    for slot, arr in enumerate(held):
        aliases[1 + len(operands)] = 1 + slot
        operands.append(arr)
        in_specs.append(anywhere)
    aliases[1 + len(operands)] = 4
    operands.append(att)
    in_specs.append(anywhere)
    if not first:
        aliases[1 + len(operands)] = 5
        operands.append(kept[3])
        in_specs.append(anywhere)
    return pl.pallas_call(
        functools.partial(state_forward_kernel, first),
        grid_spec=pltpu.PrefetchScalarGridSpec(
            num_scalar_prefetch=1,
            grid=(1,),
            in_specs=in_specs,
            out_specs=[
                full(prev),
                row_block(model),
                row_block(width),
                row_block(2 * local_w),
                phys(1),
                pl.BlockSpec((1, 3 * heads, S), lambda i, where: (where[2], 0, 0)),
                full(prev),
            ],
        ),
        out_shape=[
            jax.ShapeDtypeStruct(prev.shape, F32),
            jax.ShapeDtypeStruct((blocks * S, model), BF16),
            jax.ShapeDtypeStruct((blocks * S, width), BF16),
            jax.ShapeDtypeStruct((blocks * S, 2 * local_w), BF16),
            jax.ShapeDtypeStruct(att.shape, BF16),
            jax.ShapeDtypeStruct((blocks, 3 * heads, S), F32),
            jax.ShapeDtypeStruct(prev.shape, BF16),
        ],
        input_output_aliases=aliases,
        compiler_params=pltpu.CompilerParams(vmem_limit_bytes=VMEM_BYTES),
        cost_estimate=pl.CostEstimate(
            flops=S * model * local_w * 12 + 3 * S * W * local_w * 4,
            bytes_accessed=(w_in.size + w_out.size) * 2 + S * model * 20,
            transcendentals=3 * S * W * heads,
        ),
        name="state_forward",
    )(where, *operands)


def state_backward_kernel(last, where, *refs):
    refs = list(refs)
    if not last:
        later, mine, theirs, state_next, upd_mine, upd_theirs = refs[:6]
        refs = refs[6:]
    state, gain, gate, w_in, w_out, cq, kc, vc, dcross, cross, sproj, satt, lse = refs[:13]
    dstate, dupd, dsproj, aux, sums, part = refs[-6:]
    local_w = cq.shape[1]
    heads = local_w // HD
    model = state.shape[1]
    gate_f = gate[...]
    if last:
        dstate[...] = jnp.zeros_like(dstate)
        dupd[...] = jnp.zeros_like(dupd)
        gate_sum = jnp.zeros((1, model), F32)
    else:
        unit, inv = normalize(state_next[...])
        grad_norm = mine[...].astype(F32) + theirs[...].astype(F32)
        grad_state = gate_f * later[...] + norm_back(grad_norm, gain[...], unit, inv)
        dstate[...] = grad_state
        update = upd_mine[...].astype(F32) + upd_theirs[...].astype(F32)
        gate_sum = jnp.sum(grad_state * (state[...] - update), 0, keepdims=True)
        gate_sum = gate_sum * gate_f * (1.0 - gate_f)
        dupd[...] = ((1.0 - gate_f) * grad_state).astype(BF16)
    for h in range(heads):
        cols = [slice(p * local_w + h * HD, p * local_w + (h + 1) * HD) for p in range(4)]
        head = cols[0]
        sk, sv = sproj[:, cols[2]], sproj[:, cols[3]]
        delta = row_dot(dcross[:, head], cross[:, head])
        dq, dk, dv, _ = back_unit(
            dot_nt(sk, cq[:, head]) * SCALE2,
            cq[:, head],
            sk,
            sv,
            dcross[:, head],
            lse[0, 2 * heads + h : 2 * heads + h + 1],
            delta,
        )
        aux[:, cols[0]] = (jnp.transpose(dq) * SCALE).astype(BF16)
        if last:
            aux[:, cols[1]] = jnp.zeros((S, HD), BF16)
            aux[:, cols[2]] = jnp.zeros((S, HD), BF16)
            dsproj[:, cols[0]] = jnp.zeros((S, HD), BF16)
            dsproj[:, cols[1]] = jnp.zeros((S, HD), BF16)
        else:
            dself = dot_nn(dupd[...], w_out[:, cols[0]]).astype(BF16)
            dext = dot_nn(dupd[...], w_out[:, cols[1]]).astype(BF16)
            sq = sproj[:, cols[0]]
            dq, dk_s, dv_s, _ = back_unit(
                dot_nt(sk, sq) * SCALE2,
                sq,
                sk,
                sv,
                dself,
                lse[0, h : h + 1],
                row_dot(dself, satt[:, cols[0]]),
            )
            dsproj[:, cols[0]] = (jnp.transpose(dq) * SCALE).astype(BF16)
            dk = dk + dk_s
            dv = dv + dv_s
            sx = sproj[:, cols[1]]
            dq, dk_x, dv_x, _ = back_unit(
                dot_nt(kc[:, head], sx) * SCALE2,
                sx,
                kc[:, head],
                vc[:, head],
                dext,
                lse[0, heads + h : heads + h + 1],
                row_dot(dext, satt[:, cols[1]]),
            )
            dsproj[:, cols[1]] = (jnp.transpose(dq) * SCALE).astype(BF16)
            aux[:, cols[1]] = dk_x.astype(BF16)
            aux[:, cols[2]] = dv_x.astype(BF16)
        dsproj[:, cols[2]] = dk.astype(BF16)
        dsproj[:, cols[3]] = dv.astype(BF16)
    part[...] = dot_nt(dsproj[...], w_in[...]).astype(BF16)
    sums[...] = jnp.broadcast_to(gate_sum, sums.shape)


def state_backward(
    where, block, chain, state, gain, gate, w_in, w_out, proj, grad_att, att, sproj, satt, lse, kept
):
    seq_len, width = proj.shape
    local_w = width // 4
    heads = local_w // HD
    blocks = seq_len // W
    last = block == blocks - 1
    model = state.shape[1]

    def phys(part):
        return pl.BlockSpec(
            (W, local_w), lambda i, where: ((where[2] + blocks - where[0]) % blocks, part)
        )

    def full(arr):
        return pl.BlockSpec(arr.shape, lambda i, where: (0,) * arr.ndim)

    def row_block(cols):
        return pl.BlockSpec((S, cols), lambda i, where: (where[2], 0))

    anywhere = pl.BlockSpec(memory_space=pl.ANY)
    operands = ([] if last else list(chain)) + [state, gain, gate, w_in, w_out]
    in_specs = [full(arr) for arr in operands]
    operands += [proj, proj, proj, grad_att, att, sproj, satt, lse]
    in_specs += [phys(1), phys(2), phys(3), phys(1), phys(1)]
    in_specs += [row_block(width), row_block(2 * local_w)]
    in_specs += [pl.BlockSpec((1, 3 * heads, S), lambda i, where: (where[2], 0, 0))]
    aliases = {}
    if not last:
        for slot, arr in enumerate(kept):
            aliases[1 + len(operands)] = 1 + slot
            operands.append(arr)
            in_specs.append(anywhere)
    return pl.pallas_call(
        functools.partial(state_backward_kernel, last),
        grid_spec=pltpu.PrefetchScalarGridSpec(
            num_scalar_prefetch=1,
            grid=(1,),
            in_specs=in_specs,
            out_specs=[
                full(state),
                row_block(model),
                row_block(width),
                pl.BlockSpec(
                    (W, 3 * local_w),
                    lambda i, where: ((where[2] + blocks - where[0]) % blocks, 0),
                ),
                pl.BlockSpec((8, model), lambda i, where: (0, 0)),
                full(state),
            ],
        ),
        out_shape=[
            jax.ShapeDtypeStruct(state.shape, F32),
            jax.ShapeDtypeStruct((blocks * S, model), BF16),
            jax.ShapeDtypeStruct((blocks * S, width), BF16),
            jax.ShapeDtypeStruct((seq_len, 3 * local_w), BF16),
            jax.ShapeDtypeStruct((8, model), F32),
            jax.ShapeDtypeStruct(state.shape, BF16),
        ],
        input_output_aliases=aliases,
        compiler_params=pltpu.CompilerParams(vmem_limit_bytes=VMEM_BYTES),
        cost_estimate=pl.CostEstimate(
            flops=S * model * local_w * 12 + 3 * S * W * local_w * 10,
            bytes_accessed=(w_in.size + w_out.size) * 2 + S * model * 40,
            transcendentals=3 * S * W * heads,
        ),
        name="state_backward",
    )(where, *operands)


def up_kernel(rows, weight, act, slope):
    step = min(512, weight.shape[1])
    root = 0.7978845608028654
    for start in range(0, weight.shape[1], step):
        cols = slice(start, start + step)
        pre = dot_nn(rows[...], weight[:, cols])
        square = pre * pre
        half = 0.5 * jnp.tanh(pre * (root + (root * 0.044715) * square)) + 0.5
        value = pre * half
        act[:, cols] = value.astype(BF16)
        rise = 2.0 * root + (6.0 * root * 0.044715) * square
        slope[:, cols] = (half + value * (1.0 - half) * rise).astype(BF16)


def up_project(rows, weight):
    count, model = rows.shape
    units = weight.shape[1]
    out = jax.ShapeDtypeStruct((count, units), BF16)
    return pl.pallas_call(
        up_kernel,
        grid=(count // W,),
        in_specs=[
            pl.BlockSpec((W, model), lambda i: (i, 0)),
            pl.BlockSpec((model, units), lambda i: (0, 0)),
        ],
        out_specs=[pl.BlockSpec((W, units), lambda i: (i, 0))] * 2,
        out_shape=[out, out],
        compiler_params=pltpu.CompilerParams(vmem_limit_bytes=VMEM_BYTES),
        cost_estimate=pl.CostEstimate(
            flops=2 * count * model * units,
            bytes_accessed=count * (model + 2 * units) * 2 + model * units * 2,
            transcendentals=count * units,
        ),
        name="up_project",
    )(rows, weight)


def gather_weight(shard):
    return lax.all_gather(shard, ORIG_DP, axis=0, tiled=True)


def scatter_moved(moved):
    return lax.psum_scatter(moved, ORIG_DP, scatter_dimension=0, tiled=True)


def scatter_grad(grad):
    return scatter_moved(regroup(grad.astype(BF16), False))


def local(
    tokens,
    prefix,
    init_state,
    cotangent,
    norm_gains,
    gate_bias,
    rel_table,
    tok_in_proj,
    tok_out_proj,
    st_in_proj,
    st_out_proj,
    mlp_up,
    mlp_down,
):
    rows = tokens.shape[1]
    model = tokens.shape[2]
    size = lax.axis_size(GRP)
    rank = lax.axis_index(GRP)
    seq_len = rows * size
    blocks = seq_len // W
    shard = tok_in_proj.shape[0]
    local_w = tok_in_proj.shape[2]
    heads = rel_table.shape[1]
    units = mlp_up.shape[1]

    small = jnp.concatenate([norm_gains, gate_bias[None]], 0).T
    entries = rel_table.shape[0]
    extra = jnp.zeros((shard, EXTRA), BF16)
    extra = lax.dynamic_update_slice(extra, small, (0, 0))
    extra = lax.dynamic_update_slice(extra, rel_table, (0, 4))
    tok_rows = regroup(tokens[0], True)
    wide = 4 * local_w
    shard_tin = tok_in_proj.reshape(shard, wide)
    shard_sin = st_in_proj.reshape(shard, wide)
    first = gather_weight(jnp.concatenate([shard_tin, extra], 1))
    second = jnp.concatenate([shard_sin, st_out_proj.reshape(2 * local_w, shard).T], 1)
    third = jnp.concatenate(
        [tok_out_proj.reshape(2 * local_w, shard).T, mlp_up, mlp_down.T], 1
    )
    first, tok_rows, second = lax.optimization_barrier((first, tok_rows, second))
    first = regroup(first, True)
    second = gather_weight(second)
    w_tin, extra = first[:, :wide], first[:, wide:]
    small = extra[:, :4].T.astype(F32)
    table = extra.reshape(-1, shard, EXTRA)[:, :entries, 4 : 4 + heads]
    table = table.reshape(-1, heads).astype(F32)
    start = regroup(init_state[0], True)
    if size == 2:
        other = shift(start, 1)
        state0 = jnp.where(
            rank == 0,
            jnp.concatenate([start, other], 0),
            jnp.concatenate([other, start], 0),
        )
    else:
        state0 = lax.all_gather(start, GRP, axis=0, tiled=True)
    prefix_len = regroup(prefix, True)
    gain1, gain2, gain3 = small[0:1], small[1:2], small[2:3]
    gate = jax.nn.sigmoid(small[3:4])
    bias = window_bias(table * LOG2E)
    base = jnp.stack([rank.astype(jnp.int32) * (rows // W), prefix_len[0]])

    def where_at(block):
        return jnp.concatenate([base, jnp.full((1,), block, jnp.int32)])

    tok_f = tok_rows.astype(F32)
    unit1, inv1 = normalize(tok_f)
    normed = gather_rot((unit1 * gain1).astype(BF16))
    proj = dot_nn(normed, w_tin).astype(BF16)
    proj, cotangent, second, third = lax.optimization_barrier((proj, cotangent, second, third))
    third = gather_weight(third)
    second = regroup(second, True)
    w_sin, w_sout = second[:, :wide], second[:, wide:]
    cot_rows = regroup(cotangent[0], True)

    att, lse_tok = self_forward(where_at(0), proj, bias)
    states, ups = [], []
    prev, mine, theirs, kept = state0, None, None, None
    for block in range(blocks):
        outs = state_forward(
            where_at(block), block, prev, mine, theirs, gain3, gate, w_sin, w_sout, proj, kept, att
        )
        prev, norm_st, sproj, satt, att, lse_st, mine = outs
        kept = (norm_st, sproj, satt, lse_st)
        if block == 1:
            mine, third = lax.optimization_barrier((mine, third))
        if size == 2:
            theirs = shift(mine, 1)
        else:
            theirs = lax.psum(mine.astype(F32), GRP) - mine.astype(F32)
            theirs = theirs.astype(BF16)
        states.append(prev)
        ups.append((mine, theirs))
    third = regroup(third, True)
    w_tout = third[:, : 2 * local_w]
    w_up = third[:, 2 * local_w : 2 * local_w + units]
    w_down = third[:, 2 * local_w + units :]
    final = gate * prev + (1.0 - gate) * (mine.astype(F32) + theirs.astype(F32))
    final_rows = lax.dynamic_slice_in_dim(final, rank * (S // size), S // size, 0)

    def attn_term(first, count):
        return dot_nt(lax.slice_in_dim(att, first, first + count, axis=0), w_tout)

    resid = tok_f + sum_rot(attn_term, rows)
    unit2, inv2 = normalize(resid)
    normed2 = gather_rot((unit2 * gain2).astype(BF16))
    act, slope = up_project(normed2, w_up)

    def mlp_term(first, count):
        return dot_nt(lax.slice_in_dim(act, first, first + count, axis=0), w_down)

    mixed = (resid + sum_rot(mlp_term, rows)).astype(BF16)

    cot_all = gather_rot(cot_rows)
    grad_pre = (dot_nn(cot_all, w_down) * slope.astype(F32)).astype(BF16)
    grad_down = scatter_grad(dot_tn(cot_all, act))

    def up_term(first, count):
        return dot_nt(lax.slice_in_dim(grad_pre, first, first + count, axis=0), w_up)

    grad_norm2 = sum_rot(up_term, rows)
    grad_up = scatter_grad(dot_tn(normed2, grad_pre))
    grad_resid = cot_rows.astype(F32) + norm_back(grad_norm2, gain2, unit2, inv2)
    grad_attn = gather_rot(grad_resid.astype(BF16))
    grad_att = dot_nn(grad_attn, w_tout).astype(BF16)
    grad_tout = scatter_grad(dot_tn(grad_attn, att))

    chain, kept_b, sums = None, None, []
    for block in reversed(range(blocks)):
        outs = state_backward(
            where_at(block),
            block,
            chain,
            states[block],
            gain3,
            gate,
            w_sin,
            w_sout,
            proj,
            grad_att,
            att,
            sproj,
            satt,
            lse_st,
            kept_b,
        )
        later, dupd, dsproj, aux, sum_b, part = outs
        kept_b = (dupd, dsproj, aux)
        sums.append(sum_b)
        if block > 0:
            if size == 2:
                other = shift(part, 1)
            else:
                other = (lax.psum(part.astype(F32), GRP) - part.astype(F32)).astype(BF16)
            chain = (later, part, other, states[block]) + ups[block - 1]
    gate_grad = functools.reduce(jnp.add, sums)[0]
    mixed = regroup(mixed, False)
    final_rows = regroup(final_rows, False)
    grad_st = jnp.concatenate(
        [dot_tn(norm_st, dsproj).astype(BF16), dot_tn(dupd, satt).astype(BF16)], 1
    )
    aux, grad_st, mixed, final_rows = lax.optimization_barrier(
        (aux, grad_st, mixed, final_rows)
    )
    grad_st = regroup(grad_st, False)

    grad_proj, cells = self_backward(where_at(0), proj, bias, grad_att, att, lse_tok, aux)

    def tok_term(first, count):
        return dot_nt(lax.slice_in_dim(grad_proj, first, first + count, axis=0), w_tin)

    grad_tin = dot_tn(normed, grad_proj).astype(BF16)
    grad_tin, grad_st = lax.optimization_barrier((grad_tin, grad_st))
    grad_st = scatter_moved(grad_st)
    grad_sin, grad_sout = grad_st[:, :wide], grad_st[:, wide:]
    grad_norm1 = sum_rot(tok_term, rows)
    input_grad = grad_resid + norm_back(grad_norm1, gain1, unit1, inv1)

    grad_table = table_grad(cells, table.shape[0])
    packed = jnp.zeros((model // shard, shard, EXTRA), F32)
    packed = packed.at[:, :, 0].set(gate_grad.reshape(-1, shard))
    packed = packed.at[:, :entries, 1 : 1 + heads].set(grad_table.reshape(-1, entries, heads))
    packed = scatter_grad(packed.reshape(model, EXTRA)).astype(F32)
    grad_tin = scatter_grad(grad_tin)

    def gain_sum(shard_in, grad):
        return jnp.sum(shard_in.astype(F32) * grad.astype(F32), 1)

    ranks = lax.axis_size(("mph", "mpl"))
    vectors = jnp.stack(
        [
            gain_sum(shard_tin, grad_tin),
            gain_sum(mlp_up, grad_up),
            gain_sum(shard_sin, grad_sin),
            packed[:, 0] / ranks,
        ]
    )
    if ranks == 2:
        vectors = vectors + lax.ppermute(vectors, ("mph", "mpl"), [(0, 1), (1, 0)])
    else:
        vectors = lax.psum(vectors, ("mph", "mpl"))
    gains = vectors[:3] / norm_gains.astype(F32)
    grad_table = packed[:entries, 1 : 1 + heads]

    return (
        mixed[None],
        final_rows[None],
        regroup(input_grad.astype(BF16), False).astype(F32)[None],
        gains,
        vectors[3],
        grad_table,
        grad_tin.astype(F32).reshape(shard, 4, local_w),
        grad_tout.T.astype(F32).reshape(2, local_w, shard),
        grad_sin.astype(F32).reshape(shard, 4, local_w),
        grad_sout.T.astype(F32).reshape(2, local_w, shard),
        grad_up.astype(F32),
        grad_down.T.astype(F32),
    )


def solution(mesh):
    devs = mesh.devices
    dp_n, mp_n = devs.shape
    fine = jax.sharding.Mesh(
        devs.reshape(dp_n // 2, 2, 2, mp_n // 2), ("dph", "core", "mph", "mpl")
    )
    dp, mp = ("dph", "core"), ("mph", "mpl")
    weights = (
        P(None, dp),
        P(dp),
        P(dp, mp),
        P(dp, None, mp),
        P(None, mp, dp),
        P(dp, None, mp),
        P(None, mp, dp),
        P(dp, mp),
        P(mp, dp),
    )
    rows = P(dp, mp, None)
    return jax.shard_map(
        local,
        mesh=fine,
        in_specs=(rows, P(dp), rows, rows) + weights,
        out_specs=(rows, rows, rows) + weights,
        check_vma=False,
    )
```

profile of v0, /device:TPU:0, one launch (start us, length us, event | category | flops | bytes accessed | tf_op | source)
XLA Modules:
  0.0 1371.2 jit_solution(12833027532872050143)
XLA Ops:
  21.6 44.7 %all-gather.4.cloned.1.call-done = bf16[1024,2176]{1,0:T(8,128)(2,1)} async-done(((bf16[64,2176]{1,0:T(8,128)(2,1)}), bf16[1024,2176]{1,0:T(8,128)(2,1)}) %all-gather.4.cloned.1.call-update) | async-done | bytes 4456464 | tf_op jit(solution)/shard_map/all_gather | solution.py:641
  85.9 49.4 %collective-permute-start.5 = (bf16[2048,1024]{1,0:T(8,128)(2,1)}, bf16[2048,1024]{1,0:T(8,128)(2,1)}, u32[]{:S(2)}, u32[]{:S(2)}) collective-permute-start(bf16[2048,1024]{1,0:T(8,128)(2,1)} %fusion.5), channel_id=1, source_target_pairs={{0,2},{2,0},{1,3},{3,1},{4,6},{6,4},{5,7},{7,5},{8,10},{10,8},{9,1... | collective-permute-start | bytes 12582920 | tf_op jit(solution)/shard_map/ppermute | solution.py:56
  143.6 25.2 %convolution_convert_fusion.q.kp.kc.vp.vc.refs_5_.refs_6_.refs_7_.refs_8_.refs_9_.refs_11_.refs_12_.refs_13_ = bf16[4096,2048]{1,0:T(8,128)(2,1)} fusion(bf16[2048,1024]{1,0:T(8,128)(2,1)} %collective-permute-done.5, bf16[2048,1024]{1,0:T(8,128)(2,1)} %fusion.5, bf16[1024,2176]{0,1:T(8,128)(2,1)} %copy-done.10), kind=kOutput, calls=%fused_computation.1 | convolution fusion | flops 17205035008 | bytes 29360128 | tf_op jit(solution)/shard_map/dot_general | solution.py:74
  210.9 33.0 %select_select_fusion.bias = f32[4,1024,512]{2,1,0:T(8,128)} fusion(f32[4]{0:T(128)S(1)} %get-tuple-element.392, f32[4]{0:T(128)S(1)} %get-tuple-element.393, f32[4]{0:T(128)S(1)} %get-tuple-element.394, f32[4]{0:T(128)S(1)} %get-tuple-element.395, f32[4]{0:T(128)S(1)} %get-tuple-element.396, f32[4]{0:T(128)S(1)} %get-tuple-element.397, ...), kind=kLoop, calls=%fused_computation.41 | loop fusion | flops 67108864 | bytes 25166336 | tf_op jit(solution)/shard_map/jit(_where)/select_n | solution.py:114
  243.9 39.1 %self_forward.1 = (bf16[4096,1024]{1,0:T(8,128)(2,1)}, f32[8,4,512]{2,1,0:T(4,128)}) custom-call(s32[3]{0:T(128)} %get-tuple-element.463.where, bf16[4096,2048]{1,0:T(8,128)(2,1)} %convolution_convert_fusion.q.kp.kc.vp.vc.refs_5_.refs_6_.refs_7_.refs_8_.refs_9_.refs_11_.refs_12_.refs_13_, ...), custom_call_target="tpu_custom_call" | custom-call | flops 8589934592 | bytes 33554432 | tf_op jit(solution)/shard_map/self_forward/pallas_call | solution.py:207
  309.4 16.5 %state_forward.9 = (f32[512,1024]{1,0:T(8,128)}, bf16[4096,1024]{1,0:T(8,128)(2,1)}, bf16[4096,2048]{1,0:T(8,128)(2,1)}, bf16[4096,1024]{1,0:T(8,128)(2,1)}, bf1...) custom-call(s32[3]{0:T(128)} %get-tuple-element.462.where, ...), custom_call_target="tpu_custom_call", output_to_operand_aliasing={{1}: (11, {}), {2}: (12, {}), {3}: (13, {}), {4}: (14, {}),... | custom-call | flops 4831838208 | bytes 16777216 | tf_op jit(solution)/shard_map/state_forward/pallas_call | solution.py:417
  334.4 16.3 %state_forward.10 = (f32[512,1024]{1,0:T(8,128)}, bf16[4096,1024]{1,0:T(8,128)(2,1)}, bf16[4096,2048]{1,0:T(8,128)(2,1)}, bf16[4096,1024]{1,0:T(8,128)(2,1)}, bf...) custom-call(s32[3]{0:T(128)} %get-tuple-element.461.where, ...), custom_call_target="tpu_custom_call", output_to_operand_aliasing={{1}: (11, {}), {2}: (12, {}), {3}: (13, {}), {4}: (14, {}),... | custom-call | flops 4831838208 | bytes 16777216 | tf_op jit(solution)/shard_map/state_forward/pallas_call | solution.py:417
  354.6 16.9 %state_forward.11 = (f32[512,1024]{1,0:T(8,128)}, bf16[4096,1024]{1,0:T(8,128)(2,1)}, bf16[4096,2048]{1,0:T(8,128)(2,1)}, bf16[4096,1024]{1,0:T(8,128)(2,1)}, bf...) custom-call(s32[3]{0:T(128)} %get-tuple-element.460.where, ...), custom_call_target="tpu_custom_call", output_to_operand_aliasing={{1}: (11, {}), {2}: (12, {}), {3}: (13, {}), {4}: (14, {}),... | custom-call | flops 4831838208 | bytes 16777216 | tf_op jit(solution)/shard_map/state_forward/pallas_call | solution.py:417
  375.3 16.5 %state_forward.12 = (f32[512,1024]{1,0:T(8,128)}, bf16[4096,1024]{1,0:T(8,128)(2,1)}, bf16[4096,2048]{1,0:T(8,128)(2,1)}, bf16[4096,1024]{1,0:T(8,128)(2,1)}, bf...) custom-call(s32[3]{0:T(128)} %get-tuple-element.459.where, ...), custom_call_target="tpu_custom_call", output_to_operand_aliasing={{1}: (11, {}), {2}: (12, {}), {3}: (13, {}), {4}: (14, {}),... | custom-call | flops 4831838208 | bytes 16777216 | tf_op jit(solution)/shard_map/state_forward/pallas_call | solution.py:417
  395.7 16.5 %state_forward.13 = (f32[512,1024]{1,0:T(8,128)}, bf16[4096,1024]{1,0:T(8,128)(2,1)}, bf16[4096,2048]{1,0:T(8,128)(2,1)}, bf16[4096,1024]{1,0:T(8,128)(2,1)}, bf...) custom-call(s32[3]{0:T(128)} %get-tuple-element.458.where, ...), custom_call_target="tpu_custom_call", output_to_operand_aliasing={{1}: (11, {}), {2}: (12, {}), {3}: (13, {}), {4}: (14, {}),... | custom-call | flops 4831838208 | bytes 16777216 | tf_op jit(solution)/shard_map/state_forward/pallas_call | solution.py:417
  416.0 16.6 %state_forward.14 = (f32[512,1024]{1,0:T(8,128)}, bf16[4096,1024]{1,0:T(8,128)(2,1)}, bf16[4096,2048]{1,0:T(8,128)(2,1)}, bf16[4096,1024]{1,0:T(8,128)(2,1)}, bf...) custom-call(s32[3]{0:T(128)} %get-tuple-element.457.where, ...), custom_call_target="tpu_custom_call", output_to_operand_aliasing={{1}: (11, {}), {2}: (12, {}), {3}: (13, {}), {4}: (14, {}),... | custom-call | flops 4831838208 | bytes 16777216 | tf_op jit(solution)/shard_map/state_forward/pallas_call | solution.py:417
  436.5 16.8 %state_forward.15 = (f32[512,1024]{1,0:T(8,128)}, bf16[4096,1024]{1,0:T(8,128)(2,1)}, bf16[4096,2048]{1,0:T(8,128)(2,1)}, bf16[4096,1024]{1,0:T(8,128)(2,1)}, bf...) custom-call(s32[3]{0:T(128)} %get-tuple-element.380.where, ...), custom_call_target="tpu_custom_call", output_to_operand_aliasing={{1}: (11, {}), {2}: (12, {}), {3}: (13, {}), {4}: (14, {}),... | custom-call | flops 4831838208 | bytes 16777216 | tf_op jit(solution)/shard_map/state_forward/pallas_call | solution.py:417
  489.2 32.2 %collective-permute-start.17 = (bf16[2048,1024]{1,0:T(8,128)(2,1)}, bf16[2048,1024]{1,0:T(8,128)(2,1)}, u32[]{:S(2)}, u32[]{:S(2)}) collective-permute-start(bf16[2048,1024]{1,0:T(8,128)(2,1)} %broadcast_select_fusion.8), channel_id=1, source_target_pairs={{0,2},{2,0},{1,3},{3,1},{4,6},{6,4},{5,7},{7,5},{8,10},{10,8},{9,1... | collective-permute-start | bytes 12582920 | tf_op jit(solution)/shard_map/ppermute | solution.py:56
  533.9 36.2 %up_project.1 = (bf16[4096,2048]{1,0:T(8,128)(2,1)}, bf16[4096,2048]{1,0:T(8,128)(2,1)}) custom-call(bf16[4096,1024]{1,0:T(8,128)(2,1)} %pad_maximum_fusion.2.rows, bf16[1024,2048]{1,0:T(8,128)(2,1)} %slice.366.weight), custom_call_target="tpu_custom_call" | custom-call | flops 17179869184 | bytes 46137344 | tf_op jit(solution)/shard_map/up_project/pallas_call | solution.py:621
  570.1 26.1 %multiply_convert_fusion = bf16[4096,2048]{1,0:T(8,128)(2,1)} fusion(bf16[4096,2048]{1,0:T(8,128)(2,1)} %get-tuple-element.220, bf16[2048,1024]{1,0:T(8,128)(2,1)} %collective-permute-done.17, bf16[2048,1024]{1,0:T(8,128)(2,1)} %broadcast_select_fusion.8, bf16[1024,5120]{1,0:T(8,128)(2,1)} %copy-done.6), kind=kOutput, calls=%fused_computation | convolution fusion | flops 17221812224 | bytes 46137344 | tf_op jit(solution)/shard_map/dot_general | solution.py:74
  616.0 17.0 %fusion.105 = (f32[2048]{0:T(1024)S(1)}, f32[2048]{0:T(1024)S(1)}, f32[2048,1024]{1,0:T(8,128)}) fusion(f32[2048]{0:T(1024)S(1)} %add_rsqrt_fusion, f32[2048,1024]{1,0:T(8,128)} %copy-done.5, f32[2048]{0:T(1024)S(1)} %broadcast_multiply_fusion.4, f32[1024]{0:T(1024)S(1)} %bitcast.170, bf16[2048,1024]{1,0:T(8,128)(2,1)S(1)} %collective-permute-done.19, ...), kind=kOutput, calls=%fused_computation.255 | convolution fusion | flops 8606707712 | bytes 33591296 | tf_op jit(solution)/shard_map/dot_general | solution.py:82
  653.3 18.8 %convolution_convert_fusion.1.refs_8_.refs_14_.dout = bf16[4096,1024]{1,0:T(8,128)(2,1)} fusion(bf16[2048,1024]{1,0:T(8,128)(2,1)S(1)} %collective-permute-done.20, bf16[2048,1024]{1,0:T(8,128)(2,1)S(1)} %get-tuple-element.378, bf16[1024,5120]{1,0:T(8,128)(2,1)} %copy-done.6), kind=kOutput, calls=%fused_computation.43 | convolution fusion | flops 8610906112 | bytes 18874368 | tf_op jit(solution)/shard_map/dot_general | solution.py:74
  685.7 23.9 %fusion.34 = bf16[1024,2048]{1,0:T(8,128)(2,1)} fusion(bf16[4096,2048]{1,0:T(8,128)(2,1)} %get-tuple-element.263, bf16[2048,1024]{1,0:T(8,128)(2,1)} %collective-permute-done.17, bf16[2048,1024]{1,0:T(8,128)(2,1)} %broadcast_select_fusion.8), kind=kOutput, calls=%fused_computation.69 | convolution fusion | flops 17198743552 | bytes 29360128 | tf_op jit(solution)/shard_map/dot_general | solution.py:78
  713.3 23.7 %state_backward.9 = (f32[512,1024]{1,0:T(8,128)}, bf16[4096,1024]{1,0:T(8,128)(2,1)}, bf16[4096,2048]{1,0:T(8,128)(2,1)}, bf16[4096,1536]{1,0:T(8,128)(2,1)}, f3...) custom-call(s32[3]{0:T(128)} %get-tuple-element.457.where, ...), custom_call_target="tpu_custom_call", output_to_operand_aliasing={{1}: (20, {}), {2}: (21, {}), {3}: (22, {})} | custom-call | flops 7247757312 | bytes 27262976 | tf_op jit(solution)/shard_map/state_backward/pallas_call | solution.py:566
  744.9 23.6 %state_backward.10 = (f32[512,1024]{1,0:T(8,128)}, bf16[4096,1024]{1,0:T(8,128)(2,1)}, bf16[4096,2048]{1,0:T(8,128)(2,1)}, bf16[4096,1536]{1,0:T(8,128)(2,1)}, f...) custom-call(s32[3]{0:T(128)} %get-tuple-element.458.where, ...), custom_call_target="tpu_custom_call", output_to_operand_aliasing={{1}: (20, {}), {2}: (21, {}), {3}: (22, {})} | custom-call | flops 7247757312 | bytes 27262976 | tf_op jit(solution)/shard_map/state_backward/pallas_call | solution.py:566
  790.5 24.5 %state_backward.11 = (f32[512,1024]{1,0:T(8,128)}, bf16[4096,1024]{1,0:T(8,128)(2,1)}, bf16[4096,2048]{1,0:T(8,128)(2,1)}, bf16[4096,1536]{1,0:T(8,128)(2,1)}, f...) custom-call(s32[3]{0:T(128)} %get-tuple-element.459.where, ...), custom_call_target="tpu_custom_call", output_to_operand_aliasing={{1}: (20, {}), {2}: (21, {}), {3}: (22, {})} | custom-call | flops 7247757312 | bytes 27262976 | tf_op jit(solution)/shard_map/state_backward/pallas_call | solution.py:566
  815.4 24.4 %convolution_convert_fusion.2 = bf16[1024,2048]{1,0:T(8,128)(2,1)} fusion(bf16[4096,2048]{1,0:T(8,128)(2,1)} %multiply_convert_fusion, bf16[2048,1024]{1,0:T(8,128)(2,1)} %collective-permute-done.18, bf16[2048,1024]{1,0:T(8,128)(2,1)} %copy-done.8), kind=kOutput, calls=%fused_computation.70 | convolution fusion | flops 17198743552 | bytes 29360128 | tf_op jit(solution)/shard_map/dot_general | solution.py:78
  843.4 23.5 %state_backward.12 = (f32[512,1024]{1,0:T(8,128)}, bf16[4096,1024]{1,0:T(8,128)(2,1)}, bf16[4096,2048]{1,0:T(8,128)(2,1)}, bf16[4096,1536]{1,0:T(8,128)(2,1)}, f...) custom-call(s32[3]{0:T(128)} %get-tuple-element.460.where, ...), custom_call_target="tpu_custom_call", output_to_operand_aliasing={{1}: (20, {}), {2}: (21, {}), {3}: (22, {})} | custom-call | flops 7247757312 | bytes 27262976 | tf_op jit(solution)/shard_map/state_backward/pallas_call | solution.py:566
  866.9 18.4 %add_convert_fusion = bf16[2048,1024]{1,0:T(8,128)(2,1)} fusion(f32[2048,1024]{1,0:T(8,128)} %copy-done.5, bf16[2048,1024]{1,0:T(8,128)(2,1)} %collective-permute-done.28, bf16[1024,5120]{1,0:T(8,128)(2,1)} %copy-done.6, bf16[4096,2048]{1,0:T(8,128)(2,1)} %get-tuple-element.263), kind=kOutput, calls=%fused_computation.31 | convolution fusion | flops 8598323200 | bytes 29360128 | tf_op jit(solution)/shard_map/dot_general | solution.py:82
  889.0 23.6 %state_backward.13 = (f32[512,1024]{1,0:T(8,128)}, bf16[4096,1024]{1,0:T(8,128)(2,1)}, bf16[4096,2048]{1,0:T(8,128)(2,1)}, bf16[4096,1536]{1,0:T(8,128)(2,1)}, f...) custom-call(s32[3]{0:T(128)} %get-tuple-element.461.where, ...), custom_call_target="tpu_custom_call", output_to_operand_aliasing={{1}: (20, {}), {2}: (21, {}), {3}: (22, {})} | custom-call | flops 7247757312 | bytes 27262976 | tf_op jit(solution)/shard_map/state_backward/pallas_call | solution.py:566
  921.1 24.2 %state_backward.14 = (f32[512,1024]{1,0:T(8,128)}, bf16[4096,1024]{1,0:T(8,128)(2,1)}, bf16[4096,2048]{1,0:T(8,128)(2,1)}, bf16[4096,1536]{1,0:T(8,128)(2,1)}, f...) custom-call(s32[3]{0:T(128)} %get-tuple-element.462.where, ...), custom_call_target="tpu_custom_call", output_to_operand_aliasing={{1}: (20, {}), {2}: (21, {}), {3}: (22, {})} | custom-call | flops 7247757312 | bytes 27262976 | tf_op jit(solution)/shard_map/state_backward/pallas_call | solution.py:566
  967.4 23.5 %state_backward.15 = (f32[512,1024]{1,0:T(8,128)}, bf16[4096,1024]{1,0:T(8,128)(2,1)}, bf16[4096,2048]{1,0:T(8,128)(2,1)}, bf16[4096,1536]{1,0:T(8,128)(2,1)}, f...) custom-call(s32[3]{0:T(128)} %get-tuple-element.463.where, ...), custom_call_target="tpu_custom_call", output_to_operand_aliasing={{1}: (20, {}), {2}: (21, {}), {3}: (22, {})} | custom-call | flops 7247757312 | bytes 27262976 | tf_op jit(solution)/shard_map/state_backward/pallas_call | solution.py:566
  990.9 23.0 %convolution_convert_fusion.3 = bf16[1024,2048]{1,0:T(8,128)(2,1)S(1)} fusion(bf16[4096,1024]{1,0:T(8,128)(2,1)} %get-tuple-element.260, bf16[4096,2048]{1,0:T(8,128)(2,1)} %get-tuple-element.261), kind=kOutput, calls=%fused_computation.71 | convolution fusion | flops 17181966336 | bytes 29360128 | tf_op jit(solution)/shard_map/dot_general | solution.py:78
  1036.2 56.3 %self_backward.1 = (bf16[4096,2048]{1,0:T(8,128)(2,1)}, f32[4,5,128,128]{3,2,1,0:T(8,128)}) custom-call(s32[3]{0:T(128)} %get-tuple-element.463.where, bf16[4096,2048]{1,0:T(8,128)(2,1)} %convolution_convert_fusion.q.kp.kc.vp.vc.refs_5_.refs_6_.refs_7_.refs_8_.refs_9_.refs_11_.refs_12_.refs_13_, ...), custom_call_target="tpu_custom_call" | custom-call | flops 21474836480 | bytes 71303168 | tf_op jit(solution)/shard_map/self_backward/pallas_call | solution.py:306
  1108.7 23.8 %fusion.33 = bf16[1024,2048]{1,0:T(8,128)(2,1)} fusion(bf16[4096,2048]{1,0:T(8,128)(2,1)} %get-tuple-element.269, bf16[2048,1024]{1,0:T(8,128)(2,1)} %collective-permute-done.5, bf16[2048,1024]{1,0:T(8,128)(2,1)} %fusion.5), kind=kOutput, calls=%fused_computation.68 | convolution fusion | flops 17198743552 | bytes 29360128 | tf_op jit(solution)/shard_map/dot_general | solution.py:78
  1211.1 69.2 %reduce-scatter.13.cloned.1.call-done = bf16[64,3072]{1,0:T(8,128)(2,1)} async-done(((bf16[1024,3072]{1,0:T(8,128)(2,1)}), bf16[64,3072]{1,0:T(8,128)(2,1)}) %reduce-scatter.13.cloned.1.call-update) | async-done | bytes 393232 | tf_op jit(solution)/shard_map/reduce_scatter | solution.py:645
  1282.5 73.2 %reduce-scatter.19.cloned.1.call-done = bf16[64,2048]{1,0:T(8,128)(2,1)} async-done(((bf16[1024,2048]{1,0:T(8,128)(2,1)}), bf16[64,2048]{1,0:T(8,128)(2,1)}) %reduce-scatter.19.cloned.1.call-update) | async-done | bytes 262160 | tf_op jit(solution)/shard_map/reduce_scatter | solution.py:645
  (323 shorter events, 438.4 us)
Async XLA Ops:
  7.2 59.2 %all-gather.4.cloned.1.call-start = ((), (), s32[]{:S(2)}) async-start(), calls=%async_computation.6 | async-start | bytes 4734976 | tf_op jit(solution)/shard_map/all_gather | solution.py:641
  11.5 157.3 %all-gather.6.cloned.1.call-start = ((), (), s32[]{:S(2)}) async-start(), calls=%async_computation.7 | async-start | bytes 6684672 | tf_op jit(solution)/shard_map/all_gather | solution.py:641
  75.6 250.3 %all-gather.8.cloned.1.call-start = ((), (), s32[]{:S(2)}) async-start(), calls=%async_computation.8 | async-start | bytes 11141120 | tf_op jit(solution)/shard_map/all_gather | solution.py:641
  85.9 57.8 %collective-permute-start.5 = (bf16[2048,1024]{1,0:T(8,128)(2,1)}, bf16[2048,1024]{1,0:T(8,128)(2,1)}, u32[]{:S(2)}, u32[]{:S(2)}) collective-permute-start(bf16[2048,1024]{1,0:T(8,128)(2,1)} %fusion.5), channel_id=1, source_target_pairs={{0,2},{2,0},{1,3},{3,1},{4,6},{6,4},{5,7},{7,5},{8,10},{10,8},{9,1... | collective-permute-start | bytes 12582920 | tf_op jit(solution)/shard_map/ppermute | solution.py:56
  168.9 1026.9 %reduce-scatter.23.cloned.1.call-start = ((), (), s32[]{:S(2)}) async-start(), calls=%async_computation.14 | async-start | bytes 4456448
  169.7 32.0 %collective-permute-start = (s32[1]{0:T(128)}, s32[1]{0:T(128)}, u32[]{:S(2)}, u32[]{:S(2)}) collective-permute-start(s32[1]{0:T(128)} %param.18), channel_id=1, source_target_pairs={{1,2},{2,1},{5,6},{6,5},{9,10},{10,9},{13,14},{14,13},{17,18},{18,... | collective-permute-start | bytes 20 | tf_op jit(solution)/shard_map/ppermute | solution.py:42
  171.3 35.4 %collective-permute-start.2 = (f32[256,1024]{1,0:T(8,128)S(1)}, f32[256,1024]{1,0:T(8,128)}, u32[]{:S(2)}, u32[]{:S(2)}) collective-permute-start(f32[256,1024]{1,0:T(8,128)S(1)} %broadcast_select_fusion.12), channel_id=1, source_target_pairs={{0,2},{2,0},{1,3},{3,1},{4,6},{6,4},{5,7},{7,5},{8,10},{10,8},{9,1... | collective-permute-start | bytes 3145736 | tf_op jit(solution)/shard_map/ppermute | solution.py:56
  202.9 80.1 %collective-permute-start.6 = (bf16[1024,3072]{1,0:T(8,128)(2,1)}, bf16[1024,3072]{1,0:T(8,128)(2,1)}, u32[]{:S(2)}, u32[]{:S(2)}) collective-permute-start(bf16[1024,3072]{1,0:T(8,128)(2,1)} %all-gather.6.cloned.1.call-done), channel_id=1, source_target_pairs={{1,2},{2,1},{5,6},{6,5},{9,10},{10,9},{13,14},{14,13},{17,18},{18,... | collective-permute-start | bytes 18874376 | tf_op jit(solution)/shard_map/ppermute | solution.py:42
  325.9 127.4 %collective-permute-start.15 = (bf16[1024,5120]{1,0:T(8,128)(2,1)}, bf16[1024,5120]{1,0:T(8,128)(2,1)}, u32[]{:S(2)}, u32[]{:S(2)}) collective-permute-start(bf16[1024,5120]{1,0:T(8,128)(2,1)} %all-gather.8.cloned.1.call-done), channel_id=1, source_target_pairs={{1,2},{2,1},{5,6},{6,5},{9,10},{10,9},{13,14},{14,13},{17,18},{18,... | collective-permute-start | bytes 31457288 | tf_op jit(solution)/shard_map/ppermute | solution.py:42
  465.2 18.2 %collective-permute-start.14 = (bf16[2048,1024]{1,0:T(8,128)(2,1)}, bf16[2048,1024]{1,0:T(8,128)(2,1)}, u32[]{:S(2)}, u32[]{:S(2)}) collective-permute-start(bf16[2048,1024]{1,0:T(8,128)(2,1)} %bitcast.45), channel_id=1, source_target_pairs={{1,2},{2,1},{5,6},{6,5},{9,10},{10,9},{13,14},{14,13},{17,18},{18,... | collective-permute-start | bytes 12582920 | tf_op jit(solution)/shard_map/ppermute | solution.py:42
  483.1 43.1 %collective-permute-start.18 = (bf16[2048,1024]{1,0:T(8,128)(2,1)S(1)}, bf16[2048,1024]{1,0:T(8,128)(2,1)}, u32[]{:S(2)}, u32[]{:S(2)}) collective-permute-start(bf16[2048,1024]{1,0:T(8,128)(2,1)S(1)} %multiply_convert_fusion.1), channel_id=1, source_target_pairs={{0,2},{2,0},{1,3},{3,1},{4,6},{6,4},{5,7},{7,5},{8,10},{10,8},{9,1... | collective-permute-start | bytes 12582920 | tf_op jit(solution)/shard_map/ppermute | solution.py:56
  489.2 80.9 %collective-permute-start.17 = (bf16[2048,1024]{1,0:T(8,128)(2,1)}, bf16[2048,1024]{1,0:T(8,128)(2,1)}, u32[]{:S(2)}, u32[]{:S(2)}) collective-permute-start(bf16[2048,1024]{1,0:T(8,128)(2,1)} %broadcast_select_fusion.8), channel_id=1, source_target_pairs={{0,2},{2,0},{1,3},{3,1},{4,6},{6,4},{5,7},{7,5},{8,10},{10,8},{9,1... | collective-permute-start | bytes 12582920 | tf_op jit(solution)/shard_map/ppermute | solution.py:56
  644.8 95.0 %collective-permute-start.30 = (bf16[512,1024]{1,0:T(8,128)(2,1)}, bf16[512,1024]{1,0:T(8,128)(2,1)}, u32[]{:S(2)}, u32[]{:S(2)}) collective-permute-start(bf16[512,1024]{1,0:T(8,128)(2,1)} %get-tuple-element.264), channel_id=1, source_target_pairs={{0,2},{2,0},{1,3},{3,1},{4,6},{6,4},{5,7},{7,5},{8,10},{10,8},{9,1... | collective-permute-start | bytes 3145736 | tf_op jit(solution)/shard_map/ppermute | solution.py:56
  685.5 26.8 %collective-permute-start.21 = (bf16[512,1024]{1,0:T(8,128)(2,1)}, bf16[512,1024]{1,0:T(8,128)(2,1)S(1)}, u32[]{:S(2)}, u32[]{:S(2)}) collective-permute-start(bf16[512,1024]{1,0:T(8,128)(2,1)} %get-tuple-element.225.refs_1_), channel_id=1, source_target_pairs={{0,2},{2,0},{1,3},{3,1},{4,6},{6,4},{5,7},{7,5},{8,10},{10,8},{9,1... | collective-permute-start | bytes 3145736 | tf_op jit(solution)/shard_map/ppermute | solution.py:56
  709.6 75.2 %collective-permute-start.40 = (bf16[1024,2048]{1,0:T(8,128)(2,1)}, bf16[1024,2048]{1,0:T(8,128)(2,1)}, u32[]{:S(2)}, u32[]{:S(2)}) collective-permute-start(bf16[1024,2048]{1,0:T(8,128)(2,1)} %fusion.34), channel_id=1, source_target_pairs={{2,1},{1,2},{6,5},{5,6},{10,9},{9,10},{14,13},{13,14},{18,17},{17,... | collective-permute-start | bytes 12582920 | tf_op jit(solution)/shard_map/ppermute | solution.py:42
  742.3 170.8 %collective-permute-start.31 = (f32[256,1024]{1,0:T(8,128)}, f32[256,1024]{1,0:T(8,128)}, u32[]{:S(2)}, u32[]{:S(2)}) collective-permute-start(f32[256,1024]{1,0:T(8,128)} %fusion.75), channel_id=1, source_target_pairs={{2,1},{1,2},{6,5},{5,6},{10,9},{9,10},{14,13},{13,14},{18,17},{17,... | collective-permute-start | bytes 3145736 | tf_op jit(solution)/shard_map/ppermute | solution.py:42
  768.5 20.9 %collective-permute-start.23 = (bf16[512,1024]{1,0:T(8,128)(2,1)}, bf16[512,1024]{1,0:T(8,128)(2,1)S(1)}, u32[]{:S(2)}, u32[]{:S(2)}) collective-permute-start(bf16[512,1024]{1,0:T(8,128)(2,1)} %get-tuple-element.235.refs_1_), channel_id=1, source_target_pairs={{0,2},{2,0},{1,3},{3,1},{4,6},{6,4},{5,7},{7,5},{8,10},{10,8},{9,1... | collective-permute-start | bytes 3145736 | tf_op jit(solution)/shard_map/ppermute | solution.py:56
  784.7 82.2 %collective-permute-start.28 = (bf16[2048,1024]{1,0:T(8,128)(2,1)}, bf16[2048,1024]{1,0:T(8,128)(2,1)}, u32[]{:S(2)}, u32[]{:S(2)}) collective-permute-start(bf16[2048,1024]{1,0:T(8,128)(2,1)} %fusion.35), channel_id=1, source_target_pairs={{0,2},{2,0},{1,3},{3,1},{4,6},{6,4},{5,7},{7,5},{8,10},{10,8},{9,1... | collective-permute-start | bytes 12582920 | tf_op jit(solution)/shard_map/ppermute | solution.py:56
  789.4 408.8 %reduce-scatter.21.cloned.1.call-start = ((), (), s32[]{:S(2)}) async-start(), calls=%async_computation.13 | async-start | bytes 4456448
  814.9 27.5 %collective-permute-start.24 = (bf16[512,1024]{1,0:T(8,128)(2,1)}, bf16[512,1024]{1,0:T(8,128)(2,1)S(1)}, u32[]{:S(2)}, u32[]{:S(2)}) collective-permute-start(bf16[512,1024]{1,0:T(8,128)(2,1)} %get-tuple-element.240.refs_1_), channel_id=1, source_target_pairs={{0,2},{2,0},{1,3},{3,1},{4,6},{6,4},{5,7},{7,5},{8,10},{10,8},{9,1... | collective-permute-start | bytes 3145736 | tf_op jit(solution)/shard_map/ppermute | solution.py:56
  839.8 75.6 %collective-permute-start.36 = (bf16[1024,2048]{1,0:T(8,128)(2,1)}, bf16[1024,2048]{1,0:T(8,128)(2,1)}, u32[]{:S(2)}, u32[]{:S(2)}) collective-permute-start(bf16[1024,2048]{1,0:T(8,128)(2,1)} %convolution_convert_fusion.2), channel_id=1, source_target_pairs={{2,1},{1,2},{6,5},{5,6},{10,9},{9,10},{14,13},{13,14},{18,17},{17,... | collective-permute-start | bytes 12582920 | tf_op jit(solution)/shard_map/ppermute | solution.py:42
  866.9 21.1 %collective-permute-start.25 = (bf16[512,1024]{1,0:T(8,128)(2,1)}, bf16[512,1024]{1,0:T(8,128)(2,1)S(1)}, u32[]{:S(2)}, u32[]{:S(2)}) collective-permute-start(bf16[512,1024]{1,0:T(8,128)(2,1)} %get-tuple-element.245.refs_1_), channel_id=1, source_target_pairs={{0,2},{2,0},{1,3},{3,1},{4,6},{6,4},{5,7},{7,5},{8,10},{10,8},{9,1... | collective-permute-start | bytes 3145736 | tf_op jit(solution)/shard_map/ppermute | solution.py:56
  885.3 76.2 %collective-permute-start.29 = (bf16[2048,1024]{1,0:T(8,128)(2,1)}, bf16[2048,1024]{1,0:T(8,128)(2,1)}, u32[]{:S(2)}, u32[]{:S(2)}) collective-permute-start(bf16[2048,1024]{1,0:T(8,128)(2,1)} %add_convert_fusion), channel_id=1, source_target_pairs={{2,1},{1,2},{6,5},{5,6},{10,9},{9,10},{14,13},{13,14},{18,17},{17,... | collective-permute-start | bytes 12582920 | tf_op jit(solution)/shard_map/ppermute | solution.py:42
  920.0 280.7 %reduce-scatter.17.cloned.1.call-start = ((), (), s32[]{:S(2)}) async-start(), calls=%async_computation.11 | async-start | bytes 2228224 | tf_op jit(solution)/shard_map/reduce_scatter | solution.py:645
  945.3 21.0 %collective-permute-start.27 = (bf16[512,1024]{1,0:T(8,128)(2,1)}, bf16[512,1024]{1,0:T(8,128)(2,1)S(1)}, u32[]{:S(2)}, u32[]{:S(2)}) collective-permute-start(bf16[512,1024]{1,0:T(8,128)(2,1)} %get-tuple-element.255.refs_1_), channel_id=1, source_target_pairs={{0,2},{2,0},{1,3},{3,1},{4,6},{6,4},{5,7},{7,5},{8,10},{10,8},{9,1... | collective-permute-start | bytes 3145736 | tf_op jit(solution)/shard_map/ppermute | solution.py:56
  959.6 74.6 %collective-permute-start.39 = (bf16[1024,1024]{1,0:T(8,128)(2,1)S(1)}, bf16[1024,1024]{1,0:T(8,128)(2,1)}, u32[]{:S(2)}, u32[]{:S(2)}) collective-permute-start(bf16[1024,1024]{1,0:T(8,128)(2,1)S(1)} %fusion.71), channel_id=1, source_target_pairs={{2,1},{1,2},{6,5},{5,6},{10,9},{9,10},{14,13},{13,14},{18,17},{17,... | collective-permute-start | bytes 6291464 | tf_op jit(solution)/shard_map/ppermute | solution.py:42
  1030.9 102.5 %collective-permute-start.34 = (bf16[1024,3072]{1,0:T(8,128)(2,1)}, bf16[1024,3072]{1,0:T(8,128)(2,1)}, u32[]{:S(2)}, u32[]{:S(2)}) collective-permute-start(bf16[1024,3072]{1,0:T(8,128)(2,1)} %pad_maximum_fusion.4), channel_id=1, source_target_pairs={{2,1},{1,2},{6,5},{5,6},{10,9},{9,10},{14,13},{13,14},{18,17},{17,... | collective-permute-start | bytes 18874376 | tf_op jit(solution)/shard_map/ppermute | solution.py:42
  1035.7 166.6 %reduce-scatter.15.cloned.1.call-start = ((), (), s32[]{:S(2)}) async-start(), calls=%async_computation.10 | async-start | bytes 278528 | tf_op jit(solution)/shard_map/reduce_scatter | solution.py:645
  1107.8 24.7 %collective-permute-start.37 = (bf16[1024,128]{1,0:T(8,128)(2,1)S(1)}, bf16[1024,128]{1,0:T(8,128)(2,1)S(1)}, u32[]{:S(2)}, u32[]{:S(2)}) collective-permute-start(bf16[1024,128]{1,0:T(8,128)(2,1)S(1)} %bitcast.152), channel_id=1, source_target_pairs={{2,1},{1,2},{6,5},{5,6},{10,9},{9,10},{14,13},{13,14},{18,17},{17,... | collective-permute-start | bytes 786440 | tf_op jit(solution)/shard_map/ppermute | solution.py:42
  1133.3 147.1 %reduce-scatter.13.cloned.1.call-start = ((), (), s32[]{:S(2)}) async-start(), calls=%async_computation.9 | async-start | bytes 6684672 | tf_op jit(solution)/shard_map/reduce_scatter | solution.py:645
  1139.5 216.2 %reduce-scatter.19.cloned.1.call-start = ((), (), s32[]{:S(2)}) async-start(), calls=%async_computation.12 | async-start | bytes 4456448 | tf_op jit(solution)/shard_map/reduce_scatter | solution.py:645
  1157.0 23.0 %collective-permute-start.35 = (bf16[1024,2048]{1,0:T(8,128)(2,1)S(1)}, bf16[1024,2048]{1,0:T(8,128)(2,1)S(1)}, u32[]{:S(2)}, u32[]{:S(2)}) collective-permute-start(bf16[1024,2048]{1,0:T(8,128)(2,1)S(1)} %copy-done.19), channel_id=1, source_target_pairs={{2,1},{1,2},{6,5},{5,6},{10,9},{9,10},{14,13},{13,14},{18,17},{17,... | collective-permute-start | bytes 12582920 | tf_op jit(solution)/shard_map/ppermute | solution.py:42
  (72 other events, 1502.6 us)
Sparse Core Ops, SparseCore 0:
  11.6 54.6 all-gather.3
  75.7 67.0 all-gather.5
  169.0 88.2 all-gather.7
  789.5 70.8 reduce-scatter.22
  920.2 70.7 reduce-scatter.20
  1035.9 61.3 reduce-scatter.16
  1133.4 58.1 reduce-scatter.14
  1196.0 84.2 reduce-scatter.12
  1284.2 71.4 reduce-scatter.18
where the time goes:
time: 1380 us; the launch traced here: 1370 us
  Pallas kernels  443 us (32%)
  matrix products  295 us (21%)
  waiting for transfers between devices  240 us (17%)
  other arithmetic  175 us (13%)
  starting transfers between devices  146 us (11%)
  local copies, waits for them, and re-layouts  55.8 us (4%)
  between operations  16.4 us (1%)
    pallas_call x8, Pallas kernels, state_backward(): pl.pallas_call(functools.partial(state_backward_kernel, last), grid_spec=...  180 us
    reduce_scatter x4, waiting for transfers between devices, scatter_moved(): return lax.psum_scatter(moved, ORIG_DP, scatter_dimension=0, tiled=True)  142 us
    pallas_call x8, Pallas kernels, state_forward(): pl.pallas_call(functools.partial(state_forward_kernel, first), grid_spec=...  131 us
    dot_general x6, matrix products, dot_tn(): lax.dot_general(left, right, (((0,), (0,)), ((), ())), preferred_element_...  122 us
    ppermute x24, starting transfers between devices, shift(): return lax.ppermute(arr, ('core', 'mpl'), pairs)  106 us
    dot_general x8, matrix products, dot_nt(): lax.dot_general(left, right, (((1,), (1,)), ((), ())), preferred_element_...  103 us
    dot_general x3, matrix products, dot_nn(): lax.dot_general(left, right, (((1,), (0,)), ((), ())), preferred_element_...  70.1 us
    pallas_call x1, Pallas kernels, self_backward(): pl.pallas_call(self_backward_kernel, grid_spec=pltpu.PrefetchScalarGridSp...  56.3 us
  transfers between devices with their start and end apart: 50, of which 15 were waited for; matrix products, arithmetic and copies ran while one was open for 31% of the time, Pallas kernels for 32%

commit v1 on v0

--- a/solution.py
+++ b/solution.py
@@ -614,9 +614,8 @@
         slope[:, cols] = (half + value * (1.0 - half) * rise).astype(BF16)
 
 
-def up_project(rows, weight):
+def up_project(rows, weight, units):
     count, model = rows.shape
-    units = weight.shape[1]
     out = jax.ShapeDtypeStruct((count, units), BF16)
     return pl.pallas_call(
         up_kernel,
@@ -637,16 +636,22 @@
     )(rows, weight)
 
 
+def after(value, *others):
+    return lax.optimization_barrier((value, *others))
+
+
+def hold(value, *others):
+    for arr in others:
+        value = value + (arr[0, 0] * 0).astype(value.dtype)
+    return value
+
+
 def gather_weight(shard):
     return lax.all_gather(shard, ORIG_DP, axis=0, tiled=True)
 
 
 def scatter_moved(moved):
     return lax.psum_scatter(moved, ORIG_DP, scatter_dimension=0, tiled=True)
-
-
-def scatter_grad(grad):
-    return scatter_moved(regroup(grad.astype(BF16), False))
 
 
 def local(
@@ -679,7 +684,16 @@
     entries = rel_table.shape[0]
     extra = jnp.zeros((shard, EXTRA), BF16)
     extra = lax.dynamic_update_slice(extra, small, (0, 0))
-    extra = lax.dynamic_update_slice(extra, rel_table, (0, 4))
+    if lax.axis_size(("mph", "mpl")) == 2:
+        other = lax.ppermute(rel_table, ("mph", "mpl"), [(0, 1), (1, 0)])
+        table = jnp.where(
+            lax.axis_index(("mph", "mpl")) == 0,
+            jnp.concatenate([rel_table, other], 1),
+            jnp.concatenate([other, rel_table], 1),
+        )
+    else:
+        table = lax.all_gather(rel_table, ("mph", "mpl"), axis=1, tiled=True)
+    extra = lax.dynamic_update_slice(extra, table, (0, 4))
     tok_rows = regroup(tokens[0], True)
     wide = 4 * local_w
     shard_tin = tok_in_proj.reshape(shard, wide)
@@ -687,16 +701,16 @@
     first = gather_weight(jnp.concatenate([shard_tin, extra], 1))
     second = jnp.concatenate([shard_sin, st_out_proj.reshape(2 * local_w, shard).T], 1)
     third = jnp.concatenate(
-        [tok_out_proj.reshape(2 * local_w, shard).T, mlp_up, mlp_down.T], 1
+        [mlp_up, mlp_down.T, tok_out_proj.reshape(2 * local_w, shard).T], 1
     )
-    first, tok_rows, second = lax.optimization_barrier((first, tok_rows, second))
-    first = regroup(first, True)
-    second = gather_weight(second)
-    w_tin, extra = first[:, :wide], first[:, wide:]
+    second = gather_weight(hold(second, first, tok_rows))
+    extra = first[:, wide:]
+    w_tin = regroup(first, True)[:, :wide]
     small = extra[:, :4].T.astype(F32)
-    table = extra.reshape(-1, shard, EXTRA)[:, :entries, 4 : 4 + heads]
-    table = table.reshape(-1, heads).astype(F32)
-    start = regroup(init_state[0], True)
+    table = extra.reshape(-1, shard, EXTRA)[:, :entries, 4 : 4 + heads * size]
+    table = table.reshape(-1, heads * size).astype(F32)
+    table = lax.dynamic_slice_in_dim(table, rank * heads, heads, 1)
+    start = regroup(hold(init_state[0], tok_rows), True)
     if size == 2:
         other = shift(start, 1)
         state0 = jnp.where(
@@ -707,6 +721,7 @@
     else:
         state0 = lax.all_gather(start, GRP, axis=0, tiled=True)
     prefix_len = regroup(prefix, True)
+
     gain1, gain2, gain3 = small[0:1], small[1:2], small[2:3]
     gate = jax.nn.sigmoid(small[3:4])
     bias = window_bias(table * LOG2E)
@@ -718,13 +733,12 @@
     tok_f = tok_rows.astype(F32)
     unit1, inv1 = normalize(tok_f)
     normed = gather_rot((unit1 * gain1).astype(BF16))
+    normed, bias, state0 = lax.optimization_barrier((normed, bias, state0))
     proj = dot_nn(normed, w_tin).astype(BF16)
-    proj, cotangent, second, third = lax.optimization_barrier((proj, cotangent, second, third))
+    third, second, proj = after(third, second, proj)
     third = gather_weight(third)
     second = regroup(second, True)
     w_sin, w_sout = second[:, :wide], second[:, wide:]
-    cot_rows = regroup(cotangent[0], True)
-
     att, lse_tok = self_forward(where_at(0), proj, bias)
     states, ups = [], []
     prev, mine, theirs, kept = state0, None, None, None
@@ -735,7 +749,10 @@
         prev, norm_st, sproj, satt, att, lse_st, mine = outs
         kept = (norm_st, sproj, satt, lse_st)
         if block == 1:
-            mine, third = lax.optimization_barrier((mine, third))
+            third, mine = after(third, mine)
+        if block == blocks - 2:
+            cot_rows, mine = after(cotangent[0], mine)
+            cot_rows = regroup(cot_rows, True)
         if size == 2:
             theirs = shift(mine, 1)
         else:
@@ -744,9 +761,7 @@
         states.append(prev)
         ups.append((mine, theirs))
     third = regroup(third, True)
-    w_tout = third[:, : 2 * local_w]
-    w_up = third[:, 2 * local_w : 2 * local_w + units]
-    w_down = third[:, 2 * local_w + units :]
+    w_up, w_down, w_tout = third[:, :units], third[:, units : 2 * units], third[:, 2 * units :]
     final = gate * prev + (1.0 - gate) * (mine.astype(F32) + theirs.astype(F32))
     final_rows = lax.dynamic_slice_in_dim(final, rank * (S // size), S // size, 0)
 
@@ -756,7 +771,7 @@
     resid = tok_f + sum_rot(attn_term, rows)
     unit2, inv2 = normalize(resid)
     normed2 = gather_rot((unit2 * gain2).astype(BF16))
-    act, slope = up_project(normed2, w_up)
+    act, slope = up_project(normed2, third, units)
 
     def mlp_term(first, count):
         return dot_nt(lax.slice_in_dim(act, first, first + count, axis=0), w_down)
@@ -765,17 +780,19 @@
 
     cot_all = gather_rot(cot_rows)
     grad_pre = (dot_nn(cot_all, w_down) * slope.astype(F32)).astype(BF16)
-    grad_down = scatter_grad(dot_tn(cot_all, act))
+    grad_down = regroup(dot_tn(cot_all, act).astype(BF16), False)
 
     def up_term(first, count):
         return dot_nt(lax.slice_in_dim(grad_pre, first, first + count, axis=0), w_up)
 
     grad_norm2 = sum_rot(up_term, rows)
-    grad_up = scatter_grad(dot_tn(normed2, grad_pre))
+    grad_up = regroup(dot_tn(normed2, grad_pre).astype(BF16), False)
     grad_resid = cot_rows.astype(F32) + norm_back(grad_norm2, gain2, unit2, inv2)
     grad_attn = gather_rot(grad_resid.astype(BF16))
     grad_att = dot_nn(grad_attn, w_tout).astype(BF16)
-    grad_tout = scatter_grad(dot_tn(grad_attn, att))
+    grad_tout = regroup(dot_tn(grad_attn, att).astype(BF16), False)
+    grad_att, grad_down = after(grad_att, grad_down)
+    grad_down = scatter_moved(grad_down)
 
     chain, kept_b, sums = None, None, []
     for block in reversed(range(blocks)):
@@ -799,6 +816,14 @@
         later, dupd, dsproj, aux, sum_b, part = outs
         kept_b = (dupd, dsproj, aux)
         sums.append(sum_b)
+        if block == blocks - 3:
+            part, grad_up = after(part, grad_up)
+            grad_up = scatter_moved(grad_up)
+        if block == blocks - 5:
+            part, grad_tout, grad_down = after(part, grad_tout, grad_down)
+            grad_tout = scatter_moved(grad_tout)
+        if block == 1:
+            part, grad_up = after(part, grad_up)
         if block > 0:
             if size == 2:
                 other = shift(part, 1)
@@ -811,8 +836,8 @@
     grad_st = jnp.concatenate(
         [dot_tn(norm_st, dsproj).astype(BF16), dot_tn(dupd, satt).astype(BF16)], 1
     )
-    aux, grad_st, mixed, final_rows = lax.optimization_barrier(
-        (aux, grad_st, mixed, final_rows)
+    aux, grad_st, mixed, final_rows, grad_tout = after(
+        aux, grad_st, mixed, final_rows, grad_tout
     )
     grad_st = regroup(grad_st, False)
 
@@ -821,19 +846,19 @@
     def tok_term(first, count):
         return dot_nt(lax.slice_in_dim(grad_proj, first, first + count, axis=0), w_tin)
 
-    grad_tin = dot_tn(normed, grad_proj).astype(BF16)
-    grad_tin, grad_st = lax.optimization_barrier((grad_tin, grad_st))
+    grad_table = table_grad(cells, table.shape[0]).reshape(-1, entries, heads)
+    grad_table = jnp.pad(grad_table, ((0, 0), (0, shard - entries), (0, 0)))
+    packed = jnp.concatenate([gate_grad[:, None], grad_table.reshape(model, heads)], 1)
+    packed = jnp.pad(packed, ((0, 0), (0, EXTRA - 1 - heads))).astype(BF16)
+    grad_tin = jnp.concatenate([dot_tn(normed, grad_proj).astype(BF16), packed], 1)
+    grad_tin, grad_st = after(grad_tin, grad_st)
+    grad_tin = regroup(grad_tin, False)
     grad_st = scatter_moved(grad_st)
     grad_sin, grad_sout = grad_st[:, :wide], grad_st[:, wide:]
+    grad_tin = scatter_moved(grad_tin)
+    grad_tin, packed = grad_tin[:, :wide], grad_tin[:, wide:].astype(F32)
     grad_norm1 = sum_rot(tok_term, rows)
     input_grad = grad_resid + norm_back(grad_norm1, gain1, unit1, inv1)
-
-    grad_table = table_grad(cells, table.shape[0])
-    packed = jnp.zeros((model // shard, shard, EXTRA), F32)
-    packed = packed.at[:, :, 0].set(gate_grad.reshape(-1, shard))
-    packed = packed.at[:, :entries, 1 : 1 + heads].set(grad_table.reshape(-1, entries, heads))
-    packed = scatter_grad(packed.reshape(model, EXTRA)).astype(F32)
-    grad_tin = scatter_grad(grad_tin)
 
     def gain_sum(shard_in, grad):
         return jnp.sum(shard_in.astype(F32) * grad.astype(F32), 1)

time: 1380 us -> 1340 us (0.971)
  waiting for transfers between devices: 240 us -> 204 us
  local copies, waits for them, and re-layouts: 55.8 us -> 39 us
  starting transfers between devices: 146 us -> 161 us
    ppermute x0 -> x1, waiting for transfers between devices: none -> 44.7 us  [local(): other = lax.ppermute(rel_table, ('mph', 'mpl'), [(0, 1), (1, 0)])]
    reduce_scatter x4 -> x5, waiting for transfers between devices: 142 us -> 104 us  [scatter_moved(): return lax.psum_scatter(moved, ORIG_DP, scatter_dimension=0, tiled=True)]
    all_gather x3, waiting for transfers between devices: 44.7 us -> 19.3 us  [gather_weight(): return lax.all_gather(shard, ORIG_DP, axis=0, tiled=True)]
    ppermute x24, waiting for transfers between devices: 52.5 us -> 35.7 us  [shift(): return lax.ppermute(arr, ('core', 'mpl'), pairs)]
    ppermute x24, starting transfers between devices: 106 us -> 121 us  [shift(): return lax.ppermute(arr, ('core', 'mpl'), pairs)]
    ppermute x16 -> x15, starting transfers between devices: 37.7 us -> 35.4 us  [regroup(): moved = lax.ppermute(arr, SWAP, pairs)]
    select_n x14 -> x12, other arithmetic: 47.8 us -> 45.7 us  [regroup(): return jnp.where(stays, arr, moved)]
  transfers between devices with their start and end apart: 50 -> 49, of which waited for: 15 -> 15; matrix products, arithmetic and copies ran while one was open for 31% -> 32% of each run, Pallas kernels for 32% -> 33%
where the time goes in v1:
time: 1340 us; the launch traced here: 1330 us
  Pallas kernels  443 us (33%)
  matrix products  284 us (21%)
  waiting for transfers between devices  204 us (15%)
  other arithmetic  183 us (14%)
  starting transfers between devices  161 us (12%)
  local copies, waits for them, and re-layouts  39 us (3%)
  between operations  18.6 us (1%)
    pallas_call x8, Pallas kernels, state_backward(): pl.pallas_call(functools.partial(state_backward_kernel, last), grid_spec=...  180 us
    pallas_call x8, Pallas kernels, state_forward(): pl.pallas_call(functools.partial(state_forward_kernel, first), grid_spec=...  131 us
    ppermute x24, starting transfers between devices, shift(): return lax.ppermute(arr, ('core', 'mpl'), pairs)  121 us
    dot_general x6, matrix products, dot_tn(): lax.dot_general(left, right, (((0,), (0,)), ((), ())), preferred_element_...  116 us
    dot_general x8, matrix products, dot_nt(): lax.dot_general(left, right, (((1,), (1,)), ((), ())), preferred_element_...  106 us
    reduce_scatter x5, waiting for transfers between devices, scatter_moved(): return lax.psum_scatter(moved, ORIG_DP, scatter_dimension=0, tiled=True)  104 us
    dot_general x3, matrix products, dot_nn(): lax.dot_general(left, right, (((1,), (0,)), ((), ())), preferred_element_...  61.7 us
    pallas_call x1, Pallas kernels, self_backward(): pl.pallas_call(self_backward_kernel, grid_spec=pltpu.PrefetchScalarGridSp...  56.2 us
  transfers between devices with their start and end apart: 49, of which 15 were waited for; matrix products, arithmetic and copies ran while one was open for 32% of the time, Pallas kernels for 33%

profile of v1, /device:TPU:0, one launch (start us, length us, event | category | flops | bytes accessed | tf_op | source)
XLA Modules:
  0.0 1331.5 jit_solution(18179686583503082864)
XLA Ops:
  14.2 44.7 %collective-permute-done.2 = bf16[2,4]{1,0:T(2,128)(2,1)S(1)} collective-permute-done((bf16[2,4]{1,0:T(2,128)(2,1)}, bf16[2,4]{1,0:T(2,128)(2,1)S(1)}, u32[]{:S(2)}, u32[]{:S(2)}) %collective-permute-start.2) | collective-permute-done | bytes 48 | tf_op jit(solution)/shard_map/ppermute | solution.py:688
  70.5 17.3 %broadcast_compare_fusion.26 = (pred[1024,512]{1,0:T(8,128)(4,1)S(1)}, pred[1024,512]{1,0:T(8,128)(4,1)S(1)}, pred[1024,512]{1,0:T(8,128)(4,1)}, pred[1024,512]{...) fusion(s32[1024]{0:T(1024)S(1)} %iota_add_fusion), kind=kLoop, calls=%fused_computation.130 | loop fusion | flops 31457280 | bytes 16781312 | tf_op jit(solution)/shard_map/eq | solution.py:114
  94.8 19.3 %all-gather.4.cloned.1.call-done = bf16[1024,2176]{1,0:T(8,128)(2,1)} async-done(((bf16[64,2176]{1,0:T(8,128)(2,1)}), bf16[1024,2176]{1,0:T(8,128)(2,1)}) %all-gather.4.cloned.1.call-update) | async-done | bytes 4456464 | tf_op jit(solution)/shard_map/all_gather | solution.py:650
  132.5 33.5 %select_select_fusion.bias = f32[4,1024,512]{2,1,0:T(8,128)} fusion(f32[4]{0:T(128)S(1)} %get-tuple-element.392, f32[4]{0:T(128)S(1)} %get-tuple-element.393, f32[4]{0:T(128)S(1)} %get-tuple-element.394, f32[4]{0:T(128)S(1)} %get-tuple-element.395, f32[4]{0:T(128)S(1)} %get-tuple-element.396, f32[4]{0:T(128)S(1)} %get-tuple-element.397, ...), kind=kLoop, calls=%fused_computation.43 | loop fusion | flops 67108864 | bytes 25166336 | tf_op jit(solution)/shard_map/jit(_where)/select_n | solution.py:114
  181.5 20.2 %convolution_convert_fusion.q.kp.kc.vp.vc.refs_5_.refs_6_.refs_7_.refs_8_.refs_9_.refs_11_.refs_12_.refs_13_ = bf16[4096,2048]{1,0:T(8,128)(2,1)} fusion(bf16[4096,1024]{1,0:T(8,128)(2,1)S(1)} %copy-done.10, bf16[1024,2048]{1,0:T(8,128)(2,1)S(1)} %slice_select_fusion), kind=kOutput, calls=%fused_computation.1 | convolution fusion | flops 17188257792 | bytes 29360128 | tf_op jit(solution)/shard_map/dot_general | solution.py:74
  208.9 38.9 %self_forward.1 = (bf16[4096,1024]{1,0:T(8,128)(2,1)}, f32[8,4,512]{2,1,0:T(4,128)}) custom-call(s32[3]{0:T(128)} %get-tuple-element.461.where, bf16[4096,2048]{1,0:T(8,128)(2,1)} %convolution_convert_fusion.q.kp.kc.vp.vc.refs_5_.refs_6_.refs_7_.refs_8_.refs_9_.refs_11_.refs_12_.refs_13_, ...), custom_call_target="tpu_custom_call" | custom-call | flops 8589934592 | bytes 33554432 | tf_op jit(solution)/shard_map/self_forward/pallas_call | solution.py:207
  270.5 74.3 %collective-permute-start.8 = (bf16[512,1024]{1,0:T(8,128)(2,1)}, bf16[512,1024]{1,0:T(8,128)(2,1)S(1)}, u32[]{:S(2)}, u32[]{:S(2)}) collective-permute-start(bf16[512,1024]{1,0:T(8,128)(2,1)} %get-tuple-element.153.refs_1_.refs_4_), channel_id=1, source_target_pairs={{0,2},{2,0},{1,3},{3,1},{4,6},{6,4},{5,7},{7,5},{8,10},{10,8},{9,1... | collective-permute-start | bytes 3145736 | tf_op jit(solution)/shard_map/ppermute | solution.py:56
  348.3 16.5 %state_forward.9 = (f32[512,1024]{1,0:T(8,128)}, bf16[4096,1024]{1,0:T(8,128)(2,1)}, bf16[4096,2048]{1,0:T(8,128)(2,1)}, bf16[4096,1024]{1,0:T(8,128)(2,1)}, bf1...) custom-call(s32[3]{0:T(128)} %get-tuple-element.460.where, ...), custom_call_target="tpu_custom_call", output_to_operand_aliasing={{1}: (11, {}), {2}: (12, {}), {3}: (13, {}), {4}: (14, {}),... | custom-call | flops 4831838208 | bytes 16777216 | tf_op jit(solution)/shard_map/state_forward/pallas_call | solution.py:417
  373.2 16.4 %state_forward.10 = (f32[512,1024]{1,0:T(8,128)}, bf16[4096,1024]{1,0:T(8,128)(2,1)}, bf16[4096,2048]{1,0:T(8,128)(2,1)}, bf16[4096,1024]{1,0:T(8,128)(2,1)}, bf...) custom-call(s32[3]{0:T(128)} %get-tuple-element.459.where, ...), custom_call_target="tpu_custom_call", output_to_operand_aliasing={{1}: (11, {}), {2}: (12, {}), {3}: (13, {}), {4}: (14, {}),... | custom-call | flops 4831838208 | bytes 16777216 | tf_op jit(solution)/shard_map/state_forward/pallas_call | solution.py:417
  393.4 16.8 %state_forward.11 = (f32[512,1024]{1,0:T(8,128)}, bf16[4096,1024]{1,0:T(8,128)(2,1)}, bf16[4096,2048]{1,0:T(8,128)(2,1)}, bf16[4096,1024]{1,0:T(8,128)(2,1)}, bf...) custom-call(s32[3]{0:T(128)} %get-tuple-element.458.where, ...), custom_call_target="tpu_custom_call", output_to_operand_aliasing={{1}: (11, {}), {2}: (12, {}), {3}: (13, {}), {4}: (14, {}),... | custom-call | flops 4831838208 | bytes 16777216 | tf_op jit(solution)/shard_map/state_forward/pallas_call | solution.py:417
  414.1 16.6 %state_forward.12 = (f32[512,1024]{1,0:T(8,128)}, bf16[4096,1024]{1,0:T(8,128)(2,1)}, bf16[4096,2048]{1,0:T(8,128)(2,1)}, bf16[4096,1024]{1,0:T(8,128)(2,1)}, bf...) custom-call(s32[3]{0:T(128)} %get-tuple-element.457.where, ...), custom_call_target="tpu_custom_call", output_to_operand_aliasing={{1}: (11, {}), {2}: (12, {}), {3}: (13, {}), {4}: (14, {}),... | custom-call | flops 4831838208 | bytes 16777216 | tf_op jit(solution)/shard_map/state_forward/pallas_call | solution.py:417
  454.7 16.8 %state_forward.14 = (f32[512,1024]{1,0:T(8,128)}, bf16[4096,1024]{1,0:T(8,128)(2,1)}, bf16[4096,2048]{1,0:T(8,128)(2,1)}, bf16[4096,1024]{1,0:T(8,128)(2,1)}, bf...) custom-call(s32[3]{0:T(128)} %get-tuple-element.455.where, ...), custom_call_target="tpu_custom_call", output_to_operand_aliasing={{1}: (11, {}), {2}: (12, {}), {3}: (13, {}), {4}: (14, {}),... | custom-call | flops 4831838208 | bytes 16777216 | tf_op jit(solution)/shard_map/state_forward/pallas_call | solution.py:417
  475.3 16.5 %state_forward.15 = (f32[512,1024]{1,0:T(8,128)}, bf16[4096,1024]{1,0:T(8,128)(2,1)}, bf16[4096,2048]{1,0:T(8,128)(2,1)}, bf16[4096,1024]{1,0:T(8,128)(2,1)}, bf...) custom-call(s32[3]{0:T(128)} %get-tuple-element.382.where, ...), custom_call_target="tpu_custom_call", output_to_operand_aliasing={{1}: (11, {}), {2}: (12, {}), {3}: (13, {}), {4}: (14, {}),... | custom-call | flops 4831838208 | bytes 16777216 | tf_op jit(solution)/shard_map/state_forward/pallas_call | solution.py:417
  533.8 30.4 %collective-permute-start.18 = (bf16[2048,1024]{1,0:T(8,128)(2,1)}, bf16[2048,1024]{1,0:T(8,128)(2,1)}, u32[]{:S(2)}, u32[]{:S(2)}) collective-permute-start(bf16[2048,1024]{1,0:T(8,128)(2,1)} %broadcast_select_fusion.7), channel_id=1, source_target_pairs={{0,2},{2,0},{1,3},{3,1},{4,6},{6,4},{5,7},{7,5},{8,10},{10,8},{9,1... | collective-permute-start | bytes 12582920 | tf_op jit(solution)/shard_map/ppermute | solution.py:56
  571.9 36.2 %up_project.1 = (bf16[4096,2048]{1,0:T(8,128)(2,1)}, bf16[4096,2048]{1,0:T(8,128)(2,1)}) custom-call(bf16[4096,1024]{1,0:T(8,128)(2,1)} %pad_maximum_fusion.2.rows, bf16[1024,5120]{1,0:T(8,128)(2,1)} %broadcast_select_fusion.weight), custom_call_target="tpu_custom_call" | custom-call | flops 17179869184 | bytes 46137344 | tf_op jit(solution)/shard_map/up_project/pallas_call | solution.py:620
  608.1 26.3 %multiply_convert_fusion = bf16[4096,2048]{1,0:T(8,128)(2,1)} fusion(bf16[4096,2048]{1,0:T(8,128)(2,1)} %get-tuple-element.208, bf16[2048,1024]{1,0:T(8,128)(2,1)} %collective-permute-done.18, bf16[2048,1024]{1,0:T(8,128)(2,1)} %broadcast_select_fusion.7, bf16[1024,5120]{1,0:T(8,128)(2,1)} %broadcast_select_fusion.weight), kind=kOutput, calls=%fused_computation | convolution fusion | flops 17221812224 | bytes 46137344 | tf_op jit(solution)/shard_map/dot_general | solution.py:74
  647.0 23.0 %fusion.34 = bf16[1024,2048]{1,0:T(8,128)(2,1)S(1)} fusion(bf16[4096,2048]{1,0:T(8,128)(2,1)} %get-tuple-element.209, bf16[2048,1024]{1,0:T(8,128)(2,1)} %collective-permute-done.18, bf16[2048,1024]{1,0:T(8,128)(2,1)} %broadcast_select_fusion.7), kind=kOutput, calls=%fused_computation.70 | convolution fusion | flops 17198743552 | bytes 29360128 | tf_op jit(solution)/shard_map/dot_general | solution.py:78
  672.7 18.3 %fusion.102 = (f32[2048]{0:T(1024)S(1)}, f32[2048]{0:T(1024)S(1)}, f32[2048,1024]{1,0:T(8,128)}) fusion(f32[2048]{0:T(1024)S(1)} %add_rsqrt_fusion, f32[2048,1024]{1,0:T(8,128)} %copy-done.2, f32[2048]{0:T(1024)S(1)} %broadcast_multiply_fusion.4, f32[1024]{0:T(1024)S(1)} %bitcast.178, bf16[2048,1024]{1,0:T(8,128)(2,1)} %collective-permute-done.20, ...), kind=kOutput, calls=%fused_computation.256 | convolution fusion | flops 8606707712 | bytes 33591296 | tf_op jit(solution)/shard_map/dot_general | solution.py:82
  705.1 22.8 %convolution_convert_fusion.4 = bf16[1024,2048]{1,0:T(8,128)(2,1)} fusion(bf16[4096,2048]{1,0:T(8,128)(2,1)} %multiply_convert_fusion, bf16[2048,1024]{1,0:T(8,128)(2,1)} %collective-permute-done.19, bf16[2048,1024]{1,0:T(8,128)(2,1)S(1)} %copy-done.7), kind=kOutput, calls=%fused_computation.73 | convolution fusion | flops 17198743552 | bytes 29360128 | tf_op jit(solution)/shard_map/dot_general | solution.py:78
  767.4 24.4 %state_backward.9 = (f32[512,1024]{1,0:T(8,128)}, bf16[4096,1024]{1,0:T(8,128)(2,1)}, bf16[4096,2048]{1,0:T(8,128)(2,1)}, bf16[4096,1536]{1,0:T(8,128)(2,1)}, f3...) custom-call(s32[3]{0:T(128)} %get-tuple-element.455.where, ...), custom_call_target="tpu_custom_call", output_to_operand_aliasing={{1}: (20, {}), {2}: (21, {}), {3}: (22, {})} | custom-call | flops 7247757312 | bytes 27262976 | tf_op jit(solution)/shard_map/state_backward/pallas_call | solution.py:566
  812.0 23.7 %state_backward.10 = (f32[512,1024]{1,0:T(8,128)}, bf16[4096,1024]{1,0:T(8,128)(2,1)}, bf16[4096,2048]{1,0:T(8,128)(2,1)}, bf16[4096,1536]{1,0:T(8,128)(2,1)}, f...) custom-call(s32[3]{0:T(128)} %get-tuple-element.456.where, ...), custom_call_target="tpu_custom_call", output_to_operand_aliasing={{1}: (20, {}), {2}: (21, {}), {3}: (22, {})} | custom-call | flops 7247757312 | bytes 27262976 | tf_op jit(solution)/shard_map/state_backward/pallas_call | solution.py:566
  852.8 24.1 %state_backward.11 = (f32[512,1024]{1,0:T(8,128)}, bf16[4096,1024]{1,0:T(8,128)(2,1)}, bf16[4096,2048]{1,0:T(8,128)(2,1)}, bf16[4096,1536]{1,0:T(8,128)(2,1)}, f...) custom-call(s32[3]{0:T(128)} %get-tuple-element.457.where, ...), custom_call_target="tpu_custom_call", output_to_operand_aliasing={{1}: (20, {}), {2}: (21, {}), {3}: (22, {})} | custom-call | flops 7247757312 | bytes 27262976 | tf_op jit(solution)/shard_map/state_backward/pallas_call | solution.py:566
  878.4 18.9 %add_convert_fusion = bf16[2048,1024]{1,0:T(8,128)(2,1)} fusion(f32[2048,1024]{1,0:T(8,128)} %copy-done.2, bf16[2048,1024]{1,0:T(8,128)(2,1)} %collective-permute-done.32, bf16[1024,5120]{1,0:T(8,128)(2,1)} %broadcast_select_fusion.weight, bf16[4096,2048]{1,0:T(8,128)(2,1)} %get-tuple-element.209), kind=kOutput, calls=%fused_computation.33 | convolution fusion | flops 8598323200 | bytes 29360128 | tf_op jit(solution)/shard_map/dot_general | solution.py:82
  902.6 23.8 %state_backward.12 = (f32[512,1024]{1,0:T(8,128)}, bf16[4096,1024]{1,0:T(8,128)(2,1)}, bf16[4096,2048]{1,0:T(8,128)(2,1)}, bf16[4096,1536]{1,0:T(8,128)(2,1)}, f...) custom-call(s32[3]{0:T(128)} %get-tuple-element.458.where, ...), custom_call_target="tpu_custom_call", output_to_operand_aliasing={{1}: (20, {}), {2}: (21, {}), {3}: (22, {})} | custom-call | flops 7247757312 | bytes 27262976 | tf_op jit(solution)/shard_map/state_backward/pallas_call | solution.py:566
  931.8 23.6 %state_backward.13 = (f32[512,1024]{1,0:T(8,128)}, bf16[4096,1024]{1,0:T(8,128)(2,1)}, bf16[4096,2048]{1,0:T(8,128)(2,1)}, bf16[4096,1536]{1,0:T(8,128)(2,1)}, f...) custom-call(s32[3]{0:T(128)} %get-tuple-element.459.where, ...), custom_call_target="tpu_custom_call", output_to_operand_aliasing={{1}: (20, {}), {2}: (21, {}), {3}: (22, {})} | custom-call | flops 7247757312 | bytes 27262976 | tf_op jit(solution)/shard_map/state_backward/pallas_call | solution.py:566
  959.3 23.6 %state_backward.14 = (f32[512,1024]{1,0:T(8,128)}, bf16[4096,1024]{1,0:T(8,128)(2,1)}, bf16[4096,2048]{1,0:T(8,128)(2,1)}, bf16[4096,1536]{1,0:T(8,128)(2,1)}, f...) custom-call(s32[3]{0:T(128)} %get-tuple-element.460.where, ...), custom_call_target="tpu_custom_call", output_to_operand_aliasing={{1}: (20, {}), {2}: (21, {}), {3}: (22, {})} | custom-call | flops 7247757312 | bytes 27262976 | tf_op jit(solution)/shard_map/state_backward/pallas_call | solution.py:566
  992.7 23.8 %state_backward.15 = (f32[512,1024]{1,0:T(8,128)}, bf16[4096,1024]{1,0:T(8,128)(2,1)}, bf16[4096,2048]{1,0:T(8,128)(2,1)}, bf16[4096,1536]{1,0:T(8,128)(2,1)}, f...) custom-call(s32[3]{0:T(128)} %get-tuple-element.461.where, ...), custom_call_target="tpu_custom_call", output_to_operand_aliasing={{1}: (20, {}), {2}: (21, {}), {3}: (22, {})} | custom-call | flops 7247757312 | bytes 27262976 | tf_op jit(solution)/shard_map/state_backward/pallas_call | solution.py:566
  1030.7 19.9 %convolution_convert_fusion.3 = bf16[1024,2048]{1,0:T(8,128)(2,1)S(1)} fusion(bf16[4096,1024]{1,0:T(8,128)(2,1)} %get-tuple-element.255, bf16[4096,2048]{1,0:T(8,128)(2,1)S(1)} %copy-done.1), kind=kOutput, calls=%fused_computation.72 | convolution fusion | flops 17181966336 | bytes 29360128 | tf_op jit(solution)/shard_map/dot_general | solution.py:78
  1057.3 56.2 %self_backward.1 = (bf16[4096,2048]{1,0:T(8,128)(2,1)}, f32[4,5,128,128]{3,2,1,0:T(8,128)}) custom-call(s32[3]{0:T(128)} %get-tuple-element.461.where, bf16[4096,2048]{1,0:T(8,128)(2,1)} %convolution_convert_fusion.q.kp.kc.vp.vc.refs_5_.refs_6_.refs_7_.refs_8_.refs_9_.refs_11_.refs_12_.refs_13_, ...), custom_call_target="tpu_custom_call" | custom-call | flops 21474836480 | bytes 71303168 | tf_op jit(solution)/shard_map/self_backward/pallas_call | solution.py:306
  1120.9 23.0 %convolution_convert_fusion.2 = bf16[1024,2048]{1,0:T(8,128)(2,1)S(1)} fusion(bf16[4096,1024]{1,0:T(8,128)(2,1)} %pad_maximum_fusion, bf16[4096,2048]{1,0:T(8,128)(2,1)} %get-tuple-element.264), kind=kOutput, calls=%fused_computation.71 | convolution fusion | flops 17181966336 | bytes 29360128 | tf_op jit(solution)/shard_map/dot_general | solution.py:78
  1208.2 31.3 %reduce-scatter.14.cloned.1.call-done = bf16[64,3072]{1,0:T(8,128)(2,1)} async-done(((bf16[1024,3072]{1,0:T(8,128)(2,1)}), bf16[64,3072]{1,0:T(8,128)(2,1)}) %reduce-scatter.14.cloned.1.call-update) | async-done | bytes 393232 | tf_op jit(solution)/shard_map/reduce_scatter | solution.py:654
  1244.5 72.3 %reduce-scatter.16.cloned.1.call-done = bf16[64,2176]{1,0:T(8,128)(2,1)} async-done(((bf16[1024,2176]{1,0:T(8,128)(2,1)}), bf16[64,2176]{1,0:T(8,128)(2,1)}) %reduce-scatter.16.cloned.1.call-update) | async-done | bytes 278544 | tf_op jit(solution)/shard_map/reduce_scatter | solution.py:654
  (375 shorter events, 419.4 us)
Async XLA Ops:
  7.2 106.9 %all-gather.4.cloned.1.call-start = ((), (), s32[]{:S(2)}) async-start(), calls=%async_computation.5 | async-start | bytes 4734976 | tf_op jit(solution)/shard_map/all_gather | solution.py:650
  7.2 53.8 %collective-permute-start.1 = (bf16[2048,1024]{1,0:T(8,128)(2,1)}, bf16[2048,1024]{1,0:T(8,128)(2,1)}, u32[]{:S(2)}, u32[]{:S(2)}) collective-permute-start(bf16[2048,1024]{1,0:T(8,128)(2,1)} %bitcast.151), channel_id=1, source_target_pairs={{1,2},{2,1},{5,6},{6,5},{9,10},{10,9},{13,14},{14,13},{17,18},{18,... | collective-permute-start | bytes 12582920 | tf_op jit(solution)/shard_map/ppermute | solution.py:42
  10.1 48.8 %collective-permute-start.2 = (bf16[2,4]{1,0:T(2,128)(2,1)}, bf16[2,4]{1,0:T(2,128)(2,1)S(1)}, u32[]{:S(2)}, u32[]{:S(2)}) collective-permute-start(bf16[2,4]{1,0:T(2,128)(2,1)} %param.19), channel_id=1, source_target_pairs={{0,1},{1,0},{2,3},{3,2},{4,5},{5,4},{6,7},{7,6},{8,9},{9,8},{10,11... | collective-permute-start | bytes 56 | tf_op jit(solution)/shard_map/ppermute | solution.py:688
  60.9 140.8 %all-gather.6.cloned.1.call-start = ((), (), s32[]{:S(2)}) async-start(), calls=%async_computation.6 | async-start | bytes 6684672 | tf_op jit(solution)/shard_map/all_gather | solution.py:650
  68.7 20.2 %collective-permute-start.4 = (f32[256,1024]{1,0:T(8,128)}, f32[256,1024]{1,0:T(8,128)}, u32[]{:S(2)}, u32[]{:S(2)}) collective-permute-start(f32[256,1024]{1,0:T(8,128)} %add_bitcast_fusion), channel_id=1, source_target_pairs={{1,2},{2,1},{5,6},{6,5},{9,10},{10,9},{13,14},{14,13},{17,18},{18,... | collective-permute-start | bytes 3145736 | tf_op jit(solution)/shard_map/ppermute | solution.py:42
  89.1 27.8 %collective-permute-start.5 = (f32[256,1024]{1,0:T(8,128)S(1)}, f32[256,1024]{1,0:T(8,128)}, u32[]{:S(2)}, u32[]{:S(2)}) collective-permute-start(f32[256,1024]{1,0:T(8,128)S(1)} %broadcast_select_fusion.11), channel_id=1, source_target_pairs={{0,2},{2,0},{1,3},{3,1},{4,6},{6,4},{5,7},{7,5},{8,10},{10,8},{9,1... | collective-permute-start | bytes 3145736 | tf_op jit(solution)/shard_map/ppermute | solution.py:56
  116.8 248.0 %all-gather.8.cloned.1.call-start = ((), (), s32[]{:S(2)}) async-start(), calls=%async_computation.7 | async-start | bytes 11141120 | tf_op jit(solution)/shard_map/all_gather | solution.py:650
  128.7 37.4 %collective-permute-start.3 = (bf16[2048,1024]{1,0:T(8,128)(2,1)S(1)}, bf16[2048,1024]{1,0:T(8,128)(2,1)}, u32[]{:S(2)}, u32[]{:S(2)}) collective-permute-start(bf16[2048,1024]{1,0:T(8,128)(2,1)S(1)} %fusion.6), channel_id=1, source_target_pairs={{0,2},{2,0},{1,3},{3,1},{4,6},{6,4},{5,7},{7,5},{8,10},{10,8},{9,1... | collective-permute-start | bytes 12582920 | tf_op jit(solution)/shard_map/ppermute | solution.py:56
  129.0 44.9 %collective-permute-start.6 = (bf16[1024,2176]{1,0:T(8,128)(2,1)}, bf16[1024,2176]{1,0:T(8,128)(2,1)}, u32[]{:S(2)}, u32[]{:S(2)}) collective-permute-start(bf16[1024,2176]{1,0:T(8,128)(2,1)} %all-gather.4.cloned.1.call-done), channel_id=1, source_target_pairs={{1,2},{2,1},{5,6},{6,5},{9,10},{10,9},{13,14},{14,13},{17,18},{18,... | collective-permute-start | bytes 13369352 | tf_op jit(solution)/shard_map/ppermute | solution.py:42
  201.7 724.6 %reduce-scatter.8.cloned.1.call-start = ((), (), s32[]{:S(2)}) async-start(), calls=%async_computation.8 | async-start | bytes 4456448 | tf_op jit(solution)/shard_map/reduce_scatter | solution.py:654
  201.8 46.1 %collective-permute-start.7 = (bf16[1024,3072]{1,0:T(8,128)(2,1)}, bf16[1024,3072]{1,0:T(8,128)(2,1)}, u32[]{:S(2)}, u32[]{:S(2)}) collective-permute-start(bf16[1024,3072]{1,0:T(8,128)(2,1)} %all-gather.6.cloned.1.call-done), channel_id=1, source_target_pairs={{1,2},{2,1},{5,6},{6,5},{9,10},{10,9},{13,14},{14,13},{17,18},{18,... | collective-permute-start | bytes 18874376 | tf_op jit(solution)/shard_map/ppermute | solution.py:42
  270.5 76.8 %collective-permute-start.8 = (bf16[512,1024]{1,0:T(8,128)(2,1)}, bf16[512,1024]{1,0:T(8,128)(2,1)S(1)}, u32[]{:S(2)}, u32[]{:S(2)}) collective-permute-start(bf16[512,1024]{1,0:T(8,128)(2,1)} %get-tuple-element.153.refs_1_.refs_4_), channel_id=1, source_target_pairs={{0,2},{2,0},{1,3},{3,1},{4,6},{6,4},{5,7},{7,5},{8,10},{10,8},{9,1... | collective-permute-start | bytes 3145736 | tf_op jit(solution)/shard_map/ppermute | solution.py:56
  364.8 127.0 %collective-permute-start.16 = (bf16[1024,5120]{1,0:T(8,128)(2,1)}, bf16[1024,5120]{1,0:T(8,128)(2,1)}, u32[]{:S(2)}, u32[]{:S(2)}) collective-permute-start(bf16[1024,5120]{1,0:T(8,128)(2,1)} %all-gather.8.cloned.1.call-done), channel_id=1, source_target_pairs={{1,2},{2,1},{5,6},{6,5},{9,10},{10,9},{13,14},{14,13},{17,18},{18,... | collective-permute-start | bytes 31457288 | tf_op jit(solution)/shard_map/ppermute | solution.py:42
  509.3 19.9 %collective-permute-start.15 = (bf16[2048,1024]{1,0:T(8,128)(2,1)}, bf16[2048,1024]{1,0:T(8,128)(2,1)}, u32[]{:S(2)}, u32[]{:S(2)}) collective-permute-start(bf16[2048,1024]{1,0:T(8,128)(2,1)} %bitcast.47), channel_id=1, source_target_pairs={{1,2},{2,1},{5,6},{6,5},{9,10},{10,9},{13,14},{14,13},{17,18},{18,... | collective-permute-start | bytes 12582920 | tf_op jit(solution)/shard_map/ppermute | solution.py:42
  527.2 37.0 %collective-permute-start.19 = (bf16[2048,1024]{1,0:T(8,128)(2,1)S(1)}, bf16[2048,1024]{1,0:T(8,128)(2,1)}, u32[]{:S(2)}, u32[]{:S(2)}) collective-permute-start(bf16[2048,1024]{1,0:T(8,128)(2,1)S(1)} %multiply_convert_fusion.1), channel_id=1, source_target_pairs={{0,2},{2,0},{1,3},{3,1},{4,6},{6,4},{5,7},{7,5},{8,10},{10,8},{9,1... | collective-permute-start | bytes 12582920 | tf_op jit(solution)/shard_map/ppermute | solution.py:56
  533.8 74.3 %collective-permute-start.18 = (bf16[2048,1024]{1,0:T(8,128)(2,1)}, bf16[2048,1024]{1,0:T(8,128)(2,1)}, u32[]{:S(2)}, u32[]{:S(2)}) collective-permute-start(bf16[2048,1024]{1,0:T(8,128)(2,1)} %broadcast_select_fusion.7), channel_id=1, source_target_pairs={{0,2},{2,0},{1,3},{3,1},{4,6},{6,4},{5,7},{7,5},{8,10},{10,8},{9,1... | collective-permute-start | bytes 12582920 | tf_op jit(solution)/shard_map/ppermute | solution.py:56
  647.0 25.7 %collective-permute-start.20 = (bf16[2048,1024]{1,0:T(8,128)(2,1)S(1)}, bf16[2048,1024]{1,0:T(8,128)(2,1)}, u32[]{:S(2)}, u32[]{:S(2)}) collective-permute-start(bf16[2048,1024]{1,0:T(8,128)(2,1)S(1)} %fusion.41), channel_id=1, source_target_pairs={{0,2},{2,0},{1,3},{3,1},{4,6},{6,4},{5,7},{7,5},{8,10},{10,8},{9,1... | collective-permute-start | bytes 12582920 | tf_op jit(solution)/shard_map/ppermute | solution.py:56
  670.1 60.3 %collective-permute-start.22 = (bf16[1024,2048]{1,0:T(8,128)(2,1)S(1)}, bf16[1024,2048]{1,0:T(8,128)(2,1)}, u32[]{:S(2)}, u32[]{:S(2)}) collective-permute-start(bf16[1024,2048]{1,0:T(8,128)(2,1)S(1)} %fusion.34), channel_id=1, source_target_pairs={{2,1},{1,2},{6,5},{5,6},{10,9},{9,10},{14,13},{13,14},{18,17},{17,... | collective-permute-start | bytes 12582920 | tf_op jit(solution)/shard_map/ppermute | solution.py:42
  704.3 28.7 %collective-permute-start.21 = (bf16[2048,1024]{1,0:T(8,128)(2,1)}, bf16[2048,1024]{1,0:T(8,128)(2,1)}, u32[]{:S(2)}, u32[]{:S(2)}) collective-permute-start(bf16[2048,1024]{1,0:T(8,128)(2,1)} %get-tuple-element.378), channel_id=1, source_target_pairs={{0,2},{2,0},{1,3},{3,1},{4,6},{6,4},{5,7},{7,5},{8,10},{10,8},{9,1... | collective-permute-start | bytes 12582920 | tf_op jit(solution)/shard_map/ppermute | solution.py:56
  727.8 78.4 %collective-permute-start.25 = (bf16[1024,2048]{1,0:T(8,128)(2,1)}, bf16[1024,2048]{1,0:T(8,128)(2,1)}, u32[]{:S(2)}, u32[]{:S(2)}) collective-permute-start(bf16[1024,2048]{1,0:T(8,128)(2,1)} %convolution_convert_fusion.4), channel_id=1, source_target_pairs={{2,1},{1,2},{6,5},{5,6},{10,9},{9,10},{14,13},{13,14},{18,17},{17,... | collective-permute-start | bytes 12582920 | tf_op jit(solution)/shard_map/ppermute | solution.py:42
  763.9 219.0 %reduce-scatter.10.cloned.1.call-start = ((), (), s32[]{:S(2)}) async-start(), calls=%async_computation.9 | async-start | bytes 4456448 | tf_op jit(solution)/shard_map/reduce_scatter | solution.py:654
  806.1 72.3 %collective-permute-start.32 = (bf16[2048,1024]{1,0:T(8,128)(2,1)}, bf16[2048,1024]{1,0:T(8,128)(2,1)}, u32[]{:S(2)}, u32[]{:S(2)}) collective-permute-start(bf16[2048,1024]{1,0:T(8,128)(2,1)} %fusion.35), channel_id=1, source_target_pairs={{0,2},{2,0},{1,3},{3,1},{4,6},{6,4},{5,7},{7,5},{8,10},{10,8},{9,1... | collective-permute-start | bytes 12582920 | tf_op jit(solution)/shard_map/ppermute | solution.py:56
  849.8 50.2 %collective-permute-start.28 = (bf16[1024,1024]{1,0:T(8,128)(2,1)S(1)}, bf16[1024,1024]{1,0:T(8,128)(2,1)}, u32[]{:S(2)}, u32[]{:S(2)}) collective-permute-start(bf16[1024,1024]{1,0:T(8,128)(2,1)S(1)} %fusion.70), channel_id=1, source_target_pairs={{2,1},{1,2},{6,5},{5,6},{10,9},{9,10},{14,13},{13,14},{18,17},{17,... | collective-permute-start | bytes 6291464 | tf_op jit(solution)/shard_map/ppermute | solution.py:42
  851.8 202.0 %reduce-scatter.12.cloned.1.call-start = ((), (), s32[]{:S(2)}) async-start(), calls=%async_computation.10 | async-start | bytes 2228224 | tf_op jit(solution)/shard_map/reduce_scatter | solution.py:654
  876.9 24.7 %collective-permute-start.27 = (bf16[512,1024]{1,0:T(8,128)(2,1)}, bf16[512,1024]{1,0:T(8,128)(2,1)S(1)}, u32[]{:S(2)}, u32[]{:S(2)}) collective-permute-start(bf16[512,1024]{1,0:T(8,128)(2,1)} %get-tuple-element.231.refs_1_), channel_id=1, source_target_pairs={{0,2},{2,0},{1,3},{3,1},{4,6},{6,4},{5,7},{7,5},{8,10},{10,8},{9,1... | collective-permute-start | bytes 3145736 | tf_op jit(solution)/shard_map/ppermute | solution.py:56
  897.3 89.7 %collective-permute-start.33 = (bf16[2048,1024]{1,0:T(8,128)(2,1)}, bf16[2048,1024]{1,0:T(8,128)(2,1)}, u32[]{:S(2)}, u32[]{:S(2)}) collective-permute-start(bf16[2048,1024]{1,0:T(8,128)(2,1)} %add_convert_fusion), channel_id=1, source_target_pairs={{2,1},{1,2},{6,5},{5,6},{10,9},{9,10},{14,13},{13,14},{18,17},{17,... | collective-permute-start | bytes 12582920 | tf_op jit(solution)/shard_map/ppermute | solution.py:42
  927.5 28.1 %collective-permute-start.34 = (bf16[512,1024]{1,0:T(8,128)(2,1)}, bf16[512,1024]{1,0:T(8,128)(2,1)}, u32[]{:S(2)}, u32[]{:S(2)}) collective-permute-start(bf16[512,1024]{1,0:T(8,128)(2,1)} %get-tuple-element.258), channel_id=1, source_target_pairs={{0,2},{2,0},{1,3},{3,1},{4,6},{6,4},{5,7},{7,5},{8,10},{10,8},{9,1... | collective-permute-start | bytes 3145736 | tf_op jit(solution)/shard_map/ppermute | solution.py:56
  957.1 28.8 %collective-permute-start.35 = (f32[256,1024]{1,0:T(8,128)S(1)}, f32[256,1024]{1,0:T(8,128)S(1)}, u32[]{:S(2)}, u32[]{:S(2)}) collective-permute-start(f32[256,1024]{1,0:T(8,128)S(1)} %fusion.74), channel_id=1, source_target_pairs={{2,1},{1,2},{6,5},{5,6},{10,9},{9,10},{14,13},{13,14},{18,17},{17,... | collective-permute-start | bytes 3145736 | tf_op jit(solution)/shard_map/ppermute | solution.py:42
  991.7 247.9 %reduce-scatter.14.cloned.1.call-start = ((), (), s32[]{:S(2)}) async-start(), calls=%async_computation.11 | async-start | bytes 6684672 | tf_op jit(solution)/shard_map/reduce_scatter | solution.py:654
  1053.8 92.6 %collective-permute-start.38 = (bf16[1024,3072]{1,0:T(8,128)(2,1)}, bf16[1024,3072]{1,0:T(8,128)(2,1)}, u32[]{:S(2)}, u32[]{:S(2)}) collective-permute-start(bf16[1024,3072]{1,0:T(8,128)(2,1)} %pad_maximum_fusion.4), channel_id=1, source_target_pairs={{2,1},{1,2},{6,5},{5,6},{10,9},{9,10},{14,13},{13,14},{18,17},{17,... | collective-permute-start | bytes 18874376 | tf_op jit(solution)/shard_map/ppermute | solution.py:42
  1149.9 166.8 %reduce-scatter.16.cloned.1.call-start = ((), (), s32[]{:S(2)}) async-start(), calls=%async_computation.12 | async-start | bytes 4734976 | tf_op jit(solution)/shard_map/reduce_scatter | solution.py:654
  1164.4 23.1 %collective-permute-start.39 = (bf16[1024,2176]{1,0:T(8,128)(2,1)}, bf16[1024,2176]{1,0:T(8,128)(2,1)S(1)}, u32[]{:S(2)}, u32[]{:S(2)}) collective-permute-start(bf16[1024,2176]{1,0:T(8,128)(2,1)} %fusion.27), channel_id=1, source_target_pairs={{2,1},{1,2},{6,5},{5,6},{10,9},{9,10},{14,13},{13,14},{18,17},{17,... | collective-permute-start | bytes 13369352 | tf_op jit(solution)/shard_map/ppermute | solution.py:42
  (95 other events, 1607.6 us)
Sparse Core Ops, SparseCore 0:
  61.1 52.9 all-gather.3
  117.0 60.3 all-gather.5
  201.9 92.8 all-gather.7
  764.1 70.9 reduce-scatter.7
  851.9 72.0 reduce-scatter.9
  991.8 59.5 reduce-scatter.11
  1150.0 89.5 reduce-scatter.13
  1243.4 73.2 reduce-scatter.15

commit v2 on v1

--- a/solution.py
+++ b/solution.py
@@ -105,14 +105,32 @@
     return magnitude + half * (offset > 0).astype(jnp.int32)
 
 
-def window_bias(table):
-    key_pos = lax.broadcasted_iota(jnp.int32, (2 * W, W), 0) - W
-    query_pos = lax.broadcasted_iota(jnp.int32, (2 * W, W), 1)
-    which = bucket_of(key_pos - query_pos, table.shape[0] // 2)
-    bias = jnp.zeros((table.shape[1], 2 * W, W), F32)
-    for entry in range(table.shape[0]):
-        bias = jnp.where((which == entry)[None], table[entry][:, None, None], bias)
-    return bias
+def near_bias(table):
+    entries, heads = table.shape
+    diag = lax.broadcasted_iota(jnp.int32, (3, TILE, TILE), 0) - 1
+    key_pos = lax.broadcasted_iota(jnp.int32, (3, TILE, TILE), 1)
+    query_pos = lax.broadcasted_iota(jnp.int32, (3, TILE, TILE), 2)
+    which = bucket_of(diag * TILE + key_pos - query_pos, entries // 2)
+    near = jnp.zeros((heads, 3, TILE, TILE), F32)
+    for entry in range(entries):
+        near = jnp.where((which == entry)[None], table[entry][:, None, None, None], near)
+    far = jnp.stack([table[entries // 2 - 1], table[entries - 1]], 1)
+    far = jnp.broadcast_to(far[:, :, None, None], (heads, 2, TILE, TILE))
+    return jnp.concatenate([near, far], 1)
+
+
+def tile_slot(kt, qt):
+    diag = kt - W // TILE - qt
+    return diag + 1 if -1 <= diag <= 1 else (3 if diag < 0 else 4)
+
+
+def fill_bias(near, bias):
+    for h in range(near.shape[0]):
+        for kt in range(2 * W // TILE):
+            for qt in range(W // TILE):
+                bias[h, kt * TILE : (kt + 1) * TILE, qt * TILE : (qt + 1) * TILE] = near[
+                    h, tile_slot(kt, qt)
+                ]
 
 
 def table_grad(cells, entries):
@@ -174,8 +192,13 @@
     return grad_queries, grad_keys, grad_values, grad_scores
 
 
-def self_forward_kernel(where, q, kp, kc, vp, vc, bias, out, lse):
+def self_forward_kernel(where, q, kp, kc, vp, vc, near, out, lse, bias):
     block = pl.program_id(0)
+
+    @pl.when(block == 0)
+    def _():
+        fill_bias(near, bias)
+
     edge = jnp.where(block == 0, NEG, 0.0)
     allowed = allowed_keys(block, where[1])
     for h in range(bias.shape[0]):
@@ -198,10 +221,10 @@
     return at
 
 
-def self_forward(where, proj, bias):
+def self_forward(where, proj, near):
     seq_len, width = proj.shape
     local_w = width // 4
-    heads = bias.shape[0]
+    heads = near.shape[0]
     blocks = seq_len // W
     at = self_specs(blocks, local_w, lambda i: i)
     return pl.pallas_call(
@@ -215,12 +238,13 @@
                 at(2, 0),
                 at(3, -1),
                 at(3, 0),
-                pl.BlockSpec(bias.shape, lambda i, where: (0, 0, 0)),
+                pl.BlockSpec(near.shape, lambda i, where: (0, 0, 0, 0)),
             ],
             out_specs=[
                 at(0, 0),
                 pl.BlockSpec((1, heads, W), lambda i, where: (i, 0, 0)),
             ],
+            scratch_shapes=[pltpu.VMEM((heads, 2 * W, W), F32)],
         ),
         out_shape=[
             jax.ShapeDtypeStruct((seq_len, 2 * local_w), BF16),
@@ -229,15 +253,15 @@
         compiler_params=pltpu.CompilerParams(vmem_limit_bytes=VMEM_BYTES),
         cost_estimate=pl.CostEstimate(
             flops=seq_len * 2 * W * local_w * 4,
-            bytes_accessed=seq_len * local_w * 12 + bias.size * 4,
+            bytes_accessed=seq_len * local_w * 12,
             transcendentals=seq_len * 2 * W * heads,
         ),
         name="self_forward",
-    )(where, proj, proj, proj, proj, proj, bias)
+    )(where, proj, proj, proj, proj, proj, near)
 
 
 def self_backward_kernel(
-    where, q, kp, kc, vp, vc, bias, dout, out, lse, aux, grad_proj, cells, carry
+    where, q, kp, kc, vp, vc, near, dout, out, lse, aux, grad_proj, cells, carry, bias
 ):
     step = pl.program_id(0)
     block = pl.num_programs(0) - 1 - step
@@ -249,6 +273,7 @@
 
     @pl.when(step == 0)
     def _():
+        fill_bias(near, bias)
         carry[...] = jnp.zeros_like(carry)
         cells[...] = jnp.zeros_like(cells)
 
@@ -270,9 +295,7 @@
             for qt in range(tiles):
                 source, row = (ds0, kt) if kt < tiles else (ds1, kt - tiles)
                 cell = source[row * TILE : (row + 1) * TILE, qt * TILE : (qt + 1) * TILE]
-                diag = kt - tiles - qt
-                slot = diag + 1 if -1 <= diag <= 1 else (3 if diag < 0 else 4)
-                parts[slot].append(cell)
+                parts[tile_slot(kt, qt)].append(cell)
         for slot, group in parts.items():
             cells[h, slot] += functools.reduce(jnp.add, group)
         grad_proj[:, cols] = (jnp.transpose(dq0 + dq1) * SCALE).astype(BF16)
@@ -289,10 +312,10 @@
         carry[:, vcols] = dv0
 
 
-def self_backward(where, proj, bias, grad_att, att, lse, aux):
+def self_backward(where, proj, near, grad_att, att, lse, aux):
     seq_len, width = proj.shape
     local_w = width // 4
-    heads = bias.shape[0]
+    heads = near.shape[0]
     blocks = seq_len // W
 
     def order(i):
@@ -314,9 +337,7 @@
                 at(2, 0),
                 at(3, -1),
                 at(3, 0),
-                pl.BlockSpec(
-                    bias.shape, lambda i, where: (0, 0, 0), pipeline_mode=pl.Buffered(1)
-                ),
+                pl.BlockSpec(near.shape, lambda i, where: (0, 0, 0, 0)),
                 at(0, 0),
                 at(0, 0),
                 pl.BlockSpec((1, heads, W), lambda i, where: (order(i), 0, 0)),
@@ -326,7 +347,10 @@
                 pl.BlockSpec((W, width), whole),
                 pl.BlockSpec((heads, 5, TILE, TILE), lambda i, where: (0, 0, 0, 0)),
             ],
-            scratch_shapes=[pltpu.VMEM((W, 2 * local_w), F32)],
+            scratch_shapes=[
+                pltpu.VMEM((W, 2 * local_w), F32),
+                pltpu.VMEM((heads, 2 * W, W), F32),
+            ],
         ),
         out_shape=[
             jax.ShapeDtypeStruct((seq_len, width), BF16),
@@ -335,11 +359,11 @@
         compiler_params=pltpu.CompilerParams(vmem_limit_bytes=VMEM_BYTES),
         cost_estimate=pl.CostEstimate(
             flops=seq_len * 2 * W * local_w * 10,
-            bytes_accessed=seq_len * local_w * 30 + bias.size * 4,
+            bytes_accessed=seq_len * local_w * 30,
             transcendentals=seq_len * 2 * W * heads,
         ),
         name="self_backward",
-    )(where, proj, proj, proj, proj, proj, bias, grad_att, att, lse, aux)
+    )(where, proj, proj, proj, proj, proj, near, grad_att, att, lse, aux)
 
 
 def state_forward_kernel(first, where, *refs):
@@ -647,7 +671,18 @@
 
 
 def gather_weight(shard):
-    return lax.all_gather(shard, ORIG_DP, axis=0, tiled=True)
+    if lax.axis_size(("mph", "mpl")) == 2:
+        whole = lax.all_gather(shard, ("mph", "mpl") + ORIG_DP, axis=0, tiled=True)
+        model = whole.shape[0] // 2
+        first = lax.axis_index(GRP) * model
+    else:
+        whole = regroup(lax.all_gather(shard, ORIG_DP, axis=0, tiled=True), True)
+        model, first = whole.shape[0], 0
+
+    def take(start, stop):
+        return lax.dynamic_slice(whole, (first, start), (model, stop - start))
+
+    return whole, take
 
 
 def scatter_moved(moved):
@@ -684,32 +719,28 @@
     entries = rel_table.shape[0]
     extra = jnp.zeros((shard, EXTRA), BF16)
     extra = lax.dynamic_update_slice(extra, small, (0, 0))
-    if lax.axis_size(("mph", "mpl")) == 2:
-        other = lax.ppermute(rel_table, ("mph", "mpl"), [(0, 1), (1, 0)])
-        table = jnp.where(
-            lax.axis_index(("mph", "mpl")) == 0,
-            jnp.concatenate([rel_table, other], 1),
-            jnp.concatenate([other, rel_table], 1),
-        )
-    else:
-        table = lax.all_gather(rel_table, ("mph", "mpl"), axis=1, tiled=True)
-    extra = lax.dynamic_update_slice(extra, table, (0, 4))
+    extra = lax.dynamic_update_slice(extra, rel_table, (0, 4))
+    digits = jnp.stack([prefix // 64, prefix % 64], 1).astype(BF16)
+    extra = lax.dynamic_update_slice(extra, digits, (0, 4 + heads))
     tok_rows = regroup(tokens[0], True)
     wide = 4 * local_w
     shard_tin = tok_in_proj.reshape(shard, wide)
     shard_sin = st_in_proj.reshape(shard, wide)
-    first = gather_weight(jnp.concatenate([shard_tin, extra], 1))
+    first, take_first = gather_weight(jnp.concatenate([shard_tin, extra], 1))
     second = jnp.concatenate([shard_sin, st_out_proj.reshape(2 * local_w, shard).T], 1)
     third = jnp.concatenate(
         [mlp_up, mlp_down.T, tok_out_proj.reshape(2 * local_w, shard).T], 1
     )
-    second = gather_weight(hold(second, first, tok_rows))
-    extra = first[:, wide:]
-    w_tin = regroup(first, True)[:, :wide]
+    second, take_second = gather_weight(hold(second, first, tok_rows))
+    extra = take_first(wide, wide + EXTRA)
+    w_tin = take_first(0, wide)
     small = extra[:, :4].T.astype(F32)
-    table = extra.reshape(-1, shard, EXTRA)[:, :entries, 4 : 4 + heads * size]
-    table = table.reshape(-1, heads * size).astype(F32)
-    table = lax.dynamic_slice_in_dim(table, rank * heads, heads, 1)
+    by_seq = extra.reshape(-1, shard, EXTRA)
+    table = by_seq[:, :entries, 4 : 4 + heads].reshape(-1, heads).astype(F32)
+    seq = lax.axis_index(("dph", "mph"))
+    digits = lax.dynamic_index_in_dim(by_seq[:, 0, 4 + heads : 6 + heads], seq, 0, False)
+    digits = digits.astype(jnp.int32)
+    prefix_len = digits[0] * 64 + digits[1]
     start = regroup(hold(init_state[0], tok_rows), True)
     if size == 2:
         other = shift(start, 1)
@@ -720,12 +751,11 @@
         )
     else:
         state0 = lax.all_gather(start, GRP, axis=0, tiled=True)
-    prefix_len = regroup(prefix, True)
 
     gain1, gain2, gain3 = small[0:1], small[1:2], small[2:3]
     gate = jax.nn.sigmoid(small[3:4])
-    bias = window_bias(table * LOG2E)
-    base = jnp.stack([rank.astype(jnp.int32) * (rows // W), prefix_len[0]])
+    near = near_bias(table * LOG2E)
+    base = jnp.stack([rank.astype(jnp.int32) * (rows // W), prefix_len])
 
     def where_at(block):
         return jnp.concatenate([base, jnp.full((1,), block, jnp.int32)])
@@ -733,13 +763,11 @@
     tok_f = tok_rows.astype(F32)
     unit1, inv1 = normalize(tok_f)
     normed = gather_rot((unit1 * gain1).astype(BF16))
-    normed, bias, state0 = lax.optimization_barrier((normed, bias, state0))
+    normed, near, state0 = lax.optimization_barrier((normed, near, state0))
     proj = dot_nn(normed, w_tin).astype(BF16)
-    third, second, proj = after(third, second, proj)
-    third = gather_weight(third)
-    second = regroup(second, True)
-    w_sin, w_sout = second[:, :wide], second[:, wide:]
-    att, lse_tok = self_forward(where_at(0), proj, bias)
+    att, lse_tok = self_forward(where_at(0), proj, near)
+    third, take_third = gather_weight(hold(third, second, att))
+    w_sin, w_sout = take_second(0, wide), take_second(wide, wide + 2 * local_w)
     states, ups = [], []
     prev, mine, theirs, kept = state0, None, None, None
     for block in range(blocks):
@@ -749,10 +777,10 @@
         prev, norm_st, sproj, satt, att, lse_st, mine = outs
         kept = (norm_st, sproj, satt, lse_st)
         if block == 1:
-            third, mine = after(third, mine)
-        if block == blocks - 2:
             cot_rows, mine = after(cotangent[0], mine)
             cot_rows = regroup(cot_rows, True)
+        if block == blocks - 2:
+            cot_rows, mine = after(cot_rows, mine)
         if size == 2:
             theirs = shift(mine, 1)
         else:
@@ -760,8 +788,8 @@
             theirs = theirs.astype(BF16)
         states.append(prev)
         ups.append((mine, theirs))
-    third = regroup(third, True)
-    w_up, w_down, w_tout = third[:, :units], third[:, units : 2 * units], third[:, 2 * units :]
+    w_up, w_down = take_third(0, units), take_third(units, 2 * units)
+    w_tout = take_third(2 * units, 2 * units + 2 * local_w)
     final = gate * prev + (1.0 - gate) * (mine.astype(F32) + theirs.astype(F32))
     final_rows = lax.dynamic_slice_in_dim(final, rank * (S // size), S // size, 0)
 
@@ -771,7 +799,7 @@
     resid = tok_f + sum_rot(attn_term, rows)
     unit2, inv2 = normalize(resid)
     normed2 = gather_rot((unit2 * gain2).astype(BF16))
-    act, slope = up_project(normed2, third, units)
+    act, slope = up_project(normed2, w_up, units)
 
     def mlp_term(first, count):
         return dot_nt(lax.slice_in_dim(act, first, first + count, axis=0), w_down)
@@ -833,15 +861,17 @@
     gate_grad = functools.reduce(jnp.add, sums)[0]
     mixed = regroup(mixed, False)
     final_rows = regroup(final_rows, False)
-    grad_st = jnp.concatenate(
-        [dot_tn(norm_st, dsproj).astype(BF16), dot_tn(dupd, satt).astype(BF16)], 1
+    grad_sout = dot_tn(dupd, satt).astype(BF16)
+    aux, grad_sout, mixed, final_rows, grad_tout = after(
+        aux, grad_sout, mixed, final_rows, grad_tout
     )
-    aux, grad_st, mixed, final_rows, grad_tout = after(
-        aux, grad_st, mixed, final_rows, grad_tout
-    )
-    grad_st = regroup(grad_st, False)
-
-    grad_proj, cells = self_backward(where_at(0), proj, bias, grad_att, att, lse_tok, aux)
+    grad_sout = regroup(grad_sout, False)
+    grad_sin = dot_tn(norm_st, dsproj).astype(BF16)
+    aux, grad_sin, grad_sout = after(aux, grad_sin, grad_sout)
+    grad_sout = scatter_moved(grad_sout)
+    grad_sin = regroup(grad_sin, False)
+
+    grad_proj, cells = self_backward(where_at(0), proj, near, grad_att, att, lse_tok, aux)
 
     def tok_term(first, count):
         return dot_nt(lax.slice_in_dim(grad_proj, first, first + count, axis=0), w_tin)
@@ -851,11 +881,10 @@
     packed = jnp.concatenate([gate_grad[:, None], grad_table.reshape(model, heads)], 1)
     packed = jnp.pad(packed, ((0, 0), (0, EXTRA - 1 - heads))).astype(BF16)
     grad_tin = jnp.concatenate([dot_tn(normed, grad_proj).astype(BF16), packed], 1)
-    grad_tin, grad_st = after(grad_tin, grad_st)
-    grad_tin = regroup(grad_tin, False)
-    grad_st = scatter_moved(grad_st)
-    grad_sin, grad_sout = grad_st[:, :wide], grad_st[:, wide:]
-    grad_tin = scatter_moved(grad_tin)
+    grad_tin, grad_sin = after(grad_tin, grad_sin)
+    grad_sin = scatter_moved(grad_sin)
+    grad_proj, grad_tin = after(grad_proj, grad_tin)
+    grad_tin = scatter_moved(regroup(grad_tin, False))
     grad_tin, packed = grad_tin[:, :wide], grad_tin[:, wide:].astype(F32)
     grad_norm1 = sum_rot(tok_term, rows)
     input_grad = grad_resid + norm_back(grad_norm1, gain1, unit1, inv1)

time: 1340 us -> 1250 us (0.933)
  other arithmetic: 183 us -> 117 us
  starting transfers between devices: 161 us -> 95.8 us
  local copies, waits for them, and re-layouts: 39 us -> 60.8 us
  waiting for transfers between devices: 204 us -> 219 us
    all_gather x3, waiting for transfers between devices: 19.3 us -> 75.6 us  [gather_weight(): whole = lax.all_gather(shard, ('mph', 'mpl') + ORIG_DP, axis=0, tiled=True)]
    ppermute x24, starting transfers between devices: 121 us -> 68 us  [shift(): return lax.ppermute(arr, ('core', 'mpl'), pairs)]
    ppermute x1 -> x0, waiting for transfers between devices: 44.7 us -> none  [local(): other = lax.ppermute(rel_table, ('mph', 'mpl'), [(0, 1), (1, 0)])]
    select_n x2 -> x1, other arithmetic: 34.3 us -> 4.29 us  [near_bias(): jnp.where((which == entry)[None], table[entry][:, None, None, None], near)]
    select_n x12 -> x10, other arithmetic: 45.7 us -> 28.5 us  [regroup(): return jnp.where(stays, arr, moved)]
    dynamic_slice x0 -> x4, local copies, waits for them, and re-layouts: none -> 16.9 us  [take(): return lax.dynamic_slice(whole, (first, start), (model, stop - start))]
    eq x1, other arithmetic: 17.3 us -> 2.06 us  [near_bias(): which == entry]
    ppermute x15 -> x12, starting transfers between devices: 35.4 us -> 24.9 us  [regroup(): moved = lax.ppermute(arr, SWAP, pairs)]
  transfers between devices with their start and end apart: 49 -> 46, of which waited for: 15 -> 13; matrix products, arithmetic and copies ran while one was open for 32% -> 31% of each run, Pallas kernels for 33% -> 33%
where the time goes in v2:
time: 1250 us; the launch traced here: 1240 us
  Pallas kernels  441 us (35%)
  matrix products  291 us (23%)
  waiting for transfers between devices  219 us (18%)
  other arithmetic  117 us (9%)
  starting transfers between devices  95.8 us (8%)
  local copies, waits for them, and re-layouts  60.8 us (5%)
  between operations  19.9 us (2%)
    pallas_call x8, Pallas kernels, state_backward(): pl.pallas_call(functools.partial(state_backward_kernel, last), grid_spec=...  180 us
    pallas_call x8, Pallas kernels, state_forward(): pl.pallas_call(functools.partial(state_forward_kernel, first), grid_spec=...  132 us
    dot_general x6, matrix products, dot_tn(): lax.dot_general(left, right, (((0,), (0,)), ((), ())), preferred_element_...  120 us
    reduce_scatter x6, waiting for transfers between devices, scatter_moved(): return lax.psum_scatter(moved, ORIG_DP, scatter_dimension=0, tiled=True)  110 us
    dot_general x8, matrix products, dot_nt(): lax.dot_general(left, right, (((1,), (1,)), ((), ())), preferred_element_...  107 us
    all_gather x3, waiting for transfers between devices, gather_weight(): whole = lax.all_gather(shard, ('mph', 'mpl') + ORIG_DP, axis=0, tiled=True)  75.6 us
    ppermute x24, starting transfers between devices, shift(): return lax.ppermute(arr, ('core', 'mpl'), pairs)  68 us
    dot_general x3, matrix products, dot_nn(): lax.dot_general(left, right, (((1,), (0,)), ((), ())), preferred_element_...  64.4 us
  transfers between devices with their start and end apart: 46, of which 13 were waited for; matrix products, arithmetic and copies ran while one was open for 31% of the time, Pallas kernels for 33%

profile of v2, /device:TPU:0, one launch (start us, length us, event | category | flops | bytes accessed | tf_op | source)
XLA Modules:
  0.0 1243.3 jit_solution(7989170826917803493)
XLA Ops:
  24.0 75.6 %all-gather.4.cloned.1.call-done = bf16[2048,2176]{1,0:T(8,128)(2,1)} async-done(((bf16[64,2176]{1,0:T(8,128)(2,1)}), bf16[2048,2176]{1,0:T(8,128)(2,1)}) %all-gather.4.cloned.1.call-update) | async-done | bytes 8912912 | tf_op jit(solution)/shard_map/all_gather | solution.py:675
  144.6 23.8 %convolution_convert_fusion.q.kp.kc.vp.vc.refs_5_.refs_6_.refs_7_.refs_8_.refs_9_.refs_11_.refs_12_.refs_13_ = bf16[4096,2048]{1,0:T(8,128)(2,1)} fusion(bf16[4096,1024]{1,0:T(8,128)(2,1)} %pad_maximum_fusion, bf16[2048,2176]{1,0:T(8,128)(2,1)} %all-gather.4.cloned.1.call-done, s32[]{:T(128)S(6)} %select_n.430), kind=kOutput, calls=%fused_computation.1 | convolution fusion | flops 17188257792 | bytes 29360132 | tf_op jit(solution)/shard_map/dot_general | solution.py:74
  168.4 37.2 %self_forward.1 = (bf16[4096,1024]{1,0:T(8,128)(2,1)}, f32[8,4,512]{2,1,0:T(4,128)}) custom-call(s32[3]{0:T(128)} %get-tuple-element.458.where, bf16[4096,2048]{1,0:T(8,128)(2,1)} %convolution_convert_fusion.q.kp.kc.vp.vc.refs_5_.refs_6_.refs_7_.refs_8_.refs_9_.refs_11_.refs_12_.refs_13_, ...), custom_call_target="tpu_custom_call" | custom-call | flops 8589934592 | bytes 25165824 | tf_op jit(solution)/shard_map/self_forward/pallas_call | solution.py:230
  220.5 15.4 %state_forward.8 = (f32[512,1024]{1,0:T(8,128)}, bf16[4096,1024]{1,0:T(8,128)(2,1)}, bf16[4096,2048]{1,0:T(8,128)(2,1)}, bf16[4096,1024]{1,0:T(8,128)(2,1)}, bf1...) custom-call(s32[3]{0:T(128)} %get-tuple-element.458.where, ...), custom_call_target="tpu_custom_call", output_to_operand_aliasing={{4}: (9, {})} | custom-call | flops 4831838208 | bytes 16777216 | tf_op jit(solution)/shard_map/state_forward/pallas_call | solution.py:441
  239.8 17.0 %state_forward.9 = (f32[512,1024]{1,0:T(8,128)}, bf16[4096,1024]{1,0:T(8,128)(2,1)}, bf16[4096,2048]{1,0:T(8,128)(2,1)}, bf16[4096,1024]{1,0:T(8,128)(2,1)}, bf1...) custom-call(s32[3]{0:T(128)} %get-tuple-element.457.where, ...), custom_call_target="tpu_custom_call", output_to_operand_aliasing={{1}: (11, {}), {2}: (12, {}), {3}: (13, {}), {4}: (14, {}),... | custom-call | flops 4831838208 | bytes 16777216 | tf_op jit(solution)/shard_map/state_forward/pallas_call | solution.py:441
  260.6 16.9 %state_forward.10 = (f32[512,1024]{1,0:T(8,128)}, bf16[4096,1024]{1,0:T(8,128)(2,1)}, bf16[4096,2048]{1,0:T(8,128)(2,1)}, bf16[4096,1024]{1,0:T(8,128)(2,1)}, bf...) custom-call(s32[3]{0:T(128)} %get-tuple-element.456.where, ...), custom_call_target="tpu_custom_call", output_to_operand_aliasing={{1}: (11, {}), {2}: (12, {}), {3}: (13, {}), {4}: (14, {}),... | custom-call | flops 4831838208 | bytes 16777216 | tf_op jit(solution)/shard_map/state_forward/pallas_call | solution.py:441
  282.1 16.5 %state_forward.11 = (f32[512,1024]{1,0:T(8,128)}, bf16[4096,1024]{1,0:T(8,128)(2,1)}, bf16[4096,2048]{1,0:T(8,128)(2,1)}, bf16[4096,1024]{1,0:T(8,128)(2,1)}, bf...) custom-call(s32[3]{0:T(128)} %get-tuple-element.455.where, ...), custom_call_target="tpu_custom_call", output_to_operand_aliasing={{1}: (11, {}), {2}: (12, {}), {3}: (13, {}), {4}: (14, {}),... | custom-call | flops 4831838208 | bytes 16777216 | tf_op jit(solution)/shard_map/state_forward/pallas_call | solution.py:441
  302.4 16.5 %state_forward.12 = (f32[512,1024]{1,0:T(8,128)}, bf16[4096,1024]{1,0:T(8,128)(2,1)}, bf16[4096,2048]{1,0:T(8,128)(2,1)}, bf16[4096,1024]{1,0:T(8,128)(2,1)}, bf...) custom-call(s32[3]{0:T(128)} %get-tuple-element.454.where, ...), custom_call_target="tpu_custom_call", output_to_operand_aliasing={{1}: (11, {}), {2}: (12, {}), {3}: (13, {}), {4}: (14, {}),... | custom-call | flops 4831838208 | bytes 16777216 | tf_op jit(solution)/shard_map/state_forward/pallas_call | solution.py:441
  322.8 16.5 %state_forward.13 = (f32[512,1024]{1,0:T(8,128)}, bf16[4096,1024]{1,0:T(8,128)(2,1)}, bf16[4096,2048]{1,0:T(8,128)(2,1)}, bf16[4096,1024]{1,0:T(8,128)(2,1)}, bf...) custom-call(s32[3]{0:T(128)} %get-tuple-element.453.where, ...), custom_call_target="tpu_custom_call", output_to_operand_aliasing={{1}: (11, {}), {2}: (12, {}), {3}: (13, {}), {4}: (14, {}),... | custom-call | flops 4831838208 | bytes 16777216 | tf_op jit(solution)/shard_map/state_forward/pallas_call | solution.py:441
  345.0 16.6 %state_forward.14 = (f32[512,1024]{1,0:T(8,128)}, bf16[4096,1024]{1,0:T(8,128)(2,1)}, bf16[4096,2048]{1,0:T(8,128)(2,1)}, bf16[4096,1024]{1,0:T(8,128)(2,1)}, bf...) custom-call(s32[3]{0:T(128)} %get-tuple-element.452.where, ...), custom_call_target="tpu_custom_call", output_to_operand_aliasing={{1}: (11, {}), {2}: (12, {}), {3}: (13, {}), {4}: (14, {}),... | custom-call | flops 4831838208 | bytes 16777216 | tf_op jit(solution)/shard_map/state_forward/pallas_call | solution.py:441
  361.6 23.6 %collective-permute-start.11 = (bf16[512,1024]{1,0:T(8,128)(2,1)}, bf16[512,1024]{1,0:T(8,128)(2,1)S(1)}, u32[]{:S(2)}, u32[]{:S(2)}) collective-permute-start(bf16[512,1024]{1,0:T(8,128)(2,1)} %get-tuple-element.198.refs_1_.refs_4_), channel_id=1, source_target_pairs={{0,2},{2,0},{1,3},{3,1},{4,6},{6,4},{5,7},{7,5},{8,10},{10,8},{9,1... | collective-permute-start | bytes 3145736 | tf_op jit(solution)/shard_map/ppermute | solution.py:56
  388.7 16.8 %state_forward.15 = (f32[512,1024]{1,0:T(8,128)}, bf16[4096,1024]{1,0:T(8,128)(2,1)}, bf16[4096,2048]{1,0:T(8,128)(2,1)}, bf16[4096,1024]{1,0:T(8,128)(2,1)}, bf...) custom-call(s32[3]{0:T(128)} %get-tuple-element.377.where, ...), custom_call_target="tpu_custom_call", output_to_operand_aliasing={{1}: (11, {}), {2}: (12, {}), {3}: (13, {}), {4}: (14, {}),... | custom-call | flops 4831838208 | bytes 16777216 | tf_op jit(solution)/shard_map/state_forward/pallas_call | solution.py:441
  459.3 36.2 %up_project.1 = (bf16[4096,2048]{1,0:T(8,128)(2,1)}, bf16[4096,2048]{1,0:T(8,128)(2,1)}) custom-call(bf16[4096,1024]{1,0:T(8,128)(2,1)} %pad_maximum_fusion.1.rows, bf16[1024,2048]{1,0:T(8,128)(2,1)} %constant_dynamic-slice_fusion.weight), custom_call_target="tpu_custom_call" | custom-call | flops 17179869184 | bytes 46137344 | tf_op jit(solution)/shard_map/up_project/pallas_call | solution.py:644
  495.4 25.5 %multiply_convert_fusion = bf16[4096,2048]{1,0:T(8,128)(2,1)} fusion(bf16[4096,2048]{1,0:T(8,128)(2,1)} %get-tuple-element.207, bf16[4096,1024]{1,0:T(8,128)(2,1)} %copy-done.23, bf16[2048,5120]{1,0:T(8,128)(2,1)} %all-gather.8.cloned.1.call-done, s32[]{:T(128)S(6)} %select_n.430), kind=kOutput, calls=%fused_computation | convolution fusion | flops 17205035008 | bytes 46137348 | tf_op jit(solution)/shard_map/dot_general | solution.py:74
  532.7 22.8 %convolution_convert_fusion.5 = bf16[1024,2048]{1,0:T(8,128)(2,1)S(1)} fusion(bf16[4096,1024]{1,0:T(8,128)(2,1)} %copy-done.23, bf16[4096,2048]{1,0:T(8,128)(2,1)} %get-tuple-element.208), kind=kOutput, calls=%fused_computation.65 | convolution fusion | flops 17181966336 | bytes 29360128 | tf_op jit(solution)/shard_map/dot_general | solution.py:78
  558.1 18.1 %fusion.57 = (f32[2048]{0:T(1024)S(1)}, f32[2048]{0:T(1024)S(1)}, f32[2048,1024]{1,0:T(8,128)}) fusion(f32[1024]{0:T(1024)S(1)} %copy-done.42, bf16[2048,1024]{1,0:T(8,128)(2,1)} %collective-permute-done.15, f32[2048]{0:T(1024)S(1)} %add_rsqrt_fusion, f32[2048,1024]{1,0:T(8,128)} %copy-done.1, f32[2048]{0:T(1024)S(1)} %broadcast_multiply_fusion.4, ...), kind=kOutput, calls=%fused_computation.76 | convolution fusion | flops 8606707712 | bytes 33591296 | tf_op jit(solution)/shard_map/dot_general | solution.py:82
  591.0 22.8 %convolution_convert_fusion.4 = bf16[1024,2048]{1,0:T(8,128)(2,1)} fusion(bf16[4096,2048]{1,0:T(8,128)(2,1)} %multiply_convert_fusion, bf16[2048,1024]{1,0:T(8,128)(2,1)} %collective-permute-done.14, bf16[2048,1024]{1,0:T(8,128)(2,1)S(1)} %copy-done.7), kind=kOutput, calls=%fused_computation.64 | convolution fusion | flops 17198743552 | bytes 29360128 | tf_op jit(solution)/shard_map/dot_general | solution.py:78
  653.5 24.2 %state_backward.9 = (f32[512,1024]{1,0:T(8,128)}, bf16[4096,1024]{1,0:T(8,128)(2,1)}, bf16[4096,2048]{1,0:T(8,128)(2,1)}, bf16[4096,1536]{1,0:T(8,128)(2,1)}, f3...) custom-call(s32[3]{0:T(128)} %get-tuple-element.452.where, ...), custom_call_target="tpu_custom_call", output_to_operand_aliasing={{1}: (20, {}), {2}: (21, {}), {3}: (22, {})} | custom-call | flops 7247757312 | bytes 27262976 | tf_op jit(solution)/shard_map/state_backward/pallas_call | solution.py:590
  698.3 23.9 %state_backward.10 = (f32[512,1024]{1,0:T(8,128)}, bf16[4096,1024]{1,0:T(8,128)(2,1)}, bf16[4096,2048]{1,0:T(8,128)(2,1)}, bf16[4096,1536]{1,0:T(8,128)(2,1)}, f...) custom-call(s32[3]{0:T(128)} %get-tuple-element.453.where, ...), custom_call_target="tpu_custom_call", output_to_operand_aliasing={{1}: (20, {}), {2}: (21, {}), {3}: (22, {})} | custom-call | flops 7247757312 | bytes 27262976 | tf_op jit(solution)/shard_map/state_backward/pallas_call | solution.py:590
  739.5 23.7 %state_backward.11 = (f32[512,1024]{1,0:T(8,128)}, bf16[4096,1024]{1,0:T(8,128)(2,1)}, bf16[4096,2048]{1,0:T(8,128)(2,1)}, bf16[4096,1536]{1,0:T(8,128)(2,1)}, f...) custom-call(s32[3]{0:T(128)} %get-tuple-element.454.where, ...), custom_call_target="tpu_custom_call", output_to_operand_aliasing={{1}: (20, {}), {2}: (21, {}), {3}: (22, {})} | custom-call | flops 7247757312 | bytes 27262976 | tf_op jit(solution)/shard_map/state_backward/pallas_call | solution.py:590
  764.1 18.3 %add_convert_fusion = bf16[2048,1024]{1,0:T(8,128)(2,1)} fusion(f32[2048,1024]{1,0:T(8,128)} %copy-done.1, bf16[2048,1024]{1,0:T(8,128)(2,1)} %collective-permute-done.27, bf16[2048,5120]{1,0:T(8,128)(2,1)} %all-gather.8.cloned.1.call-done, s32[]{:T(128)S(6)} %select_n.430, bf16[4096,2048]{1,0:T(8,128)(2,1)} %get-tuple-element.208), kind=kOutput, calls=%fused_computation.31 | convolution fusion | flops 8598323200 | bytes 29360132 | tf_op jit(solution)/shard_map/dot_general | solution.py:82
  787.6 24.0 %state_backward.12 = (f32[512,1024]{1,0:T(8,128)}, bf16[4096,1024]{1,0:T(8,128)(2,1)}, bf16[4096,2048]{1,0:T(8,128)(2,1)}, bf16[4096,1536]{1,0:T(8,128)(2,1)}, f...) custom-call(s32[3]{0:T(128)} %get-tuple-element.455.where, ...), custom_call_target="tpu_custom_call", output_to_operand_aliasing={{1}: (20, {}), {2}: (21, {}), {3}: (22, {})} | custom-call | flops 7247757312 | bytes 27262976 | tf_op jit(solution)/shard_map/state_backward/pallas_call | solution.py:590
  817.9 23.6 %state_backward.13 = (f32[512,1024]{1,0:T(8,128)}, bf16[4096,1024]{1,0:T(8,128)(2,1)}, bf16[4096,2048]{1,0:T(8,128)(2,1)}, bf16[4096,1536]{1,0:T(8,128)(2,1)}, f...) custom-call(s32[3]{0:T(128)} %get-tuple-element.456.where, ...), custom_call_target="tpu_custom_call", output_to_operand_aliasing={{1}: (20, {}), {2}: (21, {}), {3}: (22, {})} | custom-call | flops 7247757312 | bytes 27262976 | tf_op jit(solution)/shard_map/state_backward/pallas_call | solution.py:590
  845.4 23.6 %state_backward.14 = (f32[512,1024]{1,0:T(8,128)}, bf16[4096,1024]{1,0:T(8,128)(2,1)}, bf16[4096,2048]{1,0:T(8,128)(2,1)}, bf16[4096,1536]{1,0:T(8,128)(2,1)}, f...) custom-call(s32[3]{0:T(128)} %get-tuple-element.457.where, ...), custom_call_target="tpu_custom_call", output_to_operand_aliasing={{1}: (20, {}), {2}: (21, {}), {3}: (22, {})} | custom-call | flops 7247757312 | bytes 27262976 | tf_op jit(solution)/shard_map/state_backward/pallas_call | solution.py:590
  878.0 23.9 %state_backward.15 = (f32[512,1024]{1,0:T(8,128)}, bf16[4096,1024]{1,0:T(8,128)(2,1)}, bf16[4096,2048]{1,0:T(8,128)(2,1)}, bf16[4096,1536]{1,0:T(8,128)(2,1)}, f...) custom-call(s32[3]{0:T(128)} %get-tuple-element.458.where, ...), custom_call_target="tpu_custom_call", output_to_operand_aliasing={{1}: (20, {}), {2}: (21, {}), {3}: (22, {})} | custom-call | flops 7247757312 | bytes 27262976 | tf_op jit(solution)/shard_map/state_backward/pallas_call | solution.py:590
  915.7 19.0 %reduce-scatter.11.cloned.1.call-done = bf16[64,1024]{1,0:T(8,128)(2,1)} async-done(((bf16[1024,1024]{1,0:T(8,128)(2,1)}), bf16[64,1024]{1,0:T(8,128)(2,1)}) %reduce-scatter.11.cloned.1.call-update) | async-done | bytes 131088 | tf_op jit(solution)/shard_map/reduce_scatter | solution.py:689
  936.4 23.9 %convolution_convert_fusion.3 = bf16[1024,2048]{1,0:T(8,128)(2,1)} fusion(bf16[4096,1024]{1,0:T(8,128)(2,1)} %get-tuple-element.261, bf16[4096,2048]{1,0:T(8,128)(2,1)} %get-tuple-element.262), kind=kOutput, calls=%fused_computation.63 | convolution fusion | flops 17181966336 | bytes 29360128 | tf_op jit(solution)/shard_map/dot_general | solution.py:78
  962.1 54.7 %self_backward.1 = (bf16[4096,2048]{1,0:T(8,128)(2,1)}, f32[4,5,128,128]{3,2,1,0:T(8,128)}) custom-call(s32[3]{0:T(128)} %get-tuple-element.458.where, bf16[4096,2048]{1,0:T(8,128)(2,1)} %convolution_convert_fusion.q.kp.kc.vp.vc.refs_5_.refs_6_.refs_7_.refs_8_.refs_9_.refs_11_.refs_12_.refs_13_, ...), custom_call_target="tpu_custom_call" | custom-call | flops 21474836480 | bytes 62914560 | tf_op jit(solution)/shard_map/self_backward/pallas_call | solution.py:329
  1025.9 22.8 %convolution_convert_fusion.2 = bf16[1024,2048]{1,0:T(8,128)(2,1)S(1)} fusion(bf16[4096,1024]{1,0:T(8,128)(2,1)} %pad_maximum_fusion, bf16[4096,2048]{1,0:T(8,128)(2,1)} %get-tuple-element.277), kind=kOutput, calls=%fused_computation.62 | convolution fusion | flops 17181966336 | bytes 29360128 | tf_op jit(solution)/shard_map/dot_general | solution.py:78
  1070.3 22.7 %collective-permute-start.33 = (bf16[2048,1024]{1,0:T(8,128)(2,1)}, bf16[2048,1024]{1,0:T(8,128)(2,1)}, u32[]{:S(2)}, u32[]{:S(2)}) collective-permute-start(bf16[2048,1024]{1,0:T(8,128)(2,1)} %fusion.36), channel_id=1, source_target_pairs={{0,2},{2,0},{1,3},{3,1},{4,6},{6,4},{5,7},{7,5},{8,10},{10,8},{9,1... | collective-permute-start | bytes 12582920 | tf_op jit(solution)/shard_map/ppermute | solution.py:56
  1128.6 22.8 %reduce-scatter.15.cloned.1.call-done = bf16[64,2048]{1,0:T(8,128)(2,1)} async-done(((bf16[1024,2048]{1,0:T(8,128)(2,1)}), bf16[64,2048]{1,0:T(8,128)(2,1)}) %reduce-scatter.15.cloned.1.call-update) | async-done | bytes 262160 | tf_op jit(solution)/shard_map/reduce_scatter | solution.py:689
  1160.9 68.1 %reduce-scatter.13.cloned.1.call-done = bf16[64,2176]{1,0:T(8,128)(2,1)} async-done(((bf16[1024,2176]{1,0:T(8,128)(2,1)}), bf16[64,2176]{1,0:T(8,128)(2,1)}) %reduce-scatter.13.cloned.1.call-update) | async-done | bytes 278544 | tf_op jit(solution)/shard_map/reduce_scatter | solution.py:689
  (328 shorter events, 386.5 us)
Async XLA Ops:
  7.2 92.3 %all-gather.4.cloned.1.call-start = ((), (), s32[]{:S(2)}) async-start(), calls=%async_computation.6 | async-start | bytes 9191424 | tf_op jit(solution)/shard_map/all_gather | solution.py:675
  12.6 194.9 %all-gather.6.cloned.1.call-start = ((), (), s32[]{:S(2)}) async-start(), calls=%async_computation.7 | async-start | bytes 12976128 | tf_op jit(solution)/shard_map/all_gather | solution.py:675
  102.2 303.3 %all-gather.8.cloned.1.call-start = ((), (), s32[]{:S(2)}) async-start(), calls=%async_computation.8 | async-start | bytes 21626880 | tf_op jit(solution)/shard_map/all_gather | solution.py:675
  112.0 24.7 %collective-permute-start.1 = (bf16[2048,1024]{1,0:T(8,128)(2,1)}, bf16[2048,1024]{1,0:T(8,128)(2,1)}, u32[]{:S(2)}, u32[]{:S(2)}) collective-permute-start(bf16[2048,1024]{1,0:T(8,128)(2,1)} %fusion.6), channel_id=1, source_target_pairs={{0,2},{2,0},{1,3},{3,1},{4,6},{6,4},{5,7},{7,5},{8,10},{10,8},{9,1... | collective-permute-start | bytes 12582920 | tf_op jit(solution)/shard_map/ppermute | solution.py:56
  210.4 601.2 %reduce-scatter.7.cloned.1.call-start = ((), (), s32[]{:S(2)}) async-start(), calls=%async_computation.9 | async-start | bytes 4456448 | tf_op jit(solution)/shard_map/reduce_scatter | solution.py:689
  277.7 61.7 %collective-permute-start.10 = (bf16[2048,1024]{1,0:T(8,128)(2,1)}, bf16[2048,1024]{1,0:T(8,128)(2,1)}, u32[]{:S(2)}, u32[]{:S(2)}) collective-permute-start(bf16[2048,1024]{1,0:T(8,128)(2,1)} %bitcast.153), channel_id=1, source_target_pairs={{1,2},{2,1},{5,6},{6,5},{9,10},{10,9},{13,14},{14,13},{17,18},{18,... | collective-permute-start | bytes 12582920 | tf_op jit(solution)/shard_map/ppermute | solution.py:42
  361.6 26.1 %collective-permute-start.11 = (bf16[512,1024]{1,0:T(8,128)(2,1)}, bf16[512,1024]{1,0:T(8,128)(2,1)S(1)}, u32[]{:S(2)}, u32[]{:S(2)}) collective-permute-start(bf16[512,1024]{1,0:T(8,128)(2,1)} %get-tuple-element.198.refs_1_.refs_4_), channel_id=1, source_target_pairs={{0,2},{2,0},{1,3},{3,1},{4,6},{6,4},{5,7},{7,5},{8,10},{10,8},{9,1... | collective-permute-start | bytes 3145736 | tf_op jit(solution)/shard_map/ppermute | solution.py:56
  413.3 12.7 %collective-permute-start.12 = (bf16[2048,1024]{1,0:T(8,128)(2,1)S(1)}, bf16[2048,1024]{1,0:T(8,128)(2,1)}, u32[]{:S(2)}, u32[]{:S(2)}) collective-permute-start(bf16[2048,1024]{1,0:T(8,128)(2,1)S(1)} %fusion.42), channel_id=1, source_target_pairs={{0,2},{2,0},{1,3},{3,1},{4,6},{6,4},{5,7},{7,5},{8,10},{10,8},{9,1... | collective-permute-start | bytes 12582920 | tf_op jit(solution)/shard_map/ppermute | solution.py:56
  413.9 27.2 %collective-permute-start.13 = (bf16[2048,1024]{1,0:T(8,128)(2,1)}, bf16[2048,1024]{1,0:T(8,128)(2,1)}, u32[]{:S(2)}, u32[]{:S(2)}) collective-permute-start(bf16[2048,1024]{1,0:T(8,128)(2,1)} %broadcast_select_fusion.5), channel_id=1, source_target_pairs={{0,2},{2,0},{1,3},{3,1},{4,6},{6,4},{5,7},{7,5},{8,10},{10,8},{9,1... | collective-permute-start | bytes 12582920 | tf_op jit(solution)/shard_map/ppermute | solution.py:56
  436.9 14.6 %collective-permute-start.14 = (bf16[2048,1024]{1,0:T(8,128)(2,1)S(1)}, bf16[2048,1024]{1,0:T(8,128)(2,1)}, u32[]{:S(2)}, u32[]{:S(2)}) collective-permute-start(bf16[2048,1024]{1,0:T(8,128)(2,1)S(1)} %multiply_convert_fusion.1), channel_id=1, source_target_pairs={{0,2},{2,0},{1,3},{3,1},{4,6},{6,4},{5,7},{7,5},{8,10},{10,8},{9,1... | collective-permute-start | bytes 12582920 | tf_op jit(solution)/shard_map/ppermute | solution.py:56
  532.2 25.9 %collective-permute-start.15 = (bf16[2048,1024]{1,0:T(8,128)(2,1)S(1)}, bf16[2048,1024]{1,0:T(8,128)(2,1)}, u32[]{:S(2)}, u32[]{:S(2)}) collective-permute-start(bf16[2048,1024]{1,0:T(8,128)(2,1)S(1)} %fusion.39), channel_id=1, source_target_pairs={{0,2},{2,0},{1,3},{3,1},{4,6},{6,4},{5,7},{7,5},{8,10},{10,8},{9,1... | collective-permute-start | bytes 12582920 | tf_op jit(solution)/shard_map/ppermute | solution.py:56
  555.5 60.9 %collective-permute-start.17 = (bf16[1024,2048]{1,0:T(8,128)(2,1)S(1)}, bf16[1024,2048]{1,0:T(8,128)(2,1)}, u32[]{:S(2)}, u32[]{:S(2)}) collective-permute-start(bf16[1024,2048]{1,0:T(8,128)(2,1)S(1)} %convolution_convert_fusion.5), channel_id=1, source_target_pairs={{2,1},{1,2},{6,5},{5,6},{10,9},{9,10},{14,13},{13,14},{18,17},{17,... | collective-permute-start | bytes 12582920 | tf_op jit(solution)/shard_map/ppermute | solution.py:42
  591.0 28.0 %collective-permute-start.16 = (bf16[2048,1024]{1,0:T(8,128)(2,1)}, bf16[2048,1024]{1,0:T(8,128)(2,1)}, u32[]{:S(2)}, u32[]{:S(2)}) collective-permute-start(bf16[2048,1024]{1,0:T(8,128)(2,1)} %get-tuple-element.373), channel_id=1, source_target_pairs={{0,2},{2,0},{1,3},{3,1},{4,6},{6,4},{5,7},{7,5},{8,10},{10,8},{9,1... | collective-permute-start | bytes 12582920 | tf_op jit(solution)/shard_map/ppermute | solution.py:56
  613.7 78.9 %collective-permute-start.20 = (bf16[1024,2048]{1,0:T(8,128)(2,1)}, bf16[1024,2048]{1,0:T(8,128)(2,1)}, u32[]{:S(2)}, u32[]{:S(2)}) collective-permute-start(bf16[1024,2048]{1,0:T(8,128)(2,1)} %convolution_convert_fusion.4), channel_id=1, source_target_pairs={{2,1},{1,2},{6,5},{5,6},{10,9},{9,10},{14,13},{13,14},{18,17},{17,... | collective-permute-start | bytes 12582920 | tf_op jit(solution)/shard_map/ppermute | solution.py:42
  650.1 218.9 %reduce-scatter.9.cloned.1.call-start = ((), (), s32[]{:S(2)}) async-start(), calls=%async_computation.10 | async-start | bytes 4456448 | tf_op jit(solution)/shard_map/reduce_scatter | solution.py:689
  677.8 19.6 %collective-permute-start.19 = (bf16[512,1024]{1,0:T(8,128)(2,1)}, bf16[512,1024]{1,0:T(8,128)(2,1)S(1)}, u32[]{:S(2)}, u32[]{:S(2)}) collective-permute-start(bf16[512,1024]{1,0:T(8,128)(2,1)} %get-tuple-element.219.refs_1_), channel_id=1, source_target_pairs={{0,2},{2,0},{1,3},{3,1},{4,6},{6,4},{5,7},{7,5},{8,10},{10,8},{9,1... | collective-permute-start | bytes 3145736 | tf_op jit(solution)/shard_map/ppermute | solution.py:56
  692.6 71.6 %collective-permute-start.27 = (bf16[2048,1024]{1,0:T(8,128)(2,1)}, bf16[2048,1024]{1,0:T(8,128)(2,1)}, u32[]{:S(2)}, u32[]{:S(2)}) collective-permute-start(bf16[2048,1024]{1,0:T(8,128)(2,1)} %fusion.33), channel_id=1, source_target_pairs={{0,2},{2,0},{1,3},{3,1},{4,6},{6,4},{5,7},{7,5},{8,10},{10,8},{9,1... | collective-permute-start | bytes 12582920 | tf_op jit(solution)/shard_map/ppermute | solution.py:56
  722.2 16.3 %collective-permute-start.21 = (bf16[512,1024]{1,0:T(8,128)(2,1)}, bf16[512,1024]{1,0:T(8,128)(2,1)S(1)}, u32[]{:S(2)}, u32[]{:S(2)}) collective-permute-start(bf16[512,1024]{1,0:T(8,128)(2,1)} %get-tuple-element.225.refs_1_), channel_id=1, source_target_pairs={{0,2},{2,0},{1,3},{3,1},{4,6},{6,4},{5,7},{7,5},{8,10},{10,8},{9,1... | collective-permute-start | bytes 3145736 | tf_op jit(solution)/shard_map/ppermute | solution.py:56
  736.5 48.6 %collective-permute-start.23 = (bf16[1024,1024]{1,0:T(8,128)(2,1)S(1)}, bf16[1024,1024]{1,0:T(8,128)(2,1)}, u32[]{:S(2)}, u32[]{:S(2)}) collective-permute-start(bf16[1024,1024]{1,0:T(8,128)(2,1)S(1)} %fusion.58), channel_id=1, source_target_pairs={{2,1},{1,2},{6,5},{5,6},{10,9},{9,10},{14,13},{13,14},{18,17},{17,... | collective-permute-start | bytes 6291464 | tf_op jit(solution)/shard_map/ppermute | solution.py:42
  738.5 196.3 %reduce-scatter.11.cloned.1.call-start = ((), (), s32[]{:S(2)}) async-start(), calls=%async_computation.11 | async-start | bytes 2228224 | tf_op jit(solution)/shard_map/reduce_scatter | solution.py:689
  763.2 23.4 %collective-permute-start.22 = (bf16[512,1024]{1,0:T(8,128)(2,1)}, bf16[512,1024]{1,0:T(8,128)(2,1)S(1)}, u32[]{:S(2)}, u32[]{:S(2)}) collective-permute-start(bf16[512,1024]{1,0:T(8,128)(2,1)} %get-tuple-element.230.refs_1_), channel_id=1, source_target_pairs={{0,2},{2,0},{1,3},{3,1},{4,6},{6,4},{5,7},{7,5},{8,10},{10,8},{9,1... | collective-permute-start | bytes 3145736 | tf_op jit(solution)/shard_map/ppermute | solution.py:56
  782.4 89.9 %collective-permute-start.28 = (bf16[2048,1024]{1,0:T(8,128)(2,1)}, bf16[2048,1024]{1,0:T(8,128)(2,1)}, u32[]{:S(2)}, u32[]{:S(2)}) collective-permute-start(bf16[2048,1024]{1,0:T(8,128)(2,1)} %add_convert_fusion), channel_id=1, source_target_pairs={{2,1},{1,2},{6,5},{5,6},{10,9},{9,10},{14,13},{13,14},{18,17},{17,... | collective-permute-start | bytes 12582920 | tf_op jit(solution)/shard_map/ppermute | solution.py:42
  813.7 28.0 %collective-permute-start.29 = (bf16[512,1024]{1,0:T(8,128)(2,1)}, bf16[512,1024]{1,0:T(8,128)(2,1)}, u32[]{:S(2)}, u32[]{:S(2)}) collective-permute-start(bf16[512,1024]{1,0:T(8,128)(2,1)} %get-tuple-element.255), channel_id=1, source_target_pairs={{0,2},{2,0},{1,3},{3,1},{4,6},{6,4},{5,7},{7,5},{8,10},{10,8},{9,1... | collective-permute-start | bytes 3145736 | tf_op jit(solution)/shard_map/ppermute | solution.py:56
  843.2 28.0 %collective-permute-start.30 = (f32[256,1024]{1,0:T(8,128)S(1)}, f32[256,1024]{1,0:T(8,128)S(1)}, u32[]{:S(2)}, u32[]{:S(2)}) collective-permute-start(f32[256,1024]{1,0:T(8,128)S(1)} %fusion.62), channel_id=1, source_target_pairs={{2,1},{1,2},{6,5},{5,6},{10,9},{9,10},{14,13},{13,14},{18,17},{17,... | collective-permute-start | bytes 3145736 | tf_op jit(solution)/shard_map/ppermute | solution.py:42
  872.3 254.6 %reduce-scatter.17.cloned.1.call-start = ((), (), s32[]{:S(2)}) async-start(), calls=%async_computation.14 | async-start | bytes 2228224 | tf_op jit(solution)/shard_map/reduce_scatter | solution.py:689
  934.7 25.5 %collective-permute-start.31 = (bf16[1024,1024]{1,0:T(8,128)(2,1)S(1)}, bf16[1024,1024]{1,0:T(8,128)(2,1)S(1)}, u32[]{:S(2)}, u32[]{:S(2)}) collective-permute-start(bf16[1024,1024]{1,0:T(8,128)(2,1)S(1)} %convolution_convert_fusion.6), channel_id=1, source_target_pairs={{2,1},{1,2},{6,5},{5,6},{10,9},{9,10},{14,13},{13,14},{18,17},{17,... | collective-permute-start | bytes 6291464 | tf_op jit(solution)/shard_map/ppermute | solution.py:42
  961.8 189.5 %reduce-scatter.15.cloned.1.call-start = ((), (), s32[]{:S(2)}) async-start(), calls=%async_computation.13 | async-start | bytes 4456448 | tf_op jit(solution)/shard_map/reduce_scatter | solution.py:689
  1018.1 33.1 %collective-permute-start.32 = (bf16[1024,2048]{1,0:T(8,128)(2,1)}, bf16[1024,2048]{1,0:T(8,128)(2,1)}, u32[]{:S(2)}, u32[]{:S(2)}) collective-permute-start(bf16[1024,2048]{1,0:T(8,128)(2,1)} %convolution_convert_fusion.3), channel_id=1, source_target_pairs={{2,1},{1,2},{6,5},{5,6},{10,9},{9,10},{14,13},{13,14},{18,17},{17,... | collective-permute-start | bytes 12582920 | tf_op jit(solution)/shard_map/ppermute | solution.py:42
  1055.2 173.8 %reduce-scatter.13.cloned.1.call-start = ((), (), s32[]{:S(2)}) async-start(), calls=%async_computation.12 | async-start | bytes 4734976 | tf_op jit(solution)/shard_map/reduce_scatter | solution.py:689
  1055.2 37.8 %collective-permute-start.35 = (bf16[1024,2176]{1,0:T(8,128)(2,1)}, bf16[1024,2176]{1,0:T(8,128)(2,1)S(1)}, u32[]{:S(2)}, u32[]{:S(2)}) collective-permute-start(bf16[1024,2176]{1,0:T(8,128)(2,1)} %fusion.26), channel_id=1, source_target_pairs={{2,1},{1,2},{6,5},{5,6},{10,9},{9,10},{14,13},{13,14},{18,17},{17,... | collective-permute-start | bytes 13369352 | tf_op jit(solution)/shard_map/ppermute | solution.py:42
  1070.3 30.0 %collective-permute-start.33 = (bf16[2048,1024]{1,0:T(8,128)(2,1)}, bf16[2048,1024]{1,0:T(8,128)(2,1)}, u32[]{:S(2)}, u32[]{:S(2)}) collective-permute-start(bf16[2048,1024]{1,0:T(8,128)(2,1)} %fusion.36), channel_id=1, source_target_pairs={{0,2},{2,0},{1,3},{3,1},{4,6},{6,4},{5,7},{7,5},{8,10},{10,8},{9,1... | collective-permute-start | bytes 12582920 | tf_op jit(solution)/shard_map/ppermute | solution.py:56
  1121.7 32.9 %collective-permute-start.34 = (bf16[2048,1024]{1,0:T(8,128)(2,1)}, bf16[2048,1024]{1,0:T(8,128)(2,1)}, u32[]{:S(2)}, u32[]{:S(2)}) collective-permute-start(bf16[2048,1024]{1,0:T(8,128)(2,1)} %fusion.11), channel_id=1, source_target_pairs={{2,1},{1,2},{6,5},{5,6},{10,9},{9,10},{14,13},{13,14},{18,17},{17,... | collective-permute-start | bytes 12582920 | tf_op jit(solution)/shard_map/ppermute | solution.py:42
  (69 other events, 1263.4 us)
Sparse Core Ops, SparseCore 0:
  12.7 86.7 all-gather.3
  103.0 96.5 all-gather.5
  210.5 151.1 all-gather.7
  650.2 72.8 reduce-scatter.6
  738.6 73.4 reduce-scatter.8
  872.5 62.2 reduce-scatter.10
  962.0 62.4 reduce-scatter.16
  1055.3 96.0 reduce-scatter.14
  1155.7 73.1 reduce-scatter.12

commit v3 on v2

--- a/solution.py
+++ b/solution.py
@@ -260,11 +260,10 @@
     )(where, proj, proj, proj, proj, proj, near)
 
 
-def self_backward_kernel(
-    where, q, kp, kc, vp, vc, near, dout, out, lse, aux, grad_proj, cells, carry, bias
-):
+def self_backward_kernel(top, where, q, kp, kc, vp, vc, near, dout, lse, aux, *refs):
+    grad_proj, cells, carry, bias = refs[-4:]
     step = pl.program_id(0)
-    block = pl.num_programs(0) - 1 - step
+    block = top - step
     edge = jnp.where(block == 0, NEG, 0.0)
     allowed = allowed_keys(block, where[1])
     heads = bias.shape[0]
@@ -274,31 +273,40 @@
     @pl.when(step == 0)
     def _():
         fill_bias(near, bias)
-        carry[...] = jnp.zeros_like(carry)
-        cells[...] = jnp.zeros_like(cells)
+        if len(refs) > 4:
+            cells[...] = refs[1][...]
+            carry[...] = refs[2][...]
+        else:
+            carry[...] = jnp.zeros_like(carry)
+            cells[...] = jnp.zeros_like(cells)
 
     for h in range(heads):
         cols = slice(h * HD, (h + 1) * HD)
         vcols = slice(local_w + h * HD, local_w + (h + 1) * HD)
-        delta = row_dot(dout[:, cols], out[:, cols])
         row_lse = lse[0, h : h + 1]
         before = dot_nt(kp[:, cols], q[:, cols]) * SCALE2 + (bias[h, :W] + edge)
-        dq0, dk0, dv0, ds0 = back_unit(
-            before, q[:, cols], kp[:, cols], vp[:, cols], dout[:, cols], row_lse, delta
-        )
         here = jnp.where(allowed, dot_nt(kc[:, cols], q[:, cols]) * SCALE2 + bias[h, W:], NEG)
-        dq1, dk1, dv1, ds1 = back_unit(
-            here, q[:, cols], kc[:, cols], vc[:, cols], dout[:, cols], row_lse, delta
-        )
+        probs0, probs1 = jnp.exp2(before - row_lse), jnp.exp2(here - row_lse)
+        prod0 = probs0 * dot_nt(vp[:, cols], dout[:, cols])
+        prod1 = probs1 * dot_nt(vc[:, cols], dout[:, cols])
+        delta = jnp.sum(prod0, 0, keepdims=True) + jnp.sum(prod1, 0, keepdims=True)
+        ds0 = (prod0 - probs0 * delta).astype(BF16)
+        ds1 = (prod1 - probs1 * delta).astype(BF16)
+        dv0 = dot_nn(probs0.astype(BF16), dout[:, cols])
+        dv1 = dot_nn(probs1.astype(BF16), dout[:, cols])
+        dk0 = dot_nn(ds0, q[:, cols]) * SCALE
+        dk1 = dot_nn(ds1, q[:, cols]) * SCALE
+        dq = dot_tn(kp[:, cols], ds0) + dot_tn(kc[:, cols], ds1)
         parts = {0: [], 1: [], 2: [], 3: [], 4: []}
         for kt in range(2 * tiles):
             for qt in range(tiles):
                 source, row = (ds0, kt) if kt < tiles else (ds1, kt - tiles)
                 cell = source[row * TILE : (row + 1) * TILE, qt * TILE : (qt + 1) * TILE]
+                cell = cell.astype(F32)
                 parts[tile_slot(kt, qt)].append(cell)
         for slot, group in parts.items():
             cells[h, slot] += functools.reduce(jnp.add, group)
-        grad_proj[:, cols] = (jnp.transpose(dq0 + dq1) * SCALE).astype(BF16)
+        grad_proj[:, cols] = (jnp.transpose(dq) * SCALE).astype(BF16)
         grad_proj[:, local_w + h * HD : local_w + (h + 1) * HD] = aux[:, cols]
         grad_proj[:, 2 * local_w + h * HD : 2 * local_w + (h + 1) * HD] = (
             dk1 + carry[:, cols] + aux[:, vcols].astype(F32)
@@ -312,25 +320,27 @@
         carry[:, vcols] = dv0
 
 
-def self_backward(where, proj, near, grad_att, att, lse, aux):
+def self_backward(top, steps, where, proj, near, grad_att, lse, aux, *kept):
     seq_len, width = proj.shape
     local_w = width // 4
     heads = near.shape[0]
     blocks = seq_len // W
 
     def order(i):
-        return blocks - 1 - i
+        return top - i
 
     at = self_specs(blocks, local_w, order)
 
     def whole(i, where):
         return ((order(i) + blocks - where[0]) % blocks, 0)
 
+    cell_spec = pl.BlockSpec((heads, 5, TILE, TILE), lambda i, where: (0, 0, 0, 0))
+    carry_spec = pl.BlockSpec((W, 2 * local_w), lambda i, where: (0, 0))
     return pl.pallas_call(
-        self_backward_kernel,
+        functools.partial(self_backward_kernel, top),
         grid_spec=pltpu.PrefetchScalarGridSpec(
             num_scalar_prefetch=1,
-            grid=(blocks,),
+            grid=(steps,),
             in_specs=[
                 at(0, 0),
                 at(2, -1),
@@ -339,31 +349,27 @@
                 at(3, 0),
                 pl.BlockSpec(near.shape, lambda i, where: (0, 0, 0, 0)),
                 at(0, 0),
-                at(0, 0),
                 pl.BlockSpec((1, heads, W), lambda i, where: (order(i), 0, 0)),
                 pl.BlockSpec((W, 3 * local_w), whole),
-            ],
-            out_specs=[
-                pl.BlockSpec((W, width), whole),
-                pl.BlockSpec((heads, 5, TILE, TILE), lambda i, where: (0, 0, 0, 0)),
-            ],
-            scratch_shapes=[
-                pltpu.VMEM((W, 2 * local_w), F32),
-                pltpu.VMEM((heads, 2 * W, W), F32),
-            ],
+            ]
+            + ([pl.BlockSpec(memory_space=pl.ANY), cell_spec, carry_spec] if kept else []),
+            out_specs=[pl.BlockSpec((W, width), whole), cell_spec, carry_spec],
+            scratch_shapes=[pltpu.VMEM((heads, 2 * W, W), F32)],
         ),
         out_shape=[
             jax.ShapeDtypeStruct((seq_len, width), BF16),
             jax.ShapeDtypeStruct((heads, 5, TILE, TILE), F32),
+            jax.ShapeDtypeStruct((W, 2 * local_w), F32),
         ],
+        input_output_aliases={10: 0} if kept else {},
         compiler_params=pltpu.CompilerParams(vmem_limit_bytes=VMEM_BYTES),
         cost_estimate=pl.CostEstimate(
-            flops=seq_len * 2 * W * local_w * 10,
-            bytes_accessed=seq_len * local_w * 30,
-            transcendentals=seq_len * 2 * W * heads,
+            flops=steps * W * 2 * W * local_w * 20,
+            bytes_accessed=steps * W * local_w * 30,
+            transcendentals=steps * W * 2 * W * heads,
         ),
-        name="self_backward",
-    )(where, proj, proj, proj, proj, proj, near, grad_att, att, lse, aux)
+        name="self_backward_second" if kept else "self_backward_first",
+    )(where, proj, proj, proj, proj, proj, near, grad_att, lse, aux, *kept)
 
 
 def state_forward_kernel(first, where, *refs):
@@ -624,6 +630,346 @@
     )(where, *operands)
 
 
+def partner_copy(send, recv, sems, slot):
+    other = {"core": 1 - lax.axis_index("core")}
+    return pltpu.make_async_remote_copy(
+        src_ref=send.at[slot],
+        dst_ref=recv.at[slot],
+        send_sem=sems.at[0, slot],
+        recv_sem=sems.at[1, slot],
+        device_id=other,
+        device_id_type=pl.DeviceIdType.MESH,
+    )
+
+
+def greet():
+    barrier = pltpu.get_barrier_semaphore()
+    other = {"core": 1 - lax.axis_index("core")}
+    pl.semaphore_signal(barrier, inc=1, device_id=other, device_id_type=pl.DeviceIdType.MESH)
+    pl.semaphore_wait(barrier, 1)
+
+
+def chain_forward_kernel(
+    state0,
+    gain,
+    gate,
+    w_in,
+    w_out,
+    cq,
+    kc,
+    vc,
+    held,
+    states,
+    norm,
+    sproj,
+    satt,
+    att,
+    lse,
+    final,
+    state,
+    send,
+    recv,
+    sems,
+):
+    step = pl.program_id(0)
+    steps = pl.num_programs(0)
+    slot = lax.rem(step, 2)
+    before = lax.rem(step + 1, 2)
+    local_w = cq.shape[1]
+    heads = local_w // HD
+
+    @pl.when(step == 0)
+    def _():
+        greet()
+        state[...] = state0[...]
+
+    @pl.when(step > 0)
+    def _():
+        partner_copy(send, recv, sems, before).wait()
+        update = send[before].astype(F32) + recv[before].astype(F32)
+        state[...] = gate[...] * state[...] + (1.0 - gate[...]) * update
+
+    fresh = state[...]
+    states[...] = fresh
+    unit, _ = normalize(fresh)
+    normed = (unit * gain[...]).astype(BF16)
+    norm[...] = normed
+    for p in range(4):
+        cols = slice(p * local_w, (p + 1) * local_w)
+        sproj[:, cols] = dot_nn(normed, w_in[:, cols]).astype(BF16)
+    for h in range(heads):
+        cols = [slice(p * local_w + h * HD, p * local_w + (h + 1) * HD) for p in range(4)]
+        sk, sv = sproj[:, cols[2]], sproj[:, cols[3]]
+        satt[:, cols[0]], lse[0, h : h + 1] = soft_unit(
+            (dot_nt(sk, sproj[:, cols[0]]) * SCALE2,), (sv,)
+        )
+        satt[:, cols[1]], lse[0, heads + h : heads + h + 1] = soft_unit(
+            (dot_nt(kc[:, cols[0]], sproj[:, cols[1]]) * SCALE2,), (vc[:, cols[0]],)
+        )
+    send[slot] = dot_nt(satt[...], w_out[...]).astype(BF16)
+    copy = partner_copy(send, recv, sems, slot)
+    copy.start()
+    for h in range(heads):
+        cols = [slice(p * local_w + h * HD, p * local_w + (h + 1) * HD) for p in range(4)]
+        sk, sv = sproj[:, cols[2]], sproj[:, cols[3]]
+        att[:, cols[0]], lse[0, 2 * heads + h : 2 * heads + h + 1] = soft_unit(
+            (dot_nt(sk, cq[:, cols[0]]) * SCALE2,), (sv,)
+        )
+
+    @pl.when(step == steps - 1)
+    def _():
+        copy.wait()
+        update = send[slot].astype(F32) + recv[slot].astype(F32)
+        final[...] = gate[...] * state[...] + (1.0 - gate[...]) * update
+
+
+def rotated(block, blocks, local_blocks, part):
+    return (lax.rem(block + blocks - lax.axis_index("core") * local_blocks, blocks), part)
+
+
+def chain_forward(state0, gain, gate, w_in, w_out, proj, att):
+    seq_len, width = proj.shape
+    local_w = width // 4
+    heads = local_w // HD
+    blocks = seq_len // W
+    local_blocks = blocks // 2
+    model = state0.shape[1]
+
+    def phys(part):
+        return pl.BlockSpec((W, local_w), lambda i: rotated(i, blocks, local_blocks, part))
+
+    def full(arr):
+        return pl.BlockSpec(arr.shape, lambda i: (0,) * arr.ndim, pipeline_mode=pl.Buffered(1))
+
+    def row_block(cols):
+        return pl.BlockSpec((S, cols), lambda i: (i, 0))
+
+    return pl.pallas_call(
+        chain_forward_kernel,
+        grid=(blocks,),
+        in_specs=[full(arr) for arr in (state0, gain, gate, w_in, w_out)]
+        + [phys(1), phys(2), phys(3), pl.BlockSpec(memory_space=pl.ANY)],
+        out_specs=[
+            row_block(model),
+            row_block(model),
+            row_block(width),
+            row_block(2 * local_w),
+            phys(1),
+            pl.BlockSpec((1, 3 * heads, S), lambda i: (i, 0, 0)),
+            pl.BlockSpec((S, model), lambda i: (0, 0)),
+        ],
+        out_shape=[
+            jax.ShapeDtypeStruct((blocks * S, model), F32),
+            jax.ShapeDtypeStruct((blocks * S, model), BF16),
+            jax.ShapeDtypeStruct((blocks * S, width), BF16),
+            jax.ShapeDtypeStruct((blocks * S, 2 * local_w), BF16),
+            jax.ShapeDtypeStruct(att.shape, BF16),
+            jax.ShapeDtypeStruct((blocks, 3 * heads, S), F32),
+            jax.ShapeDtypeStruct((S, model), F32),
+        ],
+        scratch_shapes=[
+            pltpu.VMEM((S, model), F32),
+            pltpu.VMEM((2, S, model), BF16),
+            pltpu.VMEM((2, S, model), BF16),
+            pltpu.SemaphoreType.DMA((2, 2)),
+        ],
+        input_output_aliases={8: 4},
+        compiler_params=pltpu.CompilerParams(
+            vmem_limit_bytes=VMEM_BYTES, collective_id=0, has_side_effects=True
+        ),
+        cost_estimate=pl.CostEstimate(
+            flops=blocks * (S * model * local_w * 12 + 3 * S * W * local_w * 8),
+            bytes_accessed=blocks * S * model * 12,
+            transcendentals=blocks * 3 * S * W * heads,
+        ),
+        name="chain_forward",
+    )(state0, gain, gate, w_in, w_out, proj, proj, proj, att)
+
+
+def chain_backward_kernel(top, steps, start, *refs):
+    refs = list(refs)
+    later = None if start else refs.pop(0)
+    state, state_next, gain, gate, w_in, w_out, cq, kc, vc, dcross, cross, sproj, satt, lse = refs[
+        :14
+    ]
+    refs = refs[14:] if start else refs[17:]
+    dupd, dsproj, aux, sums, leave, dstate, dkv, send, recv, sems = refs
+    step = pl.program_id(0)
+    slot = lax.rem(step, 2)
+    before = lax.rem(step + 1, 2)
+    local_w = cq.shape[1]
+    heads = local_w // HD
+    gate_f = gate[...]
+    finish = top - steps + 1 == 0
+
+    def absorb(where, at):
+        grad_norm = send[where].astype(F32) + recv[where].astype(F32)
+        unit, inv = normalize(at[...])
+        dstate[...] = gate_f * dstate[...] + norm_back(grad_norm, gain[...], unit, inv)
+
+    @pl.when(step == 0)
+    def _():
+        greet()
+        sums[...] = jnp.zeros_like(sums)
+        dstate[...] = jnp.zeros_like(dstate) if start else later[...]
+
+    for h in range(heads):
+        cols = [slice(p * local_w + h * HD, p * local_w + (h + 1) * HD) for p in range(4)]
+        head = cols[0]
+        sk, sv = sproj[:, cols[2]], sproj[:, cols[3]]
+        dq, dk, dv, _ = back_unit(
+            dot_nt(sk, cq[:, head]) * SCALE2,
+            cq[:, head],
+            sk,
+            sv,
+            dcross[:, head],
+            lse[0, 2 * heads + h : 2 * heads + h + 1],
+            row_dot(dcross[:, head], cross[:, head]),
+        )
+        aux[:, head] = (jnp.transpose(dq) * SCALE).astype(BF16)
+        dkv[:, cols[0]] = dk
+        dkv[:, cols[1]] = dv
+
+    @pl.when(step > 0)
+    def _():
+        partner_copy(send, recv, sems, before).wait()
+        absorb(before, state_next)
+
+    grad_state = dstate[...]
+    change = jnp.sum(grad_state * (state[...] - state_next[...]), 0, keepdims=True)
+    sums[...] += jnp.broadcast_to(change * gate_f, sums.shape)
+    dupd[...] = ((1.0 - gate_f) * grad_state).astype(BF16)
+    for h in range(heads):
+        cols = [slice(p * local_w + h * HD, p * local_w + (h + 1) * HD) for p in range(4)]
+        head = cols[0]
+        sk, sv = sproj[:, cols[2]], sproj[:, cols[3]]
+        dself = dot_nn(dupd[...], w_out[:, cols[0]]).astype(BF16)
+        dext = dot_nn(dupd[...], w_out[:, cols[1]]).astype(BF16)
+        sq = sproj[:, cols[0]]
+        dq, dk, dv, _ = back_unit(
+            dot_nt(sk, sq) * SCALE2,
+            sq,
+            sk,
+            sv,
+            dself,
+            lse[0, h : h + 1],
+            row_dot(dself, satt[:, cols[0]]),
+        )
+        dsproj[:, cols[0]] = (jnp.transpose(dq) * SCALE).astype(BF16)
+        dsproj[:, cols[2]] = (dk + dkv[:, cols[0]]).astype(BF16)
+        dsproj[:, cols[3]] = (dv + dkv[:, cols[1]]).astype(BF16)
+        sx = sproj[:, cols[1]]
+        dq, dk, dv, _ = back_unit(
+            dot_nt(kc[:, head], sx) * SCALE2,
+            sx,
+            kc[:, head],
+            vc[:, head],
+            dext,
+            lse[0, heads + h : heads + h + 1],
+            row_dot(dext, satt[:, cols[1]]),
+        )
+        dsproj[:, cols[1]] = (jnp.transpose(dq) * SCALE).astype(BF16)
+        aux[:, cols[1]] = dk.astype(BF16)
+        aux[:, cols[2]] = dv.astype(BF16)
+
+    def pass_on():
+        send[slot] = dot_nt(dsproj[...], w_in[...]).astype(BF16)
+        partner_copy(send, recv, sems, slot).start()
+
+    if finish:
+        pl.when(step < steps - 1)(pass_on)
+
+        @pl.when(step == steps - 1)
+        def _():
+            leave[...] = jnp.zeros_like(leave)
+    else:
+        pass_on()
+
+        @pl.when(step == steps - 1)
+        def _():
+            partner_copy(send, recv, sems, slot).wait()
+            absorb(slot, state)
+            leave[...] = dstate[...]
+
+
+def chain_backward(
+    top, steps, later, states, gain, gate, w_in, w_out, proj, grad_att, att, sproj, satt, lse, kept
+):
+    seq_len, width = proj.shape
+    local_w = width // 4
+    heads = local_w // HD
+    blocks = seq_len // W
+    local_blocks = blocks // 2
+    model = states.shape[1]
+    start = later is None
+
+    def phys(part):
+        return pl.BlockSpec((W, local_w), lambda i: rotated(top - i, blocks, local_blocks, part))
+
+    def full(arr):
+        return pl.BlockSpec(arr.shape, lambda i: (0,) * arr.ndim, pipeline_mode=pl.Buffered(1))
+
+    def row_block(cols):
+        return pl.BlockSpec((S, cols), lambda i: (top - i, 0))
+
+    operands = [] if start else [later]
+    in_specs = [full(arr) for arr in operands]
+    operands += [states, states, gain, gate, w_in, w_out]
+    in_specs += [
+        row_block(model),
+        pl.BlockSpec((S, model), lambda i: (jnp.minimum(top - i + 1, blocks - 1), 0)),
+    ]
+    in_specs += [full(arr) for arr in operands[-4:]]
+    operands += [proj, proj, proj, grad_att, att, sproj, satt, lse]
+    in_specs += [phys(1), phys(2), phys(3), phys(1), phys(1)]
+    in_specs += [row_block(width), row_block(2 * local_w)]
+    in_specs += [pl.BlockSpec((1, 3 * heads, S), lambda i: (top - i, 0, 0))]
+    aliases = {}
+    if not start:
+        for place, arr in enumerate(kept):
+            aliases[len(operands)] = place
+            operands.append(arr)
+            in_specs.append(pl.BlockSpec(memory_space=pl.ANY))
+    return pl.pallas_call(
+        functools.partial(chain_backward_kernel, top, steps, start),
+        grid=(steps,),
+        in_specs=in_specs,
+        out_specs=[
+            row_block(model),
+            row_block(width),
+            pl.BlockSpec((W, 3 * local_w), lambda i: rotated(top - i, blocks, local_blocks, 0)),
+            pl.BlockSpec((8, model), lambda i: (0, 0)),
+            pl.BlockSpec((S, model), lambda i: (0, 0)),
+        ],
+        out_shape=[
+            jax.ShapeDtypeStruct((blocks * S, model), BF16),
+            jax.ShapeDtypeStruct((blocks * S, width), BF16),
+            jax.ShapeDtypeStruct((seq_len, 3 * local_w), BF16),
+            jax.ShapeDtypeStruct((8, model), F32),
+            jax.ShapeDtypeStruct((S, model), F32),
+        ],
+        scratch_shapes=[
+            pltpu.VMEM((S, model), F32),
+            pltpu.VMEM((S, 2 * local_w), F32),
+            pltpu.VMEM((2, S, model), BF16),
+            pltpu.VMEM((2, S, model), BF16),
+            pltpu.SemaphoreType.DMA((2, 2)),
+        ],
+        input_output_aliases=aliases,
+        compiler_params=pltpu.CompilerParams(
+            vmem_limit_bytes=VMEM_BYTES,
+            collective_id=1 if start else 2,
+            has_side_effects=True,
+        ),
+        cost_estimate=pl.CostEstimate(
+            flops=steps * (S * model * local_w * 12 + 3 * S * W * local_w * 12),
+            bytes_accessed=steps * S * model * 24,
+            transcendentals=steps * 3 * S * W * heads,
+        ),
+        name="chain_backward_first" if start else "chain_backward_second",
+    )(*operands)
+
+
 def up_kernel(rows, weight, act, slope):
     step = min(512, weight.shape[1])
     root = 0.7978845608028654
@@ -728,9 +1074,7 @@
     shard_sin = st_in_proj.reshape(shard, wide)
     first, take_first = gather_weight(jnp.concatenate([shard_tin, extra], 1))
     second = jnp.concatenate([shard_sin, st_out_proj.reshape(2 * local_w, shard).T], 1)
-    third = jnp.concatenate(
-        [mlp_up, mlp_down.T, tok_out_proj.reshape(2 * local_w, shard).T], 1
-    )
+    third = jnp.concatenate([mlp_up, tok_out_proj.reshape(2 * local_w, shard).T], 1)
     second, take_second = gather_weight(hold(second, first, tok_rows))
     extra = take_first(wide, wide + EXTRA)
     w_tin = take_first(0, wide)
@@ -768,30 +1112,43 @@
     att, lse_tok = self_forward(where_at(0), proj, near)
     third, take_third = gather_weight(hold(third, second, att))
     w_sin, w_sout = take_second(0, wide), take_second(wide, wide + 2 * local_w)
-    states, ups = [], []
-    prev, mine, theirs, kept = state0, None, None, None
-    for block in range(blocks):
-        outs = state_forward(
-            where_at(block), block, prev, mine, theirs, gain3, gate, w_sin, w_sout, proj, kept, att
-        )
-        prev, norm_st, sproj, satt, att, lse_st, mine = outs
-        kept = (norm_st, sproj, satt, lse_st)
-        if block == 1:
-            cot_rows, mine = after(cotangent[0], mine)
-            cot_rows = regroup(cot_rows, True)
-        if block == blocks - 2:
-            cot_rows, mine = after(cot_rows, mine)
-        if size == 2:
-            theirs = shift(mine, 1)
-        else:
+    if size == 2:
+        w_sout, cot_rows = after(w_sout, cotangent[0])
+        cot_rows = regroup(cot_rows, True)
+        outs = chain_forward(state0, gain3, gate, w_sin, w_sout, proj, att)
+        states, norm_st, sproj, satt, att, lse_st, final = outs
+        att, cot_rows = after(att, cot_rows)
+    else:
+        cot_rows = regroup(cotangent[0], True)
+        states, ups = [], []
+        prev, mine, theirs, kept = state0, None, None, None
+        for block in range(blocks):
+            outs = state_forward(
+                where_at(block),
+                block,
+                prev,
+                mine,
+                theirs,
+                gain3,
+                gate,
+                w_sin,
+                w_sout,
+                proj,
+                kept,
+                att,
+            )
+            prev, norm_st, sproj, satt, att, lse_st, mine = outs
+            kept = (norm_st, sproj, satt, lse_st)
             theirs = lax.psum(mine.astype(F32), GRP) - mine.astype(F32)
             theirs = theirs.astype(BF16)
-        states.append(prev)
-        ups.append((mine, theirs))
-    w_up, w_down = take_third(0, units), take_third(units, 2 * units)
-    w_tout = take_third(2 * units, 2 * units + 2 * local_w)
-    final = gate * prev + (1.0 - gate) * (mine.astype(F32) + theirs.astype(F32))
+            states.append(prev)
+            ups.append((mine, theirs))
+        final = gate * prev + (1.0 - gate) * (mine.astype(F32) + theirs.astype(F32))
+    fourth, take_fourth = gather_weight(hold(mlp_down.T, third, att))
+    w_up, w_tout = take_third(0, units), take_third(units, units + 2 * local_w)
+    w_down = take_fourth(0, units)
     final_rows = lax.dynamic_slice_in_dim(final, rank * (S // size), S // size, 0)
+    final_rows = regroup(final_rows, False)
 
     def attn_term(first, count):
         return dot_nt(lax.slice_in_dim(att, first, first + count, axis=0), w_tout)
@@ -819,59 +1176,63 @@
     grad_attn = gather_rot(grad_resid.astype(BF16))
     grad_att = dot_nn(grad_attn, w_tout).astype(BF16)
     grad_tout = regroup(dot_tn(grad_attn, att).astype(BF16), False)
-    grad_att, grad_down = after(grad_att, grad_down)
+    grad_att, grad_down, final_rows = after(grad_att, grad_down, final_rows)
     grad_down = scatter_moved(grad_down)
 
-    chain, kept_b, sums = None, None, []
-    for block in reversed(range(blocks)):
-        outs = state_backward(
-            where_at(block),
-            block,
-            chain,
-            states[block],
-            gain3,
-            gate,
-            w_sin,
-            w_sout,
-            proj,
-            grad_att,
-            att,
-            sproj,
-            satt,
-            lse_st,
-            kept_b,
-        )
-        later, dupd, dsproj, aux, sum_b, part = outs
-        kept_b = (dupd, dsproj, aux)
-        sums.append(sum_b)
-        if block == blocks - 3:
-            part, grad_up = after(part, grad_up)
-            grad_up = scatter_moved(grad_up)
-        if block == blocks - 5:
-            part, grad_tout, grad_down = after(part, grad_tout, grad_down)
-            grad_tout = scatter_moved(grad_tout)
-        if block == 1:
-            part, grad_up = after(part, grad_up)
-        if block > 0:
-            if size == 2:
-                other = shift(part, 1)
-            else:
+    if size == 2:
+        half = blocks // 2
+        shared = (states, gain3, gate, w_sin, w_sout, proj, grad_att, att, sproj, satt, lse_st)
+        dupd, dsproj, aux, sums, later = chain_backward(blocks - 1, half, None, *shared, None)
+        later, grad_up, grad_down = after(later, grad_up, grad_down)
+        grad_up = scatter_moved(grad_up)
+        dupd, dsproj, aux, more, _ = chain_backward(
+            half - 1, half, later, *shared, (dupd, dsproj, aux)
+        )
+        gate_grad = sums[0] + more[0]
+        aux, grad_tout = after(aux, grad_tout)
+        grad_tout = scatter_moved(grad_tout)
+    else:
+        grad_up, grad_tout = scatter_moved(grad_up), scatter_moved(grad_tout)
+        chain, kept_b, sums = None, None, []
+        for block in reversed(range(blocks)):
+            outs = state_backward(
+                where_at(block),
+                block,
+                chain,
+                states[block],
+                gain3,
+                gate,
+                w_sin,
+                w_sout,
+                proj,
+                grad_att,
+                att,
+                sproj,
+                satt,
+                lse_st,
+                kept_b,
+            )
+            later, dupd, dsproj, aux, sum_b, part = outs
+            kept_b = (dupd, dsproj, aux)
+            sums.append(sum_b)
+            if block > 0:
                 other = (lax.psum(part.astype(F32), GRP) - part.astype(F32)).astype(BF16)
-            chain = (later, part, other, states[block]) + ups[block - 1]
-    gate_grad = functools.reduce(jnp.add, sums)[0]
-    mixed = regroup(mixed, False)
-    final_rows = regroup(final_rows, False)
+                chain = (later, part, other, states[block]) + ups[block - 1]
+        gate_grad = functools.reduce(jnp.add, sums)[0]
     grad_sout = dot_tn(dupd, satt).astype(BF16)
-    aux, grad_sout, mixed, final_rows, grad_tout = after(
-        aux, grad_sout, mixed, final_rows, grad_tout
-    )
     grad_sout = regroup(grad_sout, False)
     grad_sin = dot_tn(norm_st, dsproj).astype(BF16)
-    aux, grad_sin, grad_sout = after(aux, grad_sin, grad_sout)
+    aux, grad_sin, grad_sout, grad_up = after(aux, grad_sin, grad_sout, grad_up)
     grad_sout = scatter_moved(grad_sout)
     grad_sin = regroup(grad_sin, False)
 
-    grad_proj, cells = self_backward(where_at(0), proj, near, grad_att, att, lse_tok, aux)
+    half = blocks // 2
+    shared = (where_at(0), proj, near, grad_att, lse_tok, aux)
+    grad_proj, cells, carry = self_backward(blocks - 1, half, *shared)
+    carry, grad_tout, grad_sin = after(carry, grad_tout, grad_sin)
+    grad_sin = scatter_moved(grad_sin)
+    grad_proj, cells, _ = self_backward(half - 1, half, *shared, grad_proj, cells, carry)
+    grad_proj, grad_sout = after(grad_proj, grad_sout)
 
     def tok_term(first, count):
         return dot_nt(lax.slice_in_dim(grad_proj, first, first + count, axis=0), w_tin)
@@ -881,12 +1242,17 @@
     packed = jnp.concatenate([gate_grad[:, None], grad_table.reshape(model, heads)], 1)
     packed = jnp.pad(packed, ((0, 0), (0, EXTRA - 1 - heads))).astype(BF16)
     grad_tin = jnp.concatenate([dot_tn(normed, grad_proj).astype(BF16), packed], 1)
-    grad_tin, grad_sin = after(grad_tin, grad_sin)
-    grad_sin = scatter_moved(grad_sin)
     grad_proj, grad_tin = after(grad_proj, grad_tin)
-    grad_tin = scatter_moved(regroup(grad_tin, False))
+    grad_tin, mixed = after(regroup(grad_tin, False), mixed)
+    mixed = regroup(mixed, False)
+    if size == 2:
+        sent = shift(tok_term(rows, rows).astype(BF16), 1)
+        sent, grad_tin = after(sent, grad_tin)
+        grad_norm1 = tok_term(0, rows) + sent.astype(F32)
+    else:
+        grad_norm1 = sum_rot(tok_term, rows)
+    grad_tin = scatter_moved(grad_tin)
     grad_tin, packed = grad_tin[:, :wide], grad_tin[:, wide:].astype(F32)
-    grad_norm1 = sum_rot(tok_term, rows)
     input_grad = grad_resid + norm_back(grad_norm1, gain1, unit1, inv1)
 
     def gain_sum(shard_in, grad):

time: 1250 us -> 1150 us (0.920)
  waiting for transfers between devices: 219 us -> 143 us
  local copies, waits for them, and re-layouts: 60.8 us -> 43.4 us
  starting transfers between devices: 95.8 us -> 81.1 us
    reduce_scatter x6, waiting for transfers between devices: 110 us -> 55.6 us  [scatter_moved(): return lax.psum_scatter(moved, ORIG_DP, scatter_dimension=0, tiled=True)]
    ppermute x24 -> x9, starting transfers between devices: 68 us -> 16.4 us  [shift(): return lax.ppermute(arr, ('core', 'mpl'), pairs)]
    ppermute x1, starting transfers between devices: 1.54 us -> 36.3 us  [local(): vectors = vectors + lax.ppermute(vectors, ('mph', 'mpl'), [(0, 1), (1, 0)])]
    ppermute x24 -> x9, waiting for transfers between devices: 33 us -> 11.4 us  [shift(): return lax.ppermute(arr, ('core', 'mpl'), pairs)]
    unnamed x114 -> x84, local copies, waits for them, and re-layouts: 23.5 us -> 7.19 us
    pallas_call x17 -> x5, Pallas kernels: 367 us -> 360 us  [the longest x2 194 us: chain_backward(): pl.pallas_call(functools.partial(chain_backward_kernel, top, steps, start...]
    select_n x10 -> x9, other arithmetic: 28.5 us -> 28.2 us  [regroup(): return jnp.where(stays, arr, moved)]
    all_gather x3 -> x4, waiting for transfers between devices: 75.6 us -> 75.4 us  [gather_weight(): whole = lax.all_gather(shard, ('mph', 'mpl') + ORIG_DP, axis=0, tiled=True)]
  transfers between devices with their start and end apart: 46 -> 32, of which waited for: 13 -> 4; matrix products, arithmetic and copies ran while one was open for 31% -> 36% of each run, Pallas kernels for 33% -> 38%
where the time goes in v3:
time: 1150 us; the launch traced here: 1140 us
  Pallas kernels  434 us (38%)
  matrix products  294 us (26%)
  waiting for transfers between devices  143 us (12%)
  other arithmetic  122 us (11%)
  starting transfers between devices  81.1 us (7%)
  local copies, waits for them, and re-layouts  43.4 us (4%)
  between operations  21.4 us (2%)
    pallas_call x2, Pallas kernels, chain_backward(): pl.pallas_call(functools.partial(chain_backward_kernel, top, steps, start...  194 us
    dot_general x6, matrix products, dot_tn(): lax.dot_general(left, right, (((0,), (0,)), ((), ())), preferred_element_...  122 us
    dot_general x8, matrix products, dot_nt(): lax.dot_general(left, right, (((1,), (1,)), ((), ())), preferred_element_...  107 us
    pallas_call x1, Pallas kernels, chain_forward(): pl.pallas_call(chain_forward_kernel, grid=(blocks,), in_specs=[full(arr)...  93.8 us
    all_gather x4, waiting for transfers between devices, gather_weight(): whole = lax.all_gather(shard, ('mph', 'mpl') + ORIG_DP, axis=0, tiled=True)  75.4 us
    pallas_call x2, Pallas kernels, self_backward(): pl.pallas_call(functools.partial(self_backward_kernel, top), grid_spec=pl...  72.4 us
    dot_general x3, matrix products, dot_nn(): lax.dot_general(left, right, (((1,), (0,)), ((), ())), preferred_element_...  64.3 us
    reduce_scatter x6, waiting for transfers between devices, scatter_moved(): return lax.psum_scatter(moved, ORIG_DP, scatter_dimension=0, tiled=True)  55.6 us
  transfers between devices with their start and end apart: 32, of which 4 were waited for; matrix products, arithmetic and copies ran while one was open for 36% of the time, Pallas kernels for 38%

profile of v3, /device:TPU:0, one launch (start us, length us, event | category | flops | bytes accessed | tf_op | source)
XLA Modules:
  0.0 1138.1 jit_solution(3827548403951280133)
XLA Ops:
  24.2 75.3 %all-gather.5.cloned.1.call-done = bf16[2048,2176]{1,0:T(8,128)(2,1)} async-done(((bf16[64,2176]{1,0:T(8,128)(2,1)}), bf16[2048,2176]{1,0:T(8,128)(2,1)}) %all-gather.5.cloned.1.call-update) | async-done | bytes 8912912 | tf_op jit(solution)/shard_map/all_gather | solution.py:1021
  114.5 8.0 collective-permute-start.3
  136.2 7.9 pad_maximum_fusion
  144.0 23.8 %convolution_convert_fusion.q.kp.kc.vp.vc.cq.refs_6_.refs_7_.refs_8_.refs_9_ = bf16[4096,2048]{1,0:T(8,128)(2,1)} fusion(bf16[4096,1024]{1,0:T(8,128)(2,1)} %pad_maximum_fusion, bf16[2048,2176]{1,0:T(8,128)(2,1)} %all-gather.5.cloned.1.call-done, s32[]{:T(128)S(6)} %select_n.434), kind=kOutput, calls=%fused_computation.1 | convolution fusion | flops 17188257792 | bytes 29360132 | tf_op jit(solution)/shard_map/dot_general | solution.py:74
  167.9 37.2 %self_forward.1 = (bf16[4096,1024]{1,0:T(8,128)(2,1)}, f32[8,4,512]{2,1,0:T(4,128)}) custom-call(s32[3]{0:T(128)} %pad_add_fusion.where, bf16[4096,2048]{1,0:T(8,128)(2,1)} %convolution_convert_fusion.q.kp.kc.vp.vc.cq.refs_6_.refs_7_.refs_8_.refs_9_, bf16[4096,2048]{1,0:T(8,128)(2,1)} %convolution_convert_fusion.q.kp.kc.vp.vc.cq.refs_6_.refs_7_.refs_8_.refs_9_, ...), custom_call_target="tpu_custom_call" | custom-call | flops 8589934592 | bytes 25165824 | tf_op jit(solution)/shard_map/self_forward/pallas_call | solution.py:230
  222.0 93.8 %chain_forward.1 = (f32[4096,1024]{1,0:T(8,128)}, bf16[4096,1024]{1,0:T(8,128)(2,1)}, bf16[4096,2048]{1,0:T(8,128)(2,1)}, bf16[4096,1024]{1,0:T(8,128)(2,1)}, bf...) custom-call(f32[512,1024]{1,0:T(8,128)} %maximum_select_fusion.state0, ...), custom_call_target="tpu_custom_call", output_to_operand_aliasing={{4}: (8, {})} | custom-call | flops 51539607552 | bytes 50331648 | tf_op jit(solution)/shard_map/chain_forward/pallas_call | solution.py:747
  333.5 11.4 collective-permute-done.5
  344.8 9.8 fusion.96
  367.9 8.4 pad_maximum_fusion.1.rows
  376.3 36.3 %up_project.1 = (bf16[4096,2048]{1,0:T(8,128)(2,1)}, bf16[4096,2048]{1,0:T(8,128)(2,1)}) custom-call(bf16[4096,1024]{1,0:T(8,128)(2,1)} %pad_maximum_fusion.1.rows, bf16[1024,2048]{1,0:T(8,128)(2,1)} %constant_dynamic-slice_fusion.1.weight), custom_call_target="tpu_custom_call" | custom-call | flops 17179869184 | bytes 46137344 | tf_op jit(solution)/shard_map/up_project/pallas_call | solution.py:990
  412.6 25.3 %multiply_convert_fusion = bf16[4096,2048]{1,0:T(8,128)(2,1)} fusion(bf16[4096,2048]{1,0:T(8,128)(2,1)} %get-tuple-element.76, bf16[4096,1024]{1,0:T(8,128)(2,1)} %copy-done.16, bf16[2048,2048]{1,0:T(8,128)(2,1)} %all-gather.11.cloned.1.call-done, s32[]{:T(128)S(6)} %select_n.434), kind=kOutput, calls=%fused_computation | convolution fusion | flops 17205035008 | bytes 46137348 | tf_op jit(solution)/shard_map/dot_general | solution.py:74
  437.9 11.7 %fusion.37 = bf16[2048,1024]{1,0:T(8,128)(2,1)S(1)} fusion(bf16[1024,2048]{1,0:T(8,128)(2,1)S(1)} %copy-done.10, bf16[4096,2048]{1,0:T(8,128)(2,1)} %multiply_convert_fusion), kind=kOutput, calls=%fused_computation.68 | convolution fusion | flops 8592031744 | bytes 16777216 | tf_op jit(solution)/shard_map/dot_general | solution.py:82
  449.9 23.8 %convolution_convert_fusion.5 = bf16[1024,2048]{1,0:T(8,128)(2,1)} fusion(bf16[4096,1024]{1,0:T(8,128)(2,1)} %copy-done.16, bf16[4096,2048]{1,0:T(8,128)(2,1)} %get-tuple-element.77), kind=kOutput, calls=%fused_computation.65 | convolution fusion | flops 17181966336 | bytes 29360128 | tf_op jit(solution)/shard_map/dot_general | solution.py:78
  476.6 18.1 %fusion.55 = (f32[2048]{0:T(1024)S(1)}, f32[2048]{0:T(1024)S(1)}, f32[2048,1024]{1,0:T(8,128)}) fusion(f32[1024]{0:T(1024)S(1)} %copy-done.32, bf16[2048,1024]{1,0:T(8,128)(2,1)} %collective-permute-done.8, f32[2048]{0:T(1024)S(1)} %add_rsqrt_fusion, f32[2048,1024]{1,0:T(8,128)} %copy-done, f32[2048]{0:T(1024)S(1)} %broadcast_multiply_fusion.4, ...), kind=kOutput, calls=%fused_computation.76 | convolution fusion | flops 8606707712 | bytes 33591296 | tf_op jit(solution)/shard_map/dot_general | solution.py:82
  494.7 14.0 %fusion.94 = (bf16[2048,1024]{1,0:T(8,128)(2,1)}, f32[2048,1024]{1,0:T(8,128)}) fusion(f32[2048]{0:T(1024)S(1)} %get-tuple-element.292, f32[2048,1024]{1,0:T(8,128)} %copy-done, f32[2048]{0:T(1024)S(1)} %broadcast_multiply_fusion.4, f32[2048]{0:T(1024)S(1)} %get-tuple-element.293, f32[1024]{0:T(1024)S(1)} %copy-done.32, ...), kind=kLoop, calls=%fused_computation.245 | loop fusion | flops 25165824 | bytes 37785600 | tf_op jit(solution)/shard_map/convert_element_type | solution.py:1176
  509.7 22.7 %convolution_convert_fusion.4 = bf16[1024,2048]{1,0:T(8,128)(2,1)} fusion(bf16[4096,2048]{1,0:T(8,128)(2,1)} %multiply_convert_fusion, bf16[2048,1024]{1,0:T(8,128)(2,1)} %collective-permute-done.7, bf16[2048,1024]{1,0:T(8,128)(2,1)S(1)} %copy-done.8), kind=kOutput, calls=%fused_computation.64 | convolution fusion | flops 17198743552 | bytes 29360128 | tf_op jit(solution)/shard_map/dot_general | solution.py:78
  541.7 15.2 %convolution_convert_fusion.1.refs_9_.refs_10_.dout = bf16[4096,1024]{1,0:T(8,128)(2,1)} fusion(bf16[2048,1024]{1,0:T(8,128)(2,1)} %collective-permute-done.9, bf16[2048,1024]{1,0:T(8,128)(2,1)} %get-tuple-element.208, bf16[2048,3072]{1,0:T(8,128)(2,1)} %all-gather.9.cloned.1.call-done, s32[]{:T(128)S(6)} %select_n.434), kind=kOutput, calls=%fused_computation.42 | convolution fusion | flops 8610906112 | bytes 18874372 | tf_op jit(solution)/shard_map/dot_general | solution.py:74
  561.7 13.7 %fusion.57 = bf16[1024,1024]{1,0:T(8,128)(2,1)S(1)} fusion(bf16[4096,1024]{1,0:T(8,128)(2,1)} %get-tuple-element.75.refs_10_.refs_11_, bf16[2048,1024]{1,0:T(8,128)(2,1)} %collective-permute-done.9, bf16[2048,1024]{1,0:T(8,128)(2,1)} %get-tuple-element.208), kind=kOutput, calls=%fused_computation.81 | convolution fusion | flops 8607760384 | bytes 18874368 | tf_op jit(solution)/shard_map/dot_general | solution.py:78
  577.4 127.6 %chain_backward_first.1 = (bf16[4096,1024]{1,0:T(8,128)(2,1)}, bf16[4096,2048]{1,0:T(8,128)(2,1)}, bf16[4096,1536]{1,0:T(8,128)(2,1)}, f32[8,1024]{1,0:T(8,128)}, f32[512,1024]{1,0:T(8,128)}) custom-call(f32[4096,1024]{1,0:T(8,128)} %get-tuple-element.81.refs_0_.refs_1_.refs_2_, f32[4096,1024]{1,0:T(8,128)} %get-tuple-element.81.refs_0_.refs_1_.refs_2_, ...), custom_call_target="tpu_custom_call" | custom-call | flops 32212254720 | bytes 50331648 | tf_op jit(solution)/shard_map/chain_backward_first/pallas_call | solution.py:933
  707.1 66.3 %chain_backward_second.1 = (bf16[4096,1024]{1,0:T(8,128)(2,1)}, bf16[4096,2048]{1,0:T(8,128)(2,1)}, bf16[4096,1536]{1,0:T(8,128)(2,1)}, f32[8,1024]{1,0:T(8,128)}, f32[512,1024]{1,0:T(8,128)}) custom-call(f32[512,1024]{1,0:T(8,128)} %get-tuple-element.87.refs_0_, ...), custom_call_target="tpu_custom_call", output_to_operand_aliasing={{0}: (15, {}), {1}: (16, {}), {2}: (17, {})} | custom-call | flops 32212254720 | bytes 50331648 | tf_op jit(solution)/shard_map/chain_backward_second/pallas_call | solution.py:933
  773.4 13.8 %convolution_convert_fusion.6 = bf16[1024,1024]{1,0:T(8,128)(2,1)S(1)} fusion(bf16[4096,1024]{1,0:T(8,128)(2,1)} %get-tuple-element.95, bf16[4096,1024]{1,0:T(8,128)(2,1)} %get-tuple-element.83.refs_12_.refs_13_), kind=kOutput, calls=%fused_computation.82 | convolution fusion | flops 8590983168 | bytes 18874368 | tf_op jit(solution)/shard_map/dot_general | solution.py:78
  789.4 23.8 %convolution_convert_fusion.3 = bf16[1024,2048]{1,0:T(8,128)(2,1)} fusion(bf16[4096,1024]{1,0:T(8,128)(2,1)} %get-tuple-element.93, bf16[4096,2048]{1,0:T(8,128)(2,1)} %get-tuple-element.94), kind=kOutput, calls=%fused_computation.63 | convolution fusion | flops 17181966336 | bytes 29360128 | tf_op jit(solution)/shard_map/dot_general | solution.py:78
  817.9 13.9 %fusion.31 = bf16[2048,1024]{1,0:T(8,128)(2,1)} fusion(bf16[4096,2048]{1,0:T(8,128)(2,1)} %get-tuple-element.77, bf16[2048,2048]{1,0:T(8,128)(2,1)} %all-gather.11.cloned.1.call-done, s32[]{:T(128)S(6)} %select_n.434), kind=kOutput, calls=%fused_computation.66 | convolution fusion | flops 8592031744 | bytes 16777220 | tf_op jit(solution)/shard_map/dot_general | solution.py:82
  835.6 36.0 %self_backward_first.1 = (bf16[4096,2048]{1,0:T(8,128)(2,1)}, f32[4,5,128,128]{3,2,1,0:T(8,128)}, f32[512,1024]{1,0:T(8,128)}) custom-call(s32[3]{0:T(128)} %pad_add_fusion.where, bf16[4096,2048]{1,0:T(8,128)(2,1)} %convolution_convert_fusion.q.kp.kc.vp.vc.cq.refs_6_.refs_7_.refs_8_.refs_9_, ...), custom_call_target="tpu_custom_call" | custom-call | flops 21474836480 | bytes 31457280 | tf_op jit(solution)/shard_map/self_backward_first/pallas_call | solution.py:339
  876.2 36.5 %self_backward_second.1 = (bf16[4096,2048]{1,0:T(8,128)(2,1)}, f32[4,5,128,128]{3,2,1,0:T(8,128)}, f32[512,1024]{1,0:T(8,128)}) custom-call(s32[3]{0:T(128)} %pad_add_fusion.where, bf16[4096,2048]{1,0:T(8,128)(2,1)} %convolution_convert_fusion.q.kp.kc.vp.vc.cq.refs_6_.refs_7_.refs_8_.refs_9_, ...), custom_call_target="tpu_custom_call", output_to_operand_aliasing={{0}: (10, {})} | custom-call | flops 21474836480 | bytes 31457280 | tf_op jit(solution)/shard_map/self_backward_second/pallas_call | solution.py:339
  915.7 23.9 %convolution_convert_fusion.2 = bf16[1024,2048]{1,0:T(8,128)(2,1)} fusion(bf16[4096,1024]{1,0:T(8,128)(2,1)} %pad_maximum_fusion, bf16[4096,2048]{1,0:T(8,128)(2,1)} %get-tuple-element.113), kind=kOutput, calls=%fused_computation.62 | convolution fusion | flops 17181966336 | bytes 29360128 | tf_op jit(solution)/shard_map/dot_general | solution.py:78
  951.5 14.4 %fusion.34 = bf16[2048,1024]{1,0:T(8,128)(2,1)} fusion(bf16[4096,2048]{1,0:T(8,128)(2,1)} %get-tuple-element.113, bf16[2048,2176]{1,0:T(8,128)(2,1)} %all-gather.5.cloned.1.call-done, s32[]{:T(128)S(6)} %select_n.434), kind=kOutput, calls=%fused_computation.67 | convolution fusion | flops 8592031744 | bytes 16777220 | tf_op jit(solution)/shard_map/dot_general | solution.py:82
  966.5 16.3 %add_convert_fusion = bf16[2048,1024]{1,0:T(8,128)(2,1)} fusion(f32[2048,1024]{1,0:T(8,128)S(1)} %bitcast.157, bf16[2048,1024]{1,0:T(8,128)(2,1)} %collective-permute-done.17, bf16[2048,2048]{1,0:T(8,128)(2,1)} %all-gather.11.cloned.1.call-done, s32[]{:T(128)S(6)} %select_n.434, bf16[4096,2048]{1,0:T(8,128)(2,1)} %get-tuple-element.77), kind=kOutput, calls=%fused_computation.31 | convolution fusion | flops 8598323200 | bytes 29360132 | tf_op jit(solution)/shard_map/dot_general | solution.py:82
  987.8 15.7 %fusion.56 = (f32[2048]{0:T(1024)S(1)}, f32[2048]{0:T(1024)S(1)}, f32[2048,1024]{1,0:T(8,128)S(1)}) fusion(f32[1024]{0:T(1024)S(1)} %copy-done.31, bf16[2048,1024]{1,0:T(8,128)(2,1)} %collective-permute-done.19, f32[2048]{0:T(1024)S(1)} %copy-done.29, f32[2048]{0:T(1024)S(1)} %copy-done.27, bf16[2048,1024]{1,0:T(8,128)(2,1)} %copy-done.1, ...), kind=kOutput, calls=%fused_computation.77 | convolution fusion | flops 8608804864 | bytes 29396996 | tf_op jit(solution)/shard_map/dot_general | solution.py:82
  1006.3 9.1 fusion.11
  1036.0 52.6 %reduce-scatter.15.cloned.1.call-done = bf16[64,2176]{1,0:T(8,128)(2,1)} async-done(((bf16[1024,2176]{1,0:T(8,128)(2,1)}), bf16[64,2176]{1,0:T(8,128)(2,1)}) %reduce-scatter.15.cloned.1.call-update) | async-done | bytes 278544 | tf_op jit(solution)/shard_map/reduce_scatter | solution.py:1035
  1090.6 36.3 %collective-permute-start.21 = (f32[4,64]{1,0:T(4,128)S(1)}, f32[4,64]{1,0:T(4,128)S(1)}, u32[]{:S(2)}, u32[]{:S(2)}) collective-permute-start(f32[4,64]{1,0:T(4,128)S(1)} %pad_maximum_fusion.10), channel_id=1, source_target_pairs={{0,1},{1,0},{2,3},{3,2},{4,5},{5,4},{6,7},{7,6},{8,9},{9,8},{10,11... | collective-permute-start | bytes 3080 | tf_op jit(solution)/shard_map/ppermute | solution.py:1271
  (261 shorter events, 174.2 us)
Async XLA Ops:
  7.2 92.3 %all-gather.5.cloned.1.call-start = ((), (), s32[]{:S(2)}) async-start(), calls=%async_computation.6 | async-start | bytes 9191424 | tf_op jit(solution)/shard_map/all_gather | solution.py:1021
  12.6 194.4 %all-gather.7.cloned.1.call-start = ((), (), s32[]{:S(2)}) async-start(), calls=%async_computation.7 | async-start | bytes 12976128 | tf_op jit(solution)/shard_map/all_gather | solution.py:1021
  12.6 4.7 collective-permute-start
  102.2 220.2 %all-gather.9.cloned.1.call-start = ((), (), s32[]{:S(2)}) async-start(), calls=%async_computation.8 | async-start | bytes 12976128 | tf_op jit(solution)/shard_map/all_gather | solution.py:1021
  102.4 11.9 %collective-permute-start.2 = (f32[256,1024]{1,0:T(8,128)S(1)}, f32[256,1024]{1,0:T(8,128)S(1)}, u32[]{:S(2)}, u32[]{:S(2)}) collective-permute-start(f32[256,1024]{1,0:T(8,128)S(1)} %add_bitcast_fusion), channel_id=1, source_target_pairs={{1,2},{2,1},{5,6},{6,5},{9,10},{10,9},{13,14},{14,13},{17,18},{18,... | collective-permute-start | bytes 3145736 | tf_op jit(solution)/shard_map/ppermute | solution.py:42
  111.7 24.5 %collective-permute-start.1 = (bf16[2048,1024]{1,0:T(8,128)(2,1)}, bf16[2048,1024]{1,0:T(8,128)(2,1)}, u32[]{:S(2)}, u32[]{:S(2)}) collective-permute-start(bf16[2048,1024]{1,0:T(8,128)(2,1)} %fusion.6), channel_id=1, source_target_pairs={{0,2},{2,0},{1,3},{3,1},{4,6},{6,4},{5,7},{7,5},{8,10},{10,8},{9,1... | collective-permute-start | bytes 12582920 | tf_op jit(solution)/shard_map/ppermute | solution.py:56
  114.5 10.7 collective-permute-start.3
  209.7 202.9 %all-gather.11.cloned.1.call-start = ((), (), s32[]{:S(2)}) async-start(), calls=%async_computation.9 | async-start | bytes 8650752 | tf_op jit(solution)/shard_map/all_gather | solution.py:1021
  214.3 101.5 %collective-permute-start.4 = (bf16[2048,1024]{1,0:T(8,128)(2,1)}, bf16[2048,1024]{1,0:T(8,128)(2,1)}, u32[]{:S(2)}, u32[]{:S(2)}) collective-permute-start(bf16[2048,1024]{1,0:T(8,128)(2,1)} %bitcast.159), channel_id=1, source_target_pairs={{1,2},{2,1},{5,6},{6,5},{9,10},{10,9},{13,14},{14,13},{17,18},{18,... | collective-permute-start | bytes 12582920 | tf_op jit(solution)/shard_map/ppermute | solution.py:42
  325.1 379.9 %reduce-scatter.7.cloned.1.call-start = ((), (), s32[]{:S(2)}) async-start(), calls=%async_computation.10 | async-start | bytes 4456448 | tf_op jit(solution)/shard_map/reduce_scatter | solution.py:1035
  332.9 11.9 %collective-permute-start.5 = (bf16[2048,1024]{1,0:T(8,128)(2,1)S(1)}, bf16[2048,1024]{1,0:T(8,128)(2,1)}, u32[]{:S(2)}, u32[]{:S(2)}) collective-permute-start(bf16[2048,1024]{1,0:T(8,128)(2,1)S(1)} %fusion.40), channel_id=1, source_target_pairs={{0,2},{2,0},{1,3},{3,1},{4,6},{6,4},{5,7},{7,5},{8,10},{10,8},{9,1... | collective-permute-start | bytes 12582920 | tf_op jit(solution)/shard_map/ppermute | solution.py:56
  333.1 25.4 %collective-permute-start.6 = (bf16[2048,1024]{1,0:T(8,128)(2,1)S(1)}, bf16[2048,1024]{1,0:T(8,128)(2,1)S(1)}, u32[]{:S(2)}, u32[]{:S(2)}) collective-permute-start(bf16[2048,1024]{1,0:T(8,128)(2,1)S(1)} %copy-done.5), channel_id=1, source_target_pairs={{0,2},{2,0},{1,3},{3,1},{4,6},{6,4},{5,7},{7,5},{8,10},{10,8},{9,1... | collective-permute-start | bytes 12582920 | tf_op jit(solution)/shard_map/ppermute | solution.py:56
  358.0 10.0 collective-permute-start.7
  449.6 27.0 %collective-permute-start.8 = (bf16[2048,1024]{1,0:T(8,128)(2,1)S(1)}, bf16[2048,1024]{1,0:T(8,128)(2,1)}, u32[]{:S(2)}, u32[]{:S(2)}) collective-permute-start(bf16[2048,1024]{1,0:T(8,128)(2,1)S(1)} %fusion.37), channel_id=1, source_target_pairs={{0,2},{2,0},{1,3},{3,1},{4,6},{6,4},{5,7},{7,5},{8,10},{10,8},{9,1... | collective-permute-start | bytes 12582920 | tf_op jit(solution)/shard_map/ppermute | solution.py:56
  473.7 63.3 %collective-permute-start.10 = (bf16[1024,2048]{1,0:T(8,128)(2,1)}, bf16[1024,2048]{1,0:T(8,128)(2,1)}, u32[]{:S(2)}, u32[]{:S(2)}) collective-permute-start(bf16[1024,2048]{1,0:T(8,128)(2,1)} %convolution_convert_fusion.5), channel_id=1, source_target_pairs={{2,1},{1,2},{6,5},{5,6},{10,9},{9,10},{14,13},{13,14},{18,17},{17,... | collective-permute-start | bytes 12582920 | tf_op jit(solution)/shard_map/ppermute | solution.py:42
  508.7 33.1 %collective-permute-start.9 = (bf16[2048,1024]{1,0:T(8,128)(2,1)}, bf16[2048,1024]{1,0:T(8,128)(2,1)}, u32[]{:S(2)}, u32[]{:S(2)}) collective-permute-start(bf16[2048,1024]{1,0:T(8,128)(2,1)} %get-tuple-element.208), channel_id=1, source_target_pairs={{0,2},{2,0},{1,3},{3,1},{4,6},{6,4},{5,7},{7,5},{8,10},{10,8},{9,1... | collective-permute-start | bytes 12582920 | tf_op jit(solution)/shard_map/ppermute | solution.py:56
  532.5 24.5 %collective-permute-start.12 = (bf16[1024,2048]{1,0:T(8,128)(2,1)}, bf16[1024,2048]{1,0:T(8,128)(2,1)}, u32[]{:S(2)}, u32[]{:S(2)}) collective-permute-start(bf16[1024,2048]{1,0:T(8,128)(2,1)} %convolution_convert_fusion.4), channel_id=1, source_target_pairs={{2,1},{1,2},{6,5},{5,6},{10,9},{9,10},{14,13},{13,14},{18,17},{17,... | collective-permute-start | bytes 12582920 | tf_op jit(solution)/shard_map/ppermute | solution.py:42
  535.1 0.7 collective-permute-start.11
  556.9 257.9 %reduce-scatter.9.cloned.1.call-start = ((), (), s32[]{:S(2)}) async-start(), calls=%async_computation.11 | async-start | bytes 4456448 | tf_op jit(solution)/shard_map/reduce_scatter | solution.py:1035
  575.4 130.2 %collective-permute-start.13 = (bf16[1024,1024]{1,0:T(8,128)(2,1)S(1)}, bf16[1024,1024]{1,0:T(8,128)(2,1)}, u32[]{:S(2)}, u32[]{:S(2)}) collective-permute-start(bf16[1024,1024]{1,0:T(8,128)(2,1)S(1)} %fusion.57), channel_id=1, source_target_pairs={{2,1},{1,2},{6,5},{5,6},{10,9},{9,10},{14,13},{13,14},{18,17},{17,... | collective-permute-start | bytes 6291464 | tf_op jit(solution)/shard_map/ppermute | solution.py:42
  705.0 171.2 %reduce-scatter.11.cloned.1.call-start = ((), (), s32[]{:S(2)}) async-start(), calls=%async_computation.12 | async-start | bytes 2228224 | tf_op jit(solution)/shard_map/reduce_scatter | solution.py:1035
  787.2 26.0 %collective-permute-start.14 = (bf16[1024,1024]{1,0:T(8,128)(2,1)S(1)}, bf16[1024,1024]{1,0:T(8,128)(2,1)}, u32[]{:S(2)}, u32[]{:S(2)}) collective-permute-start(bf16[1024,1024]{1,0:T(8,128)(2,1)S(1)} %convolution_convert_fusion.6), channel_id=1, source_target_pairs={{2,1},{1,2},{6,5},{5,6},{10,9},{9,10},{14,13},{13,14},{18,17},{17,... | collective-permute-start | bytes 6291464 | tf_op jit(solution)/shard_map/ppermute | solution.py:42
  789.3 126.4 %reduce-scatter.13.cloned.1.call-start = ((), (), s32[]{:S(2)}) async-start(), calls=%async_computation.13 | async-start | bytes 2228224 | tf_op jit(solution)/shard_map/reduce_scatter | solution.py:1035
  814.8 56.7 %collective-permute-start.15 = (bf16[1024,2048]{1,0:T(8,128)(2,1)}, bf16[1024,2048]{1,0:T(8,128)(2,1)}, u32[]{:S(2)}, u32[]{:S(2)}) collective-permute-start(bf16[1024,2048]{1,0:T(8,128)(2,1)} %convolution_convert_fusion.3), channel_id=1, source_target_pairs={{2,1},{1,2},{6,5},{5,6},{10,9},{9,10},{14,13},{13,14},{18,17},{17,... | collective-permute-start | bytes 12582920 | tf_op jit(solution)/shard_map/ppermute | solution.py:42
  831.7 134.8 %collective-permute-start.17 = (bf16[2048,1024]{1,0:T(8,128)(2,1)}, bf16[2048,1024]{1,0:T(8,128)(2,1)}, u32[]{:S(2)}, u32[]{:S(2)}) collective-permute-start(bf16[2048,1024]{1,0:T(8,128)(2,1)} %fusion.31), channel_id=1, source_target_pairs={{0,2},{2,0},{1,3},{3,1},{4,6},{6,4},{5,7},{7,5},{8,10},{10,8},{9,1... | collective-permute-start | bytes 12582920 | tf_op jit(solution)/shard_map/ppermute | solution.py:56
  835.5 185.8 %reduce-scatter.17.cloned.1.call-start = ((), (), s32[]{:S(2)}) async-start(), calls=%async_computation.15 | async-start | bytes 4456448 | tf_op jit(solution)/shard_map/reduce_scatter | solution.py:1035
  939.6 149.0 %reduce-scatter.15.cloned.1.call-start = ((), (), s32[]{:S(2)}) async-start(), calls=%async_computation.14 | async-start | bytes 4734976 | tf_op jit(solution)/shard_map/reduce_scatter | solution.py:1035
  948.3 34.5 %collective-permute-start.16 = (bf16[1024,2176]{1,0:T(8,128)(2,1)}, bf16[1024,2176]{1,0:T(8,128)(2,1)}, u32[]{:S(2)}, u32[]{:S(2)}) collective-permute-start(bf16[1024,2176]{1,0:T(8,128)(2,1)} %fusion.26), channel_id=1, source_target_pairs={{2,1},{1,2},{6,5},{5,6},{10,9},{9,10},{14,13},{13,14},{18,17},{17,... | collective-permute-start | bytes 13369352 | tf_op jit(solution)/shard_map/ppermute | solution.py:42
  965.8 21.9 %collective-permute-start.19 = (bf16[2048,1024]{1,0:T(8,128)(2,1)}, bf16[2048,1024]{1,0:T(8,128)(2,1)}, u32[]{:S(2)}, u32[]{:S(2)}) collective-permute-start(bf16[2048,1024]{1,0:T(8,128)(2,1)} %fusion.34), channel_id=1, source_target_pairs={{0,2},{2,0},{1,3},{3,1},{4,6},{6,4},{5,7},{7,5},{8,10},{10,8},{9,1... | collective-permute-start | bytes 12582920 | tf_op jit(solution)/shard_map/ppermute | solution.py:56
  1003.6 21.2 %collective-permute-start.18 = (bf16[2048,1024]{1,0:T(8,128)(2,1)}, bf16[2048,1024]{1,0:T(8,128)(2,1)}, u32[]{:S(2)}, u32[]{:S(2)}) collective-permute-start(bf16[2048,1024]{1,0:T(8,128)(2,1)} %add_convert_fusion), channel_id=1, source_target_pairs={{2,1},{1,2},{6,5},{5,6},{10,9},{9,10},{14,13},{13,14},{18,17},{17,... | collective-permute-start | bytes 12582920 | tf_op jit(solution)/shard_map/ppermute | solution.py:42
  1015.4 14.2 %collective-permute-start.20 = (bf16[2048,1024]{1,0:T(8,128)(2,1)}, bf16[2048,1024]{1,0:T(8,128)(2,1)}, u32[]{:S(2)}, u32[]{:S(2)}) collective-permute-start(bf16[2048,1024]{1,0:T(8,128)(2,1)} %fusion.11), channel_id=1, source_target_pairs={{2,1},{1,2},{6,5},{5,6},{10,9},{9,10},{14,13},{13,14},{18,17},{17,... | collective-permute-start | bytes 12582920 | tf_op jit(solution)/shard_map/ppermute | solution.py:42
  1090.6 39.1 %collective-permute-start.21 = (f32[4,64]{1,0:T(4,128)S(1)}, f32[4,64]{1,0:T(4,128)S(1)}, u32[]{:S(2)}, u32[]{:S(2)}) collective-permute-start(f32[4,64]{1,0:T(4,128)S(1)} %pad_maximum_fusion.10), channel_id=1, source_target_pairs={{0,1},{1,0},{2,3},{3,2},{4,5},{5,4},{6,7},{7,6},{8,9},{9,8},{10,11... | collective-permute-start | bytes 3080 | tf_op jit(solution)/shard_map/ppermute | solution.py:1271
  (40 other events, 947.0 us)
Sparse Core Ops, SparseCore 0:
  12.7 86.7 all-gather.4
  103.0 96.6 all-gather.6
  209.8 103.1 all-gather.8
  325.2 77.8 all-gather.10
  557.1 129.6 reduce-scatter.6
  705.1 72.0 reduce-scatter.8
  789.4 61.4 reduce-scatter.10
  855.2 60.5 reduce-scatter.12
  939.8 71.3 reduce-scatter.16
  1015.4 73.1 reduce-scatter.14

commit v4 on v3

--- a/solution.py
+++ b/solution.py
@@ -1157,6 +1157,7 @@
     unit2, inv2 = normalize(resid)
     normed2 = gather_rot((unit2 * gain2).astype(BF16))
     act, slope = up_project(normed2, w_up, units)
+    act, final_rows = after(act, final_rows)
 
     def mlp_term(first, count):
         return dot_nt(lax.slice_in_dim(act, first, first + count, axis=0), w_down)
@@ -1176,7 +1177,7 @@
     grad_attn = gather_rot(grad_resid.astype(BF16))
     grad_att = dot_nn(grad_attn, w_tout).astype(BF16)
     grad_tout = regroup(dot_tn(grad_attn, att).astype(BF16), False)
-    grad_att, grad_down, final_rows = after(grad_att, grad_down, final_rows)
+    grad_att, grad_down = after(grad_att, grad_down)
     grad_down = scatter_moved(grad_down)
 
     if size == 2:

time: 1150 us -> 1130 us (0.983)
  Pallas kernels: 434 us -> 402 us
  starting transfers between devices: 81.1 us -> 98.4 us
    pallas_call x2, Pallas kernels: 194 us -> 162 us  [chain_backward(): pl.pallas_call(functools.partial(chain_backward_kernel, top, steps, start...]
    ppermute x9, starting transfers between devices: 16.4 us -> 33.8 us  [shift(): return lax.ppermute(arr, ('core', 'mpl'), pairs)]
  transfers between devices with their start and end apart: 32 -> 32, of which waited for: 4 -> 4; matrix products, arithmetic and copies ran while one was open for 36% -> 36% of each run, Pallas kernels for 38% -> 36%
where the time goes in v4:
time: 1130 us; the launch traced here: 1120 us
  Pallas kernels  402 us (36%)
  matrix products  295 us (26%)
  waiting for transfers between devices  142 us (13%)
  other arithmetic  122 us (11%)
  starting transfers between devices  98.4 us (9%)
  local copies, waits for them, and re-layouts  43.3 us (4%)
  between operations  21.4 us (2%)
    pallas_call x2, Pallas kernels, chain_backward(): pl.pallas_call(functools.partial(chain_backward_kernel, top, steps, start...  162 us
    dot_general x6, matrix products, dot_tn(): lax.dot_general(left, right, (((0,), (0,)), ((), ())), preferred_element_...  122 us
    dot_general x8, matrix products, dot_nt(): lax.dot_general(left, right, (((1,), (1,)), ((), ())), preferred_element_...  109 us
    pallas_call x1, Pallas kernels, chain_forward(): pl.pallas_call(chain_forward_kernel, grid=(blocks,), in_specs=[full(arr)...  93.9 us
    all_gather x4, waiting for transfers between devices, gather_weight(): whole = lax.all_gather(shard, ('mph', 'mpl') + ORIG_DP, axis=0, tiled=True)  75.7 us
    pallas_call x2, Pallas kernels, self_backward(): pl.pallas_call(functools.partial(self_backward_kernel, top), grid_spec=pl...  72.2 us
    dot_general x3, matrix products, dot_nn(): lax.dot_general(left, right, (((1,), (0,)), ((), ())), preferred_element_...  64.2 us
    reduce_scatter x6, waiting for transfers between devices, scatter_moved(): return lax.psum_scatter(moved, ORIG_DP, scatter_dimension=0, tiled=True)  55 us
  transfers between devices with their start and end apart: 32, of which 4 were waited for; matrix products, arithmetic and copies ran while one was open for 36% of the time, Pallas kernels for 36%

profile of v4, /device:TPU:0, one launch (start us, length us, event | category | flops | bytes accessed | tf_op | source)
XLA Modules:
  0.0 1123.8 jit_solution(4850735052210284949)
XLA Ops:
  23.9 75.6 %all-gather.5.cloned.1.call-done = bf16[2048,2176]{1,0:T(8,128)(2,1)} async-done(((bf16[64,2176]{1,0:T(8,128)(2,1)}), bf16[2048,2176]{1,0:T(8,128)(2,1)}) %all-gather.5.cloned.1.call-update) | async-done | bytes 8912912 | tf_op jit(solution)/shard_map/all_gather | solution.py:1021
  114.5 8.0 collective-permute-start.3
  144.0 23.7 %convolution_convert_fusion.q.kp.kc.vp.vc.cq.refs_6_.refs_7_.refs_8_.refs_9_ = bf16[4096,2048]{1,0:T(8,128)(2,1)} fusion(bf16[4096,1024]{1,0:T(8,128)(2,1)} %pad_maximum_fusion, bf16[2048,2176]{1,0:T(8,128)(2,1)} %all-gather.5.cloned.1.call-done, s32[]{:T(128)S(6)} %select_n.434), kind=kOutput, calls=%fused_computation.1 | convolution fusion | flops 17188257792 | bytes 29360132 | tf_op jit(solution)/shard_map/dot_general | solution.py:74
  167.8 37.2 %self_forward.1 = (bf16[4096,1024]{1,0:T(8,128)(2,1)}, f32[8,4,512]{2,1,0:T(4,128)}) custom-call(s32[3]{0:T(128)} %pad_add_fusion.where, bf16[4096,2048]{1,0:T(8,128)(2,1)} %convolution_convert_fusion.q.kp.kc.vp.vc.cq.refs_6_.refs_7_.refs_8_.refs_9_, bf16[4096,2048]{1,0:T(8,128)(2,1)} %convolution_convert_fusion.q.kp.kc.vp.vc.cq.refs_6_.refs_7_.refs_8_.refs_9_, ...), custom_call_target="tpu_custom_call" | custom-call | flops 8589934592 | bytes 25165824 | tf_op jit(solution)/shard_map/self_forward/pallas_call | solution.py:230
  221.9 93.9 %chain_forward.1 = (f32[4096,1024]{1,0:T(8,128)}, bf16[4096,1024]{1,0:T(8,128)(2,1)}, bf16[4096,2048]{1,0:T(8,128)(2,1)}, bf16[4096,1024]{1,0:T(8,128)(2,1)}, bf...) custom-call(f32[512,1024]{1,0:T(8,128)} %maximum_select_fusion.state0, ...), custom_call_target="tpu_custom_call", output_to_operand_aliasing={{4}: (8, {})} | custom-call | flops 51539607552 | bytes 50331648 | tf_op jit(solution)/shard_map/chain_forward/pallas_call | solution.py:747
  333.3 10.8 collective-permute-done.5
  344.2 9.8 fusion.96
  367.2 8.4 pad_maximum_fusion.1.rows
  375.6 36.1 %up_project.1 = (bf16[4096,2048]{1,0:T(8,128)(2,1)}, bf16[4096,2048]{1,0:T(8,128)(2,1)}) custom-call(bf16[4096,1024]{1,0:T(8,128)(2,1)} %pad_maximum_fusion.1.rows, bf16[1024,2048]{1,0:T(8,128)(2,1)} %constant_dynamic-slice_fusion.1.weight), custom_call_target="tpu_custom_call" | custom-call | flops 17179869184 | bytes 46137344 | tf_op jit(solution)/shard_map/up_project/pallas_call | solution.py:990
  411.7 25.3 %multiply_convert_fusion = bf16[4096,2048]{1,0:T(8,128)(2,1)} fusion(bf16[4096,2048]{1,0:T(8,128)(2,1)} %get-tuple-element.77, bf16[4096,1024]{1,0:T(8,128)(2,1)} %copy-done.16, bf16[2048,2048]{1,0:T(8,128)(2,1)} %all-gather.11.cloned.1.call-done, s32[]{:T(128)S(6)} %select_n.434), kind=kOutput, calls=%fused_computation | convolution fusion | flops 17205035008 | bytes 46137348 | tf_op jit(solution)/shard_map/dot_general | solution.py:74
  437.0 13.3 %fusion.37 = bf16[2048,1024]{1,0:T(8,128)(2,1)} fusion(bf16[1024,2048]{1,0:T(8,128)(2,1)S(1)} %copy-done.10, bf16[4096,2048]{1,0:T(8,128)(2,1)} %multiply_convert_fusion), kind=kOutput, calls=%fused_computation.68 | convolution fusion | flops 8592031744 | bytes 16777216 | tf_op jit(solution)/shard_map/dot_general | solution.py:82
  452.5 23.8 %convolution_convert_fusion.5 = bf16[1024,2048]{1,0:T(8,128)(2,1)} fusion(bf16[4096,1024]{1,0:T(8,128)(2,1)} %copy-done.16, bf16[4096,2048]{1,0:T(8,128)(2,1)} %get-tuple-element.80), kind=kOutput, calls=%fused_computation.65 | convolution fusion | flops 17181966336 | bytes 29360128 | tf_op jit(solution)/shard_map/dot_general | solution.py:78
  479.1 17.9 %fusion.55 = (f32[2048]{0:T(1024)S(1)}, f32[2048]{0:T(1024)S(1)}, f32[2048,1024]{1,0:T(8,128)}) fusion(f32[1024]{0:T(1024)S(1)} %copy-done.32, bf16[2048,1024]{1,0:T(8,128)(2,1)} %collective-permute-done.8, f32[2048]{0:T(1024)S(1)} %add_rsqrt_fusion, f32[2048,1024]{1,0:T(8,128)} %copy-done, f32[2048]{0:T(1024)S(1)} %broadcast_multiply_fusion.4, ...), kind=kOutput, calls=%fused_computation.76 | convolution fusion | flops 8606707712 | bytes 33591296 | tf_op jit(solution)/shard_map/dot_general | solution.py:82
  497.1 13.9 %fusion.94 = (bf16[2048,1024]{1,0:T(8,128)(2,1)}, f32[2048,1024]{1,0:T(8,128)}) fusion(f32[2048]{0:T(1024)S(1)} %get-tuple-element.294, f32[2048,1024]{1,0:T(8,128)} %copy-done, f32[2048]{0:T(1024)S(1)} %broadcast_multiply_fusion.4, f32[2048]{0:T(1024)S(1)} %get-tuple-element.295, f32[1024]{0:T(1024)S(1)} %copy-done.32, ...), kind=kLoop, calls=%fused_computation.245 | loop fusion | flops 25165824 | bytes 37785600 | tf_op jit(solution)/shard_map/convert_element_type | solution.py:1177
  511.0 17.6 %collective-permute-start.9 = (bf16[2048,1024]{1,0:T(8,128)(2,1)}, bf16[2048,1024]{1,0:T(8,128)(2,1)}, u32[]{:S(2)}, u32[]{:S(2)}) collective-permute-start(bf16[2048,1024]{1,0:T(8,128)(2,1)} %get-tuple-element.210), channel_id=1, source_target_pairs={{0,2},{2,0},{1,3},{3,1},{4,6},{6,4},{5,7},{7,5},{8,10},{10,8},{9,1... | collective-permute-start | bytes 12582920 | tf_op jit(solution)/shard_map/ppermute | solution.py:56
  528.6 22.7 %convolution_convert_fusion.4 = bf16[1024,2048]{1,0:T(8,128)(2,1)} fusion(bf16[4096,2048]{1,0:T(8,128)(2,1)} %multiply_convert_fusion, bf16[2048,1024]{1,0:T(8,128)(2,1)} %collective-permute-done.7, bf16[2048,1024]{1,0:T(8,128)(2,1)S(1)} %copy-done.8), kind=kOutput, calls=%fused_computation.64 | convolution fusion | flops 17198743552 | bytes 29360128 | tf_op jit(solution)/shard_map/dot_general | solution.py:78
  558.6 15.2 %convolution_convert_fusion.1.refs_9_.refs_10_.dout = bf16[4096,1024]{1,0:T(8,128)(2,1)} fusion(bf16[2048,1024]{1,0:T(8,128)(2,1)} %collective-permute-done.9, bf16[2048,1024]{1,0:T(8,128)(2,1)} %get-tuple-element.210, bf16[2048,3072]{1,0:T(8,128)(2,1)} %all-gather.9.cloned.1.call-done, s32[]{:T(128)S(6)} %select_n.434), kind=kOutput, calls=%fused_computation.42 | convolution fusion | flops 8610906112 | bytes 18874372 | tf_op jit(solution)/shard_map/dot_general | solution.py:74
  578.5 14.3 %fusion.57 = bf16[1024,1024]{1,0:T(8,128)(2,1)S(1)} fusion(bf16[4096,1024]{1,0:T(8,128)(2,1)} %get-tuple-element.76.refs_10_.refs_11_, bf16[2048,1024]{1,0:T(8,128)(2,1)} %collective-permute-done.9, bf16[2048,1024]{1,0:T(8,128)(2,1)} %get-tuple-element.210), kind=kOutput, calls=%fused_computation.81 | convolution fusion | flops 8607760384 | bytes 18874368 | tf_op jit(solution)/shard_map/dot_general | solution.py:78
  594.8 95.8 %chain_backward_first.1 = (bf16[4096,1024]{1,0:T(8,128)(2,1)}, bf16[4096,2048]{1,0:T(8,128)(2,1)}, bf16[4096,1536]{1,0:T(8,128)(2,1)}, f32[8,1024]{1,0:T(8,128)}, f32[512,1024]{1,0:T(8,128)}) custom-call(f32[4096,1024]{1,0:T(8,128)} %get-tuple-element.83.refs_0_.refs_1_.refs_2_, f32[4096,1024]{1,0:T(8,128)} %get-tuple-element.83.refs_0_.refs_1_.refs_2_, ...), custom_call_target="tpu_custom_call" | custom-call | flops 32212254720 | bytes 50331648 | tf_op jit(solution)/shard_map/chain_backward_first/pallas_call | solution.py:933
  692.8 66.3 %chain_backward_second.1 = (bf16[4096,1024]{1,0:T(8,128)(2,1)}, bf16[4096,2048]{1,0:T(8,128)(2,1)}, bf16[4096,1536]{1,0:T(8,128)(2,1)}, f32[8,1024]{1,0:T(8,128)}, f32[512,1024]{1,0:T(8,128)}) custom-call(f32[512,1024]{1,0:T(8,128)} %get-tuple-element.89.refs_0_, ...), custom_call_target="tpu_custom_call", output_to_operand_aliasing={{0}: (15, {}), {1}: (16, {}), {2}: (17, {})} | custom-call | flops 32212254720 | bytes 50331648 | tf_op jit(solution)/shard_map/chain_backward_second/pallas_call | solution.py:933
  759.1 13.8 %convolution_convert_fusion.6 = bf16[1024,1024]{1,0:T(8,128)(2,1)S(1)} fusion(bf16[4096,1024]{1,0:T(8,128)(2,1)} %get-tuple-element.97, bf16[4096,1024]{1,0:T(8,128)(2,1)} %get-tuple-element.85.refs_12_.refs_13_), kind=kOutput, calls=%fused_computation.82 | convolution fusion | flops 8590983168 | bytes 18874368 | tf_op jit(solution)/shard_map/dot_general | solution.py:78
  775.0 23.8 %convolution_convert_fusion.3 = bf16[1024,2048]{1,0:T(8,128)(2,1)} fusion(bf16[4096,1024]{1,0:T(8,128)(2,1)} %get-tuple-element.95, bf16[4096,2048]{1,0:T(8,128)(2,1)} %get-tuple-element.96), kind=kOutput, calls=%fused_computation.63 | convolution fusion | flops 17181966336 | bytes 29360128 | tf_op jit(solution)/shard_map/dot_general | solution.py:78
  803.5 13.9 %fusion.31 = bf16[2048,1024]{1,0:T(8,128)(2,1)} fusion(bf16[4096,2048]{1,0:T(8,128)(2,1)} %get-tuple-element.80, bf16[2048,2048]{1,0:T(8,128)(2,1)} %all-gather.11.cloned.1.call-done, s32[]{:T(128)S(6)} %select_n.434), kind=kOutput, calls=%fused_computation.66 | convolution fusion | flops 8592031744 | bytes 16777220 | tf_op jit(solution)/shard_map/dot_general | solution.py:82
  822.3 35.7 %self_backward_first.1 = (bf16[4096,2048]{1,0:T(8,128)(2,1)}, f32[4,5,128,128]{3,2,1,0:T(8,128)}, f32[512,1024]{1,0:T(8,128)}) custom-call(s32[3]{0:T(128)} %pad_add_fusion.where, bf16[4096,2048]{1,0:T(8,128)(2,1)} %convolution_convert_fusion.q.kp.kc.vp.vc.cq.refs_6_.refs_7_.refs_8_.refs_9_, ...), custom_call_target="tpu_custom_call" | custom-call | flops 21474836480 | bytes 31457280 | tf_op jit(solution)/shard_map/self_backward_first/pallas_call | solution.py:339
  862.7 36.4 %self_backward_second.1 = (bf16[4096,2048]{1,0:T(8,128)(2,1)}, f32[4,5,128,128]{3,2,1,0:T(8,128)}, f32[512,1024]{1,0:T(8,128)}) custom-call(s32[3]{0:T(128)} %pad_add_fusion.where, bf16[4096,2048]{1,0:T(8,128)(2,1)} %convolution_convert_fusion.q.kp.kc.vp.vc.cq.refs_6_.refs_7_.refs_8_.refs_9_, ...), custom_call_target="tpu_custom_call", output_to_operand_aliasing={{0}: (10, {})} | custom-call | flops 21474836480 | bytes 31457280 | tf_op jit(solution)/shard_map/self_backward_second/pallas_call | solution.py:339
  901.4 23.9 %convolution_convert_fusion.2 = bf16[1024,2048]{1,0:T(8,128)(2,1)} fusion(bf16[4096,1024]{1,0:T(8,128)(2,1)} %pad_maximum_fusion, bf16[4096,2048]{1,0:T(8,128)(2,1)} %get-tuple-element.115), kind=kOutput, calls=%fused_computation.62 | convolution fusion | flops 17181966336 | bytes 29360128 | tf_op jit(solution)/shard_map/dot_general | solution.py:78
  937.1 14.3 %fusion.34 = bf16[2048,1024]{1,0:T(8,128)(2,1)} fusion(bf16[4096,2048]{1,0:T(8,128)(2,1)} %get-tuple-element.115, bf16[2048,2176]{1,0:T(8,128)(2,1)} %all-gather.5.cloned.1.call-done, s32[]{:T(128)S(6)} %select_n.434), kind=kOutput, calls=%fused_computation.67 | convolution fusion | flops 8592031744 | bytes 16777220 | tf_op jit(solution)/shard_map/dot_general | solution.py:82
  952.1 16.3 %add_convert_fusion = bf16[2048,1024]{1,0:T(8,128)(2,1)} fusion(f32[2048,1024]{1,0:T(8,128)S(1)} %bitcast.157, bf16[2048,1024]{1,0:T(8,128)(2,1)} %collective-permute-done.17, bf16[2048,2048]{1,0:T(8,128)(2,1)} %all-gather.11.cloned.1.call-done, s32[]{:T(128)S(6)} %select_n.434, bf16[4096,2048]{1,0:T(8,128)(2,1)} %get-tuple-element.80), kind=kOutput, calls=%fused_computation.31 | convolution fusion | flops 8598323200 | bytes 29360132 | tf_op jit(solution)/shard_map/dot_general | solution.py:82
  973.4 15.7 %fusion.56 = (f32[2048]{0:T(1024)S(1)}, f32[2048]{0:T(1024)S(1)}, f32[2048,1024]{1,0:T(8,128)S(1)}) fusion(f32[1024]{0:T(1024)S(1)} %copy-done.31, bf16[2048,1024]{1,0:T(8,128)(2,1)} %collective-permute-done.19, f32[2048]{0:T(1024)S(1)} %copy-done.29, f32[2048]{0:T(1024)S(1)} %copy-done.27, bf16[2048,1024]{1,0:T(8,128)(2,1)} %copy-done.1, ...), kind=kOutput, calls=%fused_computation.77 | convolution fusion | flops 8608804864 | bytes 29396996 | tf_op jit(solution)/shard_map/dot_general | solution.py:82
  991.9 9.0 fusion.11
  1021.5 52.7 %reduce-scatter.15.cloned.1.call-done = bf16[64,2176]{1,0:T(8,128)(2,1)} async-done(((bf16[1024,2176]{1,0:T(8,128)(2,1)}), bf16[64,2176]{1,0:T(8,128)(2,1)}) %reduce-scatter.15.cloned.1.call-update) | async-done | bytes 278544 | tf_op jit(solution)/shard_map/reduce_scatter | solution.py:1035
  1076.3 36.4 %collective-permute-start.21 = (f32[4,64]{1,0:T(4,128)S(1)}, f32[4,64]{1,0:T(4,128)S(1)}, u32[]{:S(2)}, u32[]{:S(2)}) collective-permute-start(f32[4,64]{1,0:T(4,128)S(1)} %pad_maximum_fusion.10), channel_id=1, source_target_pairs={{0,1},{1,0},{2,3},{3,2},{4,5},{5,4},{6,7},{7,6},{8,9},{9,8},{10,11... | collective-permute-start | bytes 3080 | tf_op jit(solution)/shard_map/ppermute | solution.py:1272
  (261 shorter events, 180.5 us)
Async XLA Ops:
  7.2 92.3 %all-gather.5.cloned.1.call-start = ((), (), s32[]{:S(2)}) async-start(), calls=%async_computation.6 | async-start | bytes 9191424 | tf_op jit(solution)/shard_map/all_gather | solution.py:1021
  12.6 194.3 %all-gather.7.cloned.1.call-start = ((), (), s32[]{:S(2)}) async-start(), calls=%async_computation.7 | async-start | bytes 12976128 | tf_op jit(solution)/shard_map/all_gather | solution.py:1021
  12.6 4.6 collective-permute-start
  102.2 220.1 %all-gather.9.cloned.1.call-start = ((), (), s32[]{:S(2)}) async-start(), calls=%async_computation.8 | async-start | bytes 12976128 | tf_op jit(solution)/shard_map/all_gather | solution.py:1021
  102.4 11.9 %collective-permute-start.2 = (f32[256,1024]{1,0:T(8,128)S(1)}, f32[256,1024]{1,0:T(8,128)S(1)}, u32[]{:S(2)}, u32[]{:S(2)}) collective-permute-start(f32[256,1024]{1,0:T(8,128)S(1)} %add_bitcast_fusion), channel_id=1, source_target_pairs={{1,2},{2,1},{5,6},{6,5},{9,10},{10,9},{13,14},{14,13},{17,18},{18,... | collective-permute-start | bytes 3145736 | tf_op jit(solution)/shard_map/ppermute | solution.py:42
  111.7 24.4 %collective-permute-start.1 = (bf16[2048,1024]{1,0:T(8,128)(2,1)}, bf16[2048,1024]{1,0:T(8,128)(2,1)}, u32[]{:S(2)}, u32[]{:S(2)}) collective-permute-start(bf16[2048,1024]{1,0:T(8,128)(2,1)} %fusion.6), channel_id=1, source_target_pairs={{0,2},{2,0},{1,3},{3,1},{4,6},{6,4},{5,7},{7,5},{8,10},{10,8},{9,1... | collective-permute-start | bytes 12582920 | tf_op jit(solution)/shard_map/ppermute | solution.py:56
  114.5 10.7 collective-permute-start.3
  209.6 202.1 %all-gather.11.cloned.1.call-start = ((), (), s32[]{:S(2)}) async-start(), calls=%async_computation.9 | async-start | bytes 8650752 | tf_op jit(solution)/shard_map/all_gather | solution.py:1021
  214.3 101.5 %collective-permute-start.4 = (bf16[2048,1024]{1,0:T(8,128)(2,1)}, bf16[2048,1024]{1,0:T(8,128)(2,1)}, u32[]{:S(2)}, u32[]{:S(2)}) collective-permute-start(bf16[2048,1024]{1,0:T(8,128)(2,1)} %bitcast.159), channel_id=1, source_target_pairs={{1,2},{2,1},{5,6},{6,5},{9,10},{10,9},{13,14},{14,13},{17,18},{18,... | collective-permute-start | bytes 12582920 | tf_op jit(solution)/shard_map/ppermute | solution.py:42
  324.9 365.7 %reduce-scatter.7.cloned.1.call-start = ((), (), s32[]{:S(2)}) async-start(), calls=%async_computation.10 | async-start | bytes 4456448 | tf_op jit(solution)/shard_map/reduce_scatter | solution.py:1035
  332.8 11.4 %collective-permute-start.5 = (bf16[2048,1024]{1,0:T(8,128)(2,1)S(1)}, bf16[2048,1024]{1,0:T(8,128)(2,1)}, u32[]{:S(2)}, u32[]{:S(2)}) collective-permute-start(bf16[2048,1024]{1,0:T(8,128)(2,1)S(1)} %fusion.40), channel_id=1, source_target_pairs={{0,2},{2,0},{1,3},{3,1},{4,6},{6,4},{5,7},{7,5},{8,10},{10,8},{9,1... | collective-permute-start | bytes 12582920 | tf_op jit(solution)/shard_map/ppermute | solution.py:56
  333.0 24.8 %collective-permute-start.6 = (bf16[2048,1024]{1,0:T(8,128)(2,1)S(1)}, bf16[2048,1024]{1,0:T(8,128)(2,1)S(1)}, u32[]{:S(2)}, u32[]{:S(2)}) collective-permute-start(bf16[2048,1024]{1,0:T(8,128)(2,1)S(1)} %copy-done.5), channel_id=1, source_target_pairs={{0,2},{2,0},{1,3},{3,1},{4,6},{6,4},{5,7},{7,5},{8,10},{10,8},{9,1... | collective-permute-start | bytes 12582920 | tf_op jit(solution)/shard_map/ppermute | solution.py:56
  357.2 10.0 collective-permute-start.7
  450.3 28.8 %collective-permute-start.8 = (bf16[2048,1024]{1,0:T(8,128)(2,1)}, bf16[2048,1024]{1,0:T(8,128)(2,1)}, u32[]{:S(2)}, u32[]{:S(2)}) collective-permute-start(bf16[2048,1024]{1,0:T(8,128)(2,1)} %fusion.37), channel_id=1, source_target_pairs={{0,2},{2,0},{1,3},{3,1},{4,6},{6,4},{5,7},{7,5},{8,10},{10,8},{9,1... | collective-permute-start | bytes 12582920 | tf_op jit(solution)/shard_map/ppermute | solution.py:56
  450.6 0.7 collective-permute-start.10
  476.3 77.7 %collective-permute-start.11 = (bf16[1024,2048]{1,0:T(8,128)(2,1)}, bf16[1024,2048]{1,0:T(8,128)(2,1)}, u32[]{:S(2)}, u32[]{:S(2)}) collective-permute-start(bf16[1024,2048]{1,0:T(8,128)(2,1)} %convolution_convert_fusion.5), channel_id=1, source_target_pairs={{2,1},{1,2},{6,5},{5,6},{10,9},{9,10},{14,13},{13,14},{18,17},{17,... | collective-permute-start | bytes 12582920 | tf_op jit(solution)/shard_map/ppermute | solution.py:42
  511.0 47.6 %collective-permute-start.9 = (bf16[2048,1024]{1,0:T(8,128)(2,1)}, bf16[2048,1024]{1,0:T(8,128)(2,1)}, u32[]{:S(2)}, u32[]{:S(2)}) collective-permute-start(bf16[2048,1024]{1,0:T(8,128)(2,1)} %get-tuple-element.210), channel_id=1, source_target_pairs={{0,2},{2,0},{1,3},{3,1},{4,6},{6,4},{5,7},{7,5},{8,10},{10,8},{9,1... | collective-permute-start | bytes 12582920 | tf_op jit(solution)/shard_map/ppermute | solution.py:56
  551.3 22.6 %collective-permute-start.12 = (bf16[1024,2048]{1,0:T(8,128)(2,1)}, bf16[1024,2048]{1,0:T(8,128)(2,1)}, u32[]{:S(2)}, u32[]{:S(2)}) collective-permute-start(bf16[1024,2048]{1,0:T(8,128)(2,1)} %convolution_convert_fusion.4), channel_id=1, source_target_pairs={{2,1},{1,2},{6,5},{5,6},{10,9},{9,10},{14,13},{13,14},{18,17},{17,... | collective-permute-start | bytes 12582920 | tf_op jit(solution)/shard_map/ppermute | solution.py:42
  573.8 226.6 %reduce-scatter.9.cloned.1.call-start = ((), (), s32[]{:S(2)}) async-start(), calls=%async_computation.11 | async-start | bytes 4456448 | tf_op jit(solution)/shard_map/reduce_scatter | solution.py:1035
  592.8 98.4 %collective-permute-start.13 = (bf16[1024,1024]{1,0:T(8,128)(2,1)S(1)}, bf16[1024,1024]{1,0:T(8,128)(2,1)}, u32[]{:S(2)}, u32[]{:S(2)}) collective-permute-start(bf16[1024,1024]{1,0:T(8,128)(2,1)S(1)} %fusion.57), channel_id=1, source_target_pairs={{2,1},{1,2},{6,5},{5,6},{10,9},{9,10},{14,13},{13,14},{18,17},{17,... | collective-permute-start | bytes 6291464 | tf_op jit(solution)/shard_map/ppermute | solution.py:42
  690.7 172.0 %reduce-scatter.11.cloned.1.call-start = ((), (), s32[]{:S(2)}) async-start(), calls=%async_computation.12 | async-start | bytes 2228224 | tf_op jit(solution)/shard_map/reduce_scatter | solution.py:1035
  772.9 25.9 %collective-permute-start.14 = (bf16[1024,1024]{1,0:T(8,128)(2,1)S(1)}, bf16[1024,1024]{1,0:T(8,128)(2,1)}, u32[]{:S(2)}, u32[]{:S(2)}) collective-permute-start(bf16[1024,1024]{1,0:T(8,128)(2,1)S(1)} %convolution_convert_fusion.6), channel_id=1, source_target_pairs={{2,1},{1,2},{6,5},{5,6},{10,9},{9,10},{14,13},{13,14},{18,17},{17,... | collective-permute-start | bytes 6291464 | tf_op jit(solution)/shard_map/ppermute | solution.py:42
  775.0 126.4 %reduce-scatter.13.cloned.1.call-start = ((), (), s32[]{:S(2)}) async-start(), calls=%async_computation.13 | async-start | bytes 2228224 | tf_op jit(solution)/shard_map/reduce_scatter | solution.py:1035
  800.5 57.5 %collective-permute-start.15 = (bf16[1024,2048]{1,0:T(8,128)(2,1)}, bf16[1024,2048]{1,0:T(8,128)(2,1)}, u32[]{:S(2)}, u32[]{:S(2)}) collective-permute-start(bf16[1024,2048]{1,0:T(8,128)(2,1)} %convolution_convert_fusion.3), channel_id=1, source_target_pairs={{2,1},{1,2},{6,5},{5,6},{10,9},{9,10},{14,13},{13,14},{18,17},{17,... | collective-permute-start | bytes 12582920 | tf_op jit(solution)/shard_map/ppermute | solution.py:42
  817.3 134.7 %collective-permute-start.17 = (bf16[2048,1024]{1,0:T(8,128)(2,1)}, bf16[2048,1024]{1,0:T(8,128)(2,1)}, u32[]{:S(2)}, u32[]{:S(2)}) collective-permute-start(bf16[2048,1024]{1,0:T(8,128)(2,1)} %fusion.31), channel_id=1, source_target_pairs={{0,2},{2,0},{1,3},{3,1},{4,6},{6,4},{5,7},{7,5},{8,10},{10,8},{9,1... | collective-permute-start | bytes 12582920 | tf_op jit(solution)/shard_map/ppermute | solution.py:56
  822.2 184.7 %reduce-scatter.17.cloned.1.call-start = ((), (), s32[]{:S(2)}) async-start(), calls=%async_computation.15 | async-start | bytes 4456448 | tf_op jit(solution)/shard_map/reduce_scatter | solution.py:1035
  925.3 149.0 %reduce-scatter.15.cloned.1.call-start = ((), (), s32[]{:S(2)}) async-start(), calls=%async_computation.14 | async-start | bytes 4734976 | tf_op jit(solution)/shard_map/reduce_scatter | solution.py:1035
  934.0 34.4 %collective-permute-start.16 = (bf16[1024,2176]{1,0:T(8,128)(2,1)}, bf16[1024,2176]{1,0:T(8,128)(2,1)}, u32[]{:S(2)}, u32[]{:S(2)}) collective-permute-start(bf16[1024,2176]{1,0:T(8,128)(2,1)} %fusion.26), channel_id=1, source_target_pairs={{2,1},{1,2},{6,5},{5,6},{10,9},{9,10},{14,13},{13,14},{18,17},{17,... | collective-permute-start | bytes 13369352 | tf_op jit(solution)/shard_map/ppermute | solution.py:42
  951.4 22.0 %collective-permute-start.19 = (bf16[2048,1024]{1,0:T(8,128)(2,1)}, bf16[2048,1024]{1,0:T(8,128)(2,1)}, u32[]{:S(2)}, u32[]{:S(2)}) collective-permute-start(bf16[2048,1024]{1,0:T(8,128)(2,1)} %fusion.34), channel_id=1, source_target_pairs={{0,2},{2,0},{1,3},{3,1},{4,6},{6,4},{5,7},{7,5},{8,10},{10,8},{9,1... | collective-permute-start | bytes 12582920 | tf_op jit(solution)/shard_map/ppermute | solution.py:56
  989.2 21.0 %collective-permute-start.18 = (bf16[2048,1024]{1,0:T(8,128)(2,1)}, bf16[2048,1024]{1,0:T(8,128)(2,1)}, u32[]{:S(2)}, u32[]{:S(2)}) collective-permute-start(bf16[2048,1024]{1,0:T(8,128)(2,1)} %add_convert_fusion), channel_id=1, source_target_pairs={{2,1},{1,2},{6,5},{5,6},{10,9},{9,10},{14,13},{13,14},{18,17},{17,... | collective-permute-start | bytes 12582920 | tf_op jit(solution)/shard_map/ppermute | solution.py:42
  1000.9 14.2 %collective-permute-start.20 = (bf16[2048,1024]{1,0:T(8,128)(2,1)}, bf16[2048,1024]{1,0:T(8,128)(2,1)}, u32[]{:S(2)}, u32[]{:S(2)}) collective-permute-start(bf16[2048,1024]{1,0:T(8,128)(2,1)} %fusion.11), channel_id=1, source_target_pairs={{2,1},{1,2},{6,5},{5,6},{10,9},{9,10},{14,13},{13,14},{18,17},{17,... | collective-permute-start | bytes 12582920 | tf_op jit(solution)/shard_map/ppermute | solution.py:42
  1076.3 39.1 %collective-permute-start.21 = (f32[4,64]{1,0:T(4,128)S(1)}, f32[4,64]{1,0:T(4,128)S(1)}, u32[]{:S(2)}, u32[]{:S(2)}) collective-permute-start(f32[4,64]{1,0:T(4,128)S(1)} %pad_maximum_fusion.10), channel_id=1, source_target_pairs={{0,1},{1,0},{2,3},{3,2},{4,5},{5,4},{6,7},{7,6},{8,9},{9,8},{10,11... | collective-permute-start | bytes 3080 | tf_op jit(solution)/shard_map/ppermute | solution.py:1272
  (40 other events, 949.3 us)
Sparse Core Ops, SparseCore 0:
  12.7 86.7 all-gather.4
  103.0 96.6 all-gather.6
  209.7 103.1 all-gather.8
  325.1 77.9 all-gather.10
  573.9 71.5 reduce-scatter.6
  690.8 72.6 reduce-scatter.8
  775.1 61.4 reduce-scatter.10
  840.8 60.5 reduce-scatter.12
  925.4 71.4 reduce-scatter.16
  1001.1 73.0 reduce-scatter.14
